TPU v7x, 256 devices: a whole 4x4x8 slice. The times are simulated.
256 devices in a mesh: line: 16 (over z, x_lo), bus: 8 (over y, core), tm: 2 (over x_hi).
Axes of the slice: x: 4 (x_hi: 2, x_lo: 2; x = x_hi * 2 + x_lo), y: 4, z: 8, core: 2. Of those that a mesh axis runs over, the one named last changes fastest.
Arguments:
- ptdf_matrix: float32 [15360, 12288], P('line', 'bus'), may hold values from -0.0546875 to 0.0546875
- bus_load: float32 [12288, 256], P('bus', 'tm'), may hold values from 0 to 1
- unit_bus: int32 [4096], P(('line', 'bus')), may hold values from 0 to 12287, as said below
- unit_type: int32 [4096], P(('line', 'bus')), may hold values from 0 to 3
- unit_limit: int32 [4096], P(('line', 'bus')), may hold values from 50 to 499
- unit_cost: float32 [4096], P(('line', 'bus')), may hold values from 0.1 to 1
- line_rating: int32 [15360], P('line'), may hold values from 20 to 299
Outputs:
- generation: float32 [4096, 256], P(('line', 'bus'), 'tm')
- line_dual: float32 [15360, 256], P('line', 'tm')
Inputs may be any that keep to these rules, and one draw needn't show every extreme that they name: `unit_bus`: let G be the number of devices of line and bus together, U = 4096 / G and S = 12288 / G. Unit u lies in group q = u // U; it sits at a bus of the S consecutive buses that begin at (q mod the size of bus) * 12288 / (size of bus) + (q // size of bus) * S.
All inputs are finite; a program needn't handle non-finite values.
Results may differ from a plain program's by a relative error of at most 0.0003.
Values sent between devices are 32-bit elements; how exact they have to be, the bound alone decides.
No kernel may reach another device: no remote copies, remote signals or barrier semaphores. Data moves between devices by JAX's collectives and lax.ppermute only.
A program may use at most 64 MiB of HBM per device.

v0:
```python
import jax
import jax.numpy as jnp
from jax import lax
from jax.sharding import Mesh
from jax.sharding import PartitionSpec as P

UNITS = 4096
ITERS = 4
LINE = ("line_0", "line_1")
BUS = ("bus_0", "bus_1")
LINE_BUS = ("line_0", "line_1", "bus_0", "bus_1")


RAMP_RATES = (0.1, 0.2, 0.4, 0.5)
COST_FACTORS = (1.0, 1.5, 3.0, 0.05)
PRIMAL_STEP = 0.5
DUAL_STEP = 0.5


def in_order(blocks, dim):
    blocks = jnp.moveaxis(blocks, 0, dim)
    lengths = blocks.shape
    return blocks.reshape(*lengths[:dim], lengths[dim] * lengths[dim + 1], *lengths[dim + 2 :])


def sent_to_all(value, axis):
    length = lax.axis_size(axis)
    return lax.all_to_all(
        jnp.broadcast_to(value[None], (length, *value.shape)), axis, 0, 0, tiled=True
    )


def gathered_copies(value, axis, dim):
    return in_order(sent_to_all(value, axis), dim)


def cut_along(value, dim, length):
    lengths = value.shape
    blocks = value.reshape(*lengths[:dim], length, lengths[dim] // length, *lengths[dim + 1 :])
    return jnp.moveaxis(blocks, dim, 0)


def sent_and_summed(value, axis, dim):
    length = lax.axis_size(axis)
    blocks = lax.all_to_all(cut_along(value, dim, length), axis, 0, 0, tiled=True)
    return jnp.sum(blocks, axis=0)


def from_behind(value, axis, by):
    length = lax.axis_size(axis)
    pairs = [(i, i + by) for i in range(length) if 0 <= i + by < length]
    return lax.ppermute(value, axis, pairs)


def joined_by_halves(pieces, combine):
    while len(jax.tree.leaves(pieces)[0]) > 1:
        pieces = jax.vmap(combine)(*(pieces[side::2] for side in (0, 1)))
    return pieces[0]


def carried_in(value, axis, combine, identity, reverse):
    length, index = (lax.axis_size(axis), lax.axis_index(axis))
    passed = jnp.arange(length) > index if reverse else jnp.arange(length) < index

    def kept(part, zero, own):
        part = jnp.where(
            passed.reshape(-1, *(1 for _ in own.shape)), part, jnp.asarray(zero, own.dtype)
        )
        return part[::-1] if reverse else part

    pieces = sent_to_all(value, axis)
    return joined_by_halves(kept(pieces, identity, value), combine)


def gathered_total(value, axis):
    return lax.all_gather(value, axis).sum(0)


def over_axes(value, axes):
    for axis in axes:
        value = lax.psum(value, axis)
    return value


def unit_tables(unit_type, unit_limit, unit_cost):
    capacity = unit_limit.astype(jnp.float32) / 100.0
    kinds = (unit_type[:, None] == jnp.arange(4, dtype=jnp.int32)[None, :]).astype(jnp.float32)
    rates = jnp.sum(kinds * jnp.array(RAMP_RATES, jnp.float32)[None, :], axis=1)
    factors = jnp.sum(kinds * jnp.array(COST_FACTORS, jnp.float32)[None, :], axis=1)
    storage = kinds[:, 3]
    return (
        unit_cost * factors,
        -capacity * storage,
        capacity,
        rates * capacity,
        storage,
        2.0 * capacity,
    )


def products(left, right):
    return jnp.dot(left, right, precision=lax.Precision.HIGHEST, preferred_element_type=jnp.float32)


def transposed(left, right):
    return lax.dot_general(
        left,
        right,
        (((0,), (0,)), ((), ())),
        precision=lax.Precision.HIGHEST,
        preferred_element_type=jnp.float32,
    )


def combine_add(earlier, later):
    return earlier + later


def on_device(ptdf_matrix, bus_load, unit_bus, unit_type, unit_limit, unit_cost, line_rating):
    line_place = lax.axis_index(LINE)
    bus_place = lax.axis_index(BUS)
    tm_place = lax.axis_index("tm")
    line_count = lax.axis_size(LINE)
    block_rows = ptdf_matrix.shape[1]
    sub_rows = block_rows // line_count
    hour_dev = bus_load.shape[1]
    cost, lower_limit, upper_limit, ramp, storage, energy = unit_tables(
        unit_type, unit_limit, unit_cost
    )
    block_bus = unit_bus - bus_place * block_rows
    unit_places = gathered_copies(block_bus, LINE, 0)
    load_flow = products(ptdf_matrix, bus_load)
    local_load = lax.dynamic_slice_in_dim(bus_load, line_place * sub_rows, sub_rows, 0)
    local_units = cost.shape[0]
    load_total = jnp.sum(local_load, axis=0)
    rating = (line_rating.astype(jnp.float32) / 100.0)[:, None]
    hour_index = tm_place * hour_dev + jnp.arange(hour_dev, dtype=jnp.int32)
    hour_mask = (hour_index >= 1).astype(jnp.float32)[None, :]
    earlier_index = jnp.arange(hour_dev, dtype=jnp.int32)[:, None]
    later_index = jnp.arange(hour_dev, dtype=jnp.int32)[None, :]
    forward_table = (earlier_index <= later_index).astype(jnp.float32)
    backward_table = (earlier_index >= later_index).astype(jnp.float32)
    generation = jnp.zeros((local_units, hour_dev), jnp.float32)
    ramp_dual = jnp.zeros((local_units, hour_dev), jnp.float32)
    store_dual = jnp.zeros((local_units, hour_dev), jnp.float32)
    balance_dual = jnp.zeros((hour_dev,), jnp.float32)
    unit_zeros = jnp.zeros((local_units,), jnp.float32)
    line_dual = jnp.zeros((ptdf_matrix.shape[0], hour_dev), jnp.float32)
    for iteration in range(ITERS):
        dual_full = line_dual
        columns = jnp.take(ptdf_matrix, unit_places, axis=1)
        unit_price = sent_and_summed(transposed(columns, dual_full), LINE, 0)
        ramp_edge = from_behind(ramp_dual[:, :1], "tm", -1)
        ramp_next = jnp.concatenate([ramp_dual[:, 1:], ramp_edge], axis=1)
        store_after = carried_in(jnp.sum(store_dual, axis=1), "tm", combine_add, unit_zeros, True)
        suffix = products(store_dual, backward_table) + store_after[:, None]
        gradient = (
            cost[:, None]
            + balance_dual[None, :]
            + unit_price
            + ramp_dual
            - ramp_next
            + storage[:, None] * suffix
        )
        updated = jnp.clip(
            generation - PRIMAL_STEP * gradient, lower_limit[:, None], upper_limit[:, None]
        )
        extrap = 2.0 * updated - generation
        add_columns = jnp.take(ptdf_matrix, unit_places, axis=1)
        flow_part = products(add_columns, gathered_copies(extrap, LINE, 0)) - load_flow
        flow = gathered_total(flow_part, BUS)
        moved = line_dual + DUAL_STEP * flow
        line_dual = moved - jnp.clip(moved, -DUAL_STEP * rating, DUAL_STEP * rating)
        surplus_part = jnp.sum(extrap, axis=0) - load_total
        surplus = over_axes(surplus_part, LINE_BUS)
        balance_dual = balance_dual + surplus / UNITS
        prev_edge = from_behind(extrap[:, -1:], "tm", 1)
        previous = jnp.concatenate([prev_edge, extrap[:, :-1]], axis=1)
        moved = ramp_dual + DUAL_STEP * (extrap - previous) * hour_mask
        ramp_dual = moved - jnp.clip(moved, -DUAL_STEP * ramp[:, None], DUAL_STEP * ramp[:, None])
        store_before = carried_in(jnp.sum(extrap, axis=1), "tm", combine_add, unit_zeros, False)
        running = products(extrap, forward_table) + store_before[:, None]
        moved = store_dual + DUAL_STEP * storage[:, None] * running
        store_dual = moved - jnp.clip(
            moved, -DUAL_STEP * energy[:, None], DUAL_STEP * energy[:, None]
        )
        generation = updated
    return (generation, line_dual)


def solution(mesh):
    finer = Mesh(
        mesh.devices.reshape(8, 2, 4, 2, mesh.shape["tm"]),
        ("line_0", "line_1", "bus_0", "bus_1", "tm"),
    )
    return jax.shard_map(
        on_device,
        mesh=finer,
        in_specs=(
            P(LINE, BUS),
            P(BUS, "tm"),
            P(LINE_BUS),
            P(LINE_BUS),
            P(LINE_BUS),
            P(LINE_BUS),
            P(LINE),
        ),
        out_specs=(P(LINE_BUS, "tm"), P(LINE, "tm")),
        check_vma=False,
    )
```

profile of v0, /device:TPU:1, one launch (start us, length us, event | category | flops | bytes accessed | tf_op | source)
XLA Modules:
  0.0 396.0 jit_solution(6639573050156399909)
XLA Ops:
  8.5 10.0 %all-to-all-start = ((s32[16,1,32]{2,1,0:T(1,128)}), s32[16,1,32]{2,1,0:T(1,128)S(1)}, u32[]{:S(2)}, u32[]{:S(2)}) async-start(s32[16,1,32]{2,1,0:T(1,128)} %broadcast_in_dim.71), calls=%async_computation | async-start | bytes 16384 | tf_op jit(solution)/shard_map/all_to_all | solution.py:28
  19.9 6.5 %copy.13 = f32[960,1536]{0,1:T(8,128)} copy(f32[960,1536]{1,0:T(8,128)} %param.11) | data formatting | bytes 11796480 | tf_op args[0]
  27.7 6.4 %gather_fusion = f32[512,960]{1,0:T(8,128)} fusion(f32[960,1536]{0,1:T(8,128)} %copy.13, s32[1024]{0:T(1024)S(1)} %pad_clamp_fusion), kind=kCustom, calls=%fused_computation.clone | custom fusion | bytes 3934208 | tf_op jit(solution)/shard_map/jit(_take)/gather | solution.py:151
  38.4 7.6 %all-to-all-start.1 = ((f32[16,32,128]{2,1,0:T(8,128)}), f32[16,32,128]{2,1,0:T(8,128)S(1)}, u32[]{:S(2)}, u32[]{:S(2)}) async-start(f32[16,32,128]{2,1,0:T(8,128)} %fusion.34), calls=%async_computation.1 | async-start | bytes 524288 | tf_op jit(solution)/shard_map/all_to_all | solution.py:45
  46.5 9.5 %all-to-all-done.1 = f32[16,32,128]{2,1,0:T(8,128)S(1)} async-done(((f32[16,32,128]{2,1,0:T(8,128)}), f32[16,32,128]{2,1,0:T(8,128)S(1)}, u32[]{:S(2)}, u32[]{:S(2)}) %all-to-all-start.1) | async-done | bytes 262176 | tf_op jit(solution)/shard_map/all_to_all | solution.py:45
  61.2 6.8 %fusion.70 = f32[960,128]{1,0:T(8,128)S(1)} fusion(f32[960,1536]{1,0:T(8,128)} %param.11, f32[1536,128]{1,0:T(8,128)S(1)} %copy-done), kind=kOutput, calls=%fused_computation.129 | convolution fusion | flops 2264924160 | bytes 7176192 | tf_op jit(solution)/shard_map/dot_general | solution.py:102
  71.1 5.2 %fusion.17 = f32[960,128]{1,0:T(8,128)} fusion(f32[960,128]{1,0:T(8,128)S(1)} %fusion.70, f32[512,128]{1,0:T(8,128)} %bitcast.3, f32[512,960]{1,0:T(8,128)S(1)} %broadcast_select_fusion), kind=kOutput, calls=%fused_computation.16 | convolution fusion | flops 755097600 | bytes 3211264 | tf_op jit(solution)/shard_map/dot_general | solution.py:102
  76.6 5.8 %collective-permute-start.1 = (f32[32,1]{1,0:T(8,128)S(1)}, f32[32,1]{1,0:T(8,128)S(1)}, u32[]{:S(2)}, u32[]{:S(2)}) collective-permute-start(f32[32,1]{1,0:T(8,128)S(1)} %slice.135), channel_id=1, source_target_pairs={{0,1},{2,3},{4,5},{6,7},{8,9},{10,11},{12,13},{14,15},{16,17},{18,... | collective-permute-start | bytes 392 | tf_op jit(solution)/shard_map/ppermute | solution.py:52
  88.4 11.1 %psum.84 = f32[128]{0:T(128)S(1)} all-reduce(f32[128]{0:T(128)S(1)} %sub.103), channel_id=1, replica_groups=mesh['line_0'=8,'line_1'=2,'bus_0'=4,'bus_1'=2,'tm'=2] {'line_0'}, use_global_device_ids=true, to_apply=%region_4.6 | all-reduce | flops 128 | bytes 1024 | tf_op jit(solution)/shard_map/psum | solution.py:81
  103.6 9.5 %psum.86 = f32[128]{0:T(128)S(1)} all-reduce(f32[128]{0:T(128)S(1)} %psum.85), channel_id=1, replica_groups=mesh['line_0'=8,'line_1'=2,'bus_0'=4,'bus_1'=2,'tm'=2] {'bus_0'}, use_global_device_ids=true, to_apply=%region_6.8 | all-reduce | flops 128 | bytes 1024 | tf_op jit(solution)/shard_map/psum | solution.py:81
  113.1 13.1 %psum.87 = f32[128]{0:T(128)S(1)} all-reduce(f32[128]{0:T(128)S(1)} %psum.86), channel_id=1, replica_groups=mesh['line_0'=8,'line_1'=2,'bus_0'=4,'bus_1'=2,'tm'=2] {'bus_1'}, use_global_device_ids=true, to_apply=%region_7.9 | all-reduce | flops 128 | bytes 1024 | tf_op jit(solution)/shard_map/psum | solution.py:81
  145.1 9.2 %all-to-all-done.3 = f32[16,32,128]{2,1,0:T(8,128)} async-done(((f32[16,32,128]{2,1,0:T(8,128)}), f32[16,32,128]{2,1,0:T(8,128)}, u32[]{:S(2)}, u32[]{:S(2)}) %all-to-all-start.3) | async-done | bytes 262176 | tf_op jit(solution)/shard_map/all_to_all | solution.py:45
  156.9 12.9 %all_to_all.102 = f32[16,32,128]{2,1,0:T(8,128)S(1)} all-to-all(f32[16,32,128]{2,1,0:T(8,128)S(1)} %broadcast_in_dim.79), channel_id=1, replica_groups=mesh['line_0'=8,'line_1'=2,'bus_0'=4,'bus_1'=2,'tm'=2] {'line_0','line_1'}, dimensions={0} | all-to-all | bytes 524288 | tf_op jit(solution)/shard_map/all_to_all | solution.py:28
  178.6 11.6 %psum.88 = f32[128]{0:T(128)S(1)} all-reduce(f32[128]{0:T(128)S(1)} %sub.112), channel_id=1, replica_groups=mesh['line_0'=8,'line_1'=2,'bus_0'=4,'bus_1'=2,'tm'=2] {'line_0'}, use_global_device_ids=true, to_apply=%region_14.16 | all-reduce | flops 128 | bytes 1024 | tf_op jit(solution)/shard_map/psum | solution.py:81
  194.4 7.2 %psum.90 = f32[128]{0:T(128)S(1)} all-reduce(f32[128]{0:T(128)S(1)} %psum.89), channel_id=1, replica_groups=mesh['line_0'=8,'line_1'=2,'bus_0'=4,'bus_1'=2,'tm'=2] {'bus_0'}, use_global_device_ids=true, to_apply=%region_16.18 | all-reduce | flops 128 | bytes 1024 | tf_op jit(solution)/shard_map/psum | solution.py:81
  201.6 10.2 %psum.91 = f32[128]{0:T(128)S(1)} all-reduce(f32[128]{0:T(128)S(1)} %psum.90), channel_id=1, replica_groups=mesh['line_0'=8,'line_1'=2,'bus_0'=4,'bus_1'=2,'tm'=2] {'bus_1'}, use_global_device_ids=true, to_apply=%region_17.19 | all-reduce | flops 128 | bytes 1024 | tf_op jit(solution)/shard_map/psum | solution.py:81
  234.6 9.1 %all-to-all-done.7 = f32[16,32,128]{2,1,0:T(8,128)} async-done(((f32[16,32,128]{2,1,0:T(8,128)}), f32[16,32,128]{2,1,0:T(8,128)}, u32[]{:S(2)}, u32[]{:S(2)}) %all-to-all-start.7) | async-done | bytes 262176 | tf_op jit(solution)/shard_map/all_to_all | solution.py:45
  246.3 12.9 %all_to_all.103 = f32[16,32,128]{2,1,0:T(8,128)S(1)} all-to-all(f32[16,32,128]{2,1,0:T(8,128)S(1)} %broadcast_in_dim.82), channel_id=1, replica_groups=mesh['line_0'=8,'line_1'=2,'bus_0'=4,'bus_1'=2,'tm'=2] {'line_0','line_1'}, dimensions={0} | all-to-all | bytes 524288 | tf_op jit(solution)/shard_map/all_to_all | solution.py:28
  268.1 11.6 %psum.92 = f32[128]{0:T(128)S(1)} all-reduce(f32[128]{0:T(128)S(1)} %sub.121), channel_id=1, replica_groups=mesh['line_0'=8,'line_1'=2,'bus_0'=4,'bus_1'=2,'tm'=2] {'line_0'}, use_global_device_ids=true, to_apply=%region_23.25 | all-reduce | flops 128 | bytes 1024 | tf_op jit(solution)/shard_map/psum | solution.py:81
  283.8 8.7 %psum.94 = f32[128]{0:T(128)S(1)} all-reduce(f32[128]{0:T(128)S(1)} %psum.93), channel_id=1, replica_groups=mesh['line_0'=8,'line_1'=2,'bus_0'=4,'bus_1'=2,'tm'=2] {'bus_0'}, use_global_device_ids=true, to_apply=%region_25.27 | all-reduce | flops 128 | bytes 1024 | tf_op jit(solution)/shard_map/psum | solution.py:81
  292.5 10.7 %psum.95 = f32[128]{0:T(128)S(1)} all-reduce(f32[128]{0:T(128)S(1)} %psum.94), channel_id=1, replica_groups=mesh['line_0'=8,'line_1'=2,'bus_0'=4,'bus_1'=2,'tm'=2] {'bus_1'}, use_global_device_ids=true, to_apply=%region_26.28 | all-reduce | flops 128 | bytes 1024 | tf_op jit(solution)/shard_map/psum | solution.py:81
  326.4 9.1 %all-to-all-done.11 = f32[16,32,128]{2,1,0:T(8,128)} async-done(((f32[16,32,128]{2,1,0:T(8,128)}), f32[16,32,128]{2,1,0:T(8,128)}, u32[]{:S(2)}, u32[]{:S(2)}) %all-to-all-start.11) | async-done | bytes 262176 | tf_op jit(solution)/shard_map/all_to_all | solution.py:45
  337.3 12.9 %all_to_all.104 = f32[16,32,128]{2,1,0:T(8,128)S(1)} all-to-all(f32[16,32,128]{2,1,0:T(8,128)S(1)} %broadcast_in_dim.85), channel_id=1, replica_groups=mesh['line_0'=8,'line_1'=2,'bus_0'=4,'bus_1'=2,'tm'=2] {'line_0','line_1'}, dimensions={0} | all-to-all | bytes 524288 | tf_op jit(solution)/shard_map/all_to_all | solution.py:28
  354.5 31.3 %all-gather.15.cloned.1.call-done = f32[7680,128]{1,0:T(8,128)} async-done(((f32[960,128]{1,0:T(8,128)}), f32[7680,128]{1,0:T(8,128)}) %all-gather.15.cloned.1.call-update) | async-done | bytes 3932176 | tf_op jit(solution)/shard_map/all_gather | solution.py:76
  (155 shorter events, 132.9 us)
Async XLA Ops:
  8.5 17.8 %all-to-all-start = ((s32[16,1,32]{2,1,0:T(1,128)}), s32[16,1,32]{2,1,0:T(1,128)S(1)}, u32[]{:S(2)}, u32[]{:S(2)}) async-start(s32[16,1,32]{2,1,0:T(1,128)} %broadcast_in_dim.71), calls=%async_computation | async-start | bytes 16384 | tf_op jit(solution)/shard_map/all_to_all | solution.py:28
  18.6 37.4 %collective-permute-start = (f32[32,1]{1,0:T(8,128)S(1)}, f32[32,1]{1,0:T(8,128)S(1)}, u32[]{:S(2)}, u32[]{:S(2)}) collective-permute-start(f32[32,1]{1,0:T(8,128)S(1)} %slice.107), channel_id=1, source_target_pairs={{1,0},{3,2},{5,4},{7,6},{9,8},{11,10},{13,12},{15,14},{17,16},{19,... | collective-permute-start | bytes 392 | tf_op jit(solution)/shard_map/ppermute | solution.py:52
  38.4 17.6 %all-to-all-start.1 = ((f32[16,32,128]{2,1,0:T(8,128)}), f32[16,32,128]{2,1,0:T(8,128)S(1)}, u32[]{:S(2)}, u32[]{:S(2)}) async-start(f32[16,32,128]{2,1,0:T(8,128)} %fusion.34), calls=%async_computation.1 | async-start | bytes 524288 | tf_op jit(solution)/shard_map/all_to_all | solution.py:45
  56.9 14.1 %all-to-all-start.2 = ((f32[16,32,128]{2,1,0:T(8,128)}), f32[16,32,128]{2,1,0:T(8,128)}, u32[]{:S(2)}, u32[]{:S(2)}) async-start(f32[16,32,128]{2,1,0:T(8,128)} %broadcast_in_dim.73), calls=%async_computation.2 | async-start | bytes 524288 | tf_op jit(solution)/shard_map/all_to_all | solution.py:28
  61.1 71.2 %all-gather.9.cloned.1.call-start = ((), (), s32[]{:S(2)}) async-start(), calls=%async_computation.15 | async-start | bytes 4423680 | tf_op jit(solution)/shard_map/all_gather | solution.py:76
  76.6 6.6 %collective-permute-start.1 = (f32[32,1]{1,0:T(8,128)S(1)}, f32[32,1]{1,0:T(8,128)S(1)}, u32[]{:S(2)}, u32[]{:S(2)}) collective-permute-start(f32[32,1]{1,0:T(8,128)S(1)} %slice.135), channel_id=1, source_target_pairs={{0,1},{2,3},{4,5},{6,7},{8,9},{10,11},{12,13},{14,15},{16,17},{18,... | collective-permute-start | bytes 392 | tf_op jit(solution)/shard_map/ppermute | solution.py:52
  83.9 42.3 %all-to-all-start.4 = ((f32[2,1,32]{2,1,0:T(1,128)}), f32[2,1,32]{2,1,0:T(1,128)S(1)}, u32[]{:S(2)}, u32[]{:S(2)}) async-start(f32[2,1,32]{2,1,0:T(1,128)} %broadcast_in_dim.75), calls=%async_computation.4 | async-start | bytes 2048 | tf_op jit(solution)/shard_map/all_to_all | solution.py:28
  127.8 11.3 %all-to-all-start.5 = ((f32[2,1,32]{2,1,0:T(1,128)}), f32[2,1,32]{2,1,0:T(1,128)S(1)}, u32[]{:S(2)}, u32[]{:S(2)}) async-start(f32[2,1,32]{2,1,0:T(1,128)} %broadcast_in_dim.78), calls=%async_computation.5 | async-start | bytes 2048 | tf_op jit(solution)/shard_map/all_to_all | solution.py:28
  139.1 15.2 %all-to-all-start.3 = ((f32[16,32,128]{2,1,0:T(8,128)}), f32[16,32,128]{2,1,0:T(8,128)}, u32[]{:S(2)}, u32[]{:S(2)}) async-start(f32[16,32,128]{2,1,0:T(8,128)} %bitcast.82), calls=%async_computation.3 | async-start | bytes 524288 | tf_op jit(solution)/shard_map/all_to_all | solution.py:45
  143.6 78.1 %all-gather.11.cloned.1.call-start = ((), (), s32[]{:S(2)}) async-start(), calls=%async_computation.16 | async-start | bytes 4423680 | tf_op jit(solution)/shard_map/all_gather | solution.py:76
  143.8 11.5 %collective-permute-start.2 = (f32[32,1]{1,0:T(8,128)S(1)}, f32[32,1]{1,0:T(8,128)S(1)}, u32[]{:S(2)}, u32[]{:S(2)}) collective-permute-start(f32[32,1]{1,0:T(8,128)S(1)} %bitcast.87), channel_id=1, source_target_pairs={{1,0},{3,2},{5,4},{7,6},{9,8},{11,10},{13,12},{15,14},{17,16},{19,... | collective-permute-start | bytes 392 | tf_op jit(solution)/shard_map/ppermute | solution.py:52
  174.7 42.3 %all-to-all-start.8 = ((f32[2,1,32]{2,1,0:T(1,128)}), f32[2,1,32]{2,1,0:T(1,128)S(1)}, u32[]{:S(2)}, u32[]{:S(2)}) async-start(f32[2,1,32]{2,1,0:T(1,128)} %broadcast_in_dim.80), calls=%async_computation.8 | async-start | bytes 2048 | tf_op jit(solution)/shard_map/all_to_all | solution.py:28
  211.8 21.2 %collective-permute-start.3 = (f32[32,1]{1,0:T(8,128)S(1)}, f32[32,1]{1,0:T(8,128)S(1)}, u32[]{:S(2)}, u32[]{:S(2)}) collective-permute-start(f32[32,1]{1,0:T(8,128)S(1)} %slice.139), channel_id=1, source_target_pairs={{0,1},{2,3},{4,5},{6,7},{8,9},{10,11},{12,13},{14,15},{16,17},{18,... | collective-permute-start | bytes 392 | tf_op jit(solution)/shard_map/ppermute | solution.py:52
  218.6 10.1 %all-to-all-start.9 = ((f32[2,1,32]{2,1,0:T(1,128)}), f32[2,1,32]{2,1,0:T(1,128)S(1)}, u32[]{:S(2)}, u32[]{:S(2)}) async-start(f32[2,1,32]{2,1,0:T(1,128)} %broadcast_in_dim.81), calls=%async_computation.9 | async-start | bytes 2048 | tf_op jit(solution)/shard_map/all_to_all | solution.py:28
  228.7 15.0 %all-to-all-start.7 = ((f32[16,32,128]{2,1,0:T(8,128)}), f32[16,32,128]{2,1,0:T(8,128)}, u32[]{:S(2)}, u32[]{:S(2)}) async-start(f32[16,32,128]{2,1,0:T(8,128)} %bitcast.78), calls=%async_computation.7 | async-start | bytes 524288 | tf_op jit(solution)/shard_map/all_to_all | solution.py:45
  233.0 80.2 %all-gather.13.cloned.1.call-start = ((), (), s32[]{:S(2)}) async-start(), calls=%async_computation.17 | async-start | bytes 4423680 | tf_op jit(solution)/shard_map/all_gather | solution.py:76
  233.2 11.4 %collective-permute-start.4 = (f32[32,1]{1,0:T(8,128)S(1)}, f32[32,1]{1,0:T(8,128)S(1)}, u32[]{:S(2)}, u32[]{:S(2)}) collective-permute-start(f32[32,1]{1,0:T(8,128)S(1)} %bitcast.88), channel_id=1, source_target_pairs={{1,0},{3,2},{5,4},{7,6},{9,8},{11,10},{13,12},{15,14},{17,16},{19,... | collective-permute-start | bytes 392 | tf_op jit(solution)/shard_map/ppermute | solution.py:52
  246.3 62.2 %copy-start.11 = (f32[32,128]{1,0:T(8,128)S(1)}, f32[32,128]{1,0:T(8,128)}, u32[]{:S(2)}) copy-start(f32[32,128]{1,0:T(8,128)} %get-tuple-element.29) | copy-start | bytes 49156
  264.1 44.3 %all-to-all-start.12 = ((f32[2,1,32]{2,1,0:T(1,128)}), f32[2,1,32]{2,1,0:T(1,128)S(1)}, u32[]{:S(2)}, u32[]{:S(2)}) async-start(f32[2,1,32]{2,1,0:T(1,128)} %broadcast_in_dim.83), calls=%async_computation.12 | async-start | bytes 2048 | tf_op jit(solution)/shard_map/all_to_all | solution.py:28
  303.3 21.6 %collective-permute-start.5 = (f32[32,1]{1,0:T(8,128)S(1)}, f32[32,1]{1,0:T(8,128)S(1)}, u32[]{:S(2)}, u32[]{:S(2)}) collective-permute-start(f32[32,1]{1,0:T(8,128)S(1)} %slice.143), channel_id=1, source_target_pairs={{0,1},{2,3},{4,5},{6,7},{8,9},{10,11},{12,13},{14,15},{16,17},{18,... | collective-permute-start | bytes 392 | tf_op jit(solution)/shard_map/ppermute | solution.py:52
  310.0 10.5 %all-to-all-start.13 = ((f32[2,1,32]{2,1,0:T(1,128)}), f32[2,1,32]{2,1,0:T(1,128)S(1)}, u32[]{:S(2)}, u32[]{:S(2)}) async-start(f32[2,1,32]{2,1,0:T(1,128)} %broadcast_in_dim.84), calls=%async_computation.13 | async-start | bytes 2048 | tf_op jit(solution)/shard_map/all_to_all | solution.py:28
  320.5 15.0 %all-to-all-start.11 = ((f32[16,32,128]{2,1,0:T(8,128)}), f32[16,32,128]{2,1,0:T(8,128)}, u32[]{:S(2)}, u32[]{:S(2)}) async-start(f32[16,32,128]{2,1,0:T(8,128)} %bitcast.83), calls=%async_computation.11 | async-start | bytes 524288 | tf_op jit(solution)/shard_map/all_to_all | solution.py:45
  324.8 60.9 %all-gather.15.cloned.1.call-start = ((), (), s32[]{:S(2)}) async-start(), calls=%async_computation.18 | async-start | bytes 4423680 | tf_op jit(solution)/shard_map/all_gather | solution.py:76
  325.1 11.4 %collective-permute-start.6 = (f32[32,1]{1,0:T(8,128)S(1)}, f32[32,1]{1,0:T(8,128)S(1)}, u32[]{:S(2)}, u32[]{:S(2)}) collective-permute-start(f32[32,1]{1,0:T(8,128)S(1)} %bitcast.89), channel_id=1, source_target_pairs={{1,0},{3,2},{5,4},{7,6},{9,8},{11,10},{13,12},{15,14},{17,16},{19,... | collective-permute-start | bytes 392 | tf_op jit(solution)/shard_map/ppermute | solution.py:52
  (13 other events, 222.2 us)
Sparse Core Ops, SparseCore 0:
  76.4 36.2 all-gather.8
  174.2 31.2 all-gather.10
  263.7 32.3 all-gather.12
  354.6 31.1 all-gather.14
where the time goes:
time: 398 us; the launch traced here: 396 us
  blocking collectives  145 us (36%)
  starting transfers between devices  79.6 us (20%)
  waiting for transfers between devices  72.2 us (18%)
  matrix products  45.4 us (11%)
  other arithmetic  20.5 us (5%)
  local copies, waits for them, and re-layouts  19.1 us (5%)
  between operations  14.3 us (4%)
    psum x12, blocking collectives, over_axes(): value = lax.psum(value, axis)  106 us
    all_to_all x3, blocking collectives, sent_to_all(): lax.all_to_all(jnp.broadcast_to(value[None], (length, *value.shape)), axi...  38.8 us
    all_to_all x8, starting transfers between devices, sent_to_all(): lax.all_to_all(jnp.broadcast_to(value[None], (length, *value.shape)), axi...  37.4 us
    all_to_all x4, waiting for transfers between devices, sent_and_summed(): lax.all_to_all(cut_along(value, dim, length), axis, 0, 0, tiled=True)  36.9 us
    dot_general x12, matrix products, products(): jnp.dot(left, right, precision=lax.Precision.HIGHEST, preferred_element_t...  31.3 us
    all_gather x4, waiting for transfers between devices, gathered_total(): return lax.all_gather(value, axis).sum(0)  31.3 us
    ppermute x7, starting transfers between devices, from_behind(): return lax.ppermute(value, axis, pairs)  21.2 us
    all_to_all x4, starting transfers between devices, sent_and_summed(): lax.all_to_all(cut_along(value, dim, length), axis, 0, 0, tiled=True)  20.8 us
  transfers between devices with their start and end apart: 23, of which 7 were waited for; matrix products, arithmetic and copies ran while one was open for 14% of the time, Pallas kernels for 0%

commit v1 on v0

v1 whole, which is shorter than its diff:
```python
import functools

import jax
import jax.numpy as jnp
from jax import lax
from jax.experimental import pallas as pl
from jax.experimental.pallas import tpu as pltpu
from jax.sharding import Mesh
from jax.sharding import PartitionSpec as P

UNITS = 4096
ITERS = 4
LINE = ("z", "xl")
BUS = ("y", "c")
LINE_BUS = ("z", "xl", "y", "c")
LINE_TM = ("z", "xl", "t")

RAMP_RATES = (0.1, 0.2, 0.4, 0.5)
COST_FACTORS = (1.0, 1.5, 3.0, 0.05)
PRIMAL_STEP = 0.5
DUAL_STEP = 0.5

LINES_DEV = 960
ROWS = 1024
HALF = 496
BLOCK = 256
BF16 = jnp.bfloat16
F32 = jnp.float32
VMEM = pl.BlockSpec(memory_space=pltpu.VMEM)
SMEM = pl.BlockSpec(memory_space=pltpu.SMEM)


def params(mib):
    return pltpu.CompilerParams(vmem_limit_bytes=mib << 20)


def cost_of(flops, size):
    return pl.CostEstimate(flops=flops, bytes_accessed=size, transcendentals=0)


def halves(value):
    high = value.astype(BF16)
    return high, (value - high.astype(F32)).astype(BF16)


def dot(left, right, dims=((1,), (0,))):
    return lax.dot_general(left, right, (dims, ((), ())), preferred_element_type=F32)


def row_index(shape, first):
    return first + lax.broadcasted_iota(jnp.int32, shape, 0)


def picked(kinds, values):
    total = 0.0
    for kind, value in enumerate(values):
        total = total + jnp.where(kinds == kind, value, 0.0)
    return total


def column(row):
    count = row.shape[1]
    same = lax.broadcasted_iota(jnp.int32, (count, count), 0) == lax.broadcasted_iota(
        jnp.int32, (count, count), 1
    )
    return jnp.sum(jnp.where(same, row, jnp.zeros_like(row)), axis=1, keepdims=True)


def table_kernel(place_ref, bus_ref, type_ref, limit_ref, cost_ref, table_ref, first_ref, copies_ref):
    kinds = column(type_ref[...])
    capacity = column(limit_ref[...]).astype(F32) / 100.0
    cost = column(cost_ref[...]) * picked(kinds, COST_FACTORS)
    storage = jnp.where(kinds == 3, 1.0, 0.0)
    lower = -capacity * storage
    lane = lax.broadcasted_iota(jnp.int32, table_ref.shape, 1)
    table = jnp.zeros(table_ref.shape, F32)
    parts = (cost, lower, capacity, picked(kinds, RAMP_RATES) * capacity, storage, 2.0 * capacity)
    for spot, part in enumerate(parts):
        table = jnp.where(lane == spot, part, table)
    table_ref[...] = table
    first = jnp.clip(-PRIMAL_STEP * cost, lower, capacity)
    first_ref[...] = jnp.broadcast_to(first, first_ref.shape)
    bus = column(bus_ref[...] - place_ref[0]).astype(F32)
    sent = jnp.where(lane < 64, 2.0 * first, bus)
    copies_ref[...] = jnp.broadcast_to(sent[None], copies_ref.shape)


def unit_tables(place, unit_bus, unit_type, unit_limit, unit_cost, line_count):
    units = unit_bus.shape[0]
    rows = [x.reshape(1, units) for x in (unit_bus, unit_type, unit_limit, unit_cost)]
    one = jax.ShapeDtypeStruct((units, 128), F32)
    return pl.pallas_call(
        table_kernel,
        in_specs=[SMEM] + [VMEM] * 4,
        out_specs=[VMEM] * 3,
        out_shape=[one, one, jax.ShapeDtypeStruct((line_count, units, 128), F32)],
        compiler_params=params(16),
        name="unit_tables",
    )(place, *rows)


def load_kernel(ptdf_ref, load_ref, out_ref, pair_ref):
    step = pl.program_id(0)

    @pl.when(step == 0)
    def _():
        high, low = halves(load_ref[...])
        pair_ref[:, :128] = high
        pair_ref[:, 128:] = low

    rows = row_index(ptdf_ref.shape, step * BLOCK)
    ptdf = jnp.where(rows < LINES_DEV, ptdf_ref[...], jnp.where(rows == LINES_DEV, 1.0, 0.0))
    high, low = halves(ptdf)
    both = dot(high, pair_ref[...])
    out_ref[...] = -(both[:, :128] + both[:, 128:] + dot(low, pair_ref[:, :128]))


def load_flows(ptdf, load):
    buses = ptdf.shape[1]
    return pl.pallas_call(
        load_kernel,
        grid=(ROWS // BLOCK,),
        in_specs=[
            pl.BlockSpec((BLOCK, buses), lambda i: (i, 0)),
            pl.BlockSpec((buses, 128), lambda i: (0, 0)),
        ],
        out_specs=pl.BlockSpec((BLOCK, 128), lambda i: (i, 0)),
        out_shape=jax.ShapeDtypeStruct((ROWS, 128), F32),
        scratch_shapes=[pltpu.VMEM((buses, 256), BF16)],
        compiler_params=params(48),
        cost_estimate=cost_of(3 * 2 * ROWS * buses * 128, 4 * ROWS * buses),
        name="load_flows",
    )(ptdf, load)


def columns_kernel(ptdf_ref, unit_ref, high_ref, low_ref, pick_ref):
    step = pl.program_id(0)
    span = ptdf_ref.shape[1] // 2
    units = unit_ref.shape[0] // 2

    @pl.when(step == 0)
    def _():
        for group in range(2):
            spots = unit_ref[group * units : (group + 1) * units, 64:65].astype(jnp.int32)
            index = lax.broadcasted_iota(jnp.int32, (units, span), 1) + group * span
            pick_ref[group] = jnp.where(index == spots, 1.0, 0.0).astype(BF16)

    rows = row_index((BLOCK, units), step * BLOCK)
    inside = row_index((BLOCK, span), step * BLOCK) < LINES_DEV
    for group in range(2):
        ptdf = jnp.where(inside, ptdf_ref[:, group * span : (group + 1) * span], 0.0)
        high, low = halves(ptdf)
        pick = pick_ref[group]
        high = dot(high, pick, ((1,), (1,)))
        low = dot(low, pick, ((1,), (1,)))
        where = slice(group * units, (group + 1) * units)
        high_ref[:, where] = jnp.where(rows == LINES_DEV, 1.0, high).astype(BF16)
        low_ref[:, where] = low.astype(BF16)


def unit_columns(ptdf, unit_rows):
    buses = ptdf.shape[1]
    units = unit_rows.shape[0]
    by_row = pl.BlockSpec((BLOCK, units), lambda i: (i, 0))
    return pl.pallas_call(
        columns_kernel,
        grid=(ROWS // BLOCK,),
        in_specs=[
            pl.BlockSpec((BLOCK, buses), lambda i: (i, 0)),
            pl.BlockSpec((units, 128), lambda i: (0, 0)),
        ],
        out_specs=[by_row, by_row],
        out_shape=[jax.ShapeDtypeStruct((ROWS, units), BF16)] * 2,
        scratch_shapes=[pltpu.VMEM((2, units // 2, buses // 2), BF16)],
        compiler_params=params(48),
        cost_estimate=cost_of(2 * 2 * ROWS * buses * units // 2, 4 * ROWS * buses),
        name="unit_columns",
    )(ptdf, unit_rows)


def flow_kernel(first, core_ref, high_ref, low_ref, extrap_ref, *refs):
    core = core_ref[0]
    mine_ref, other_ref = refs[-2:]
    extrap = extrap_ref[...]
    if first:
        extrap = jnp.broadcast_to(extrap[:, :1], extrap.shape)
    high, low = halves(extrap)
    pair = jnp.concatenate([high, low], axis=1)
    for ref, place in ((other_ref, 1 - core), (mine_ref, core)):
        rows = pl.ds(pl.multiple_of(place * HALF, 16), HALF)
        both = dot(high_ref[rows, :], pair)
        flow = both[:, :128] + both[:, 128:] + dot(low_ref[rows, :], high)
        ref[...] = flow + refs[0][rows, :] if first else flow


def unit_flows(core, high, low, extrap, *load):
    half = jax.ShapeDtypeStruct((HALF, 128), F32)
    return pl.pallas_call(
        functools.partial(flow_kernel, bool(load)),
        in_specs=[SMEM] + [VMEM] * (3 + len(load)),
        out_specs=[VMEM, VMEM],
        out_shape=[half, half],
        compiler_params=params(8),
        cost_estimate=cost_of(3 * 2 * ROWS * 512 * 128, 4 * ROWS * 512),
        name="unit_flows",
    )(core, high, low, extrap, *load)


def dual_kernel(left_ref, right_ref, flow_ref, dual_ref, step_ref, limit_ref, flow_out, dual_out):
    flow = flow_ref[...] + (left_ref[...] + right_ref[...])
    flow_out[...] = flow
    moved = dual_ref[...] + step_ref[...] * flow
    limit = limit_ref[...]
    dual_out[...] = moved - jnp.clip(moved, -limit, limit)


def dual_step(left, right, flow, dual, steps, limits):
    half = jax.ShapeDtypeStruct((HALF, 128), F32)
    return pl.pallas_call(
        dual_kernel,
        in_specs=[VMEM] * 6,
        out_specs=[VMEM, VMEM],
        out_shape=[half, half],
        compiler_params=params(8),
        name="dual_step",
    )(left, right, flow, dual, steps, limits)


def price_kernel(core_ref, mine_ref, other_ref, high_ref, low_ref, price_ref, dual_ref):
    core = core_ref[0]
    for ref, place in ((mine_ref, core), (other_ref, 1 - core)):
        dual_ref[pl.ds(pl.multiple_of(place * HALF, 8), HALF), :] = ref[...]
    dual_ref[2 * HALF :, :] = jnp.zeros((ROWS - 2 * HALF, 128), F32)
    high, low = halves(dual_ref[...].T)
    both = dot(jnp.concatenate([high, low], axis=0), high_ref[...])
    price = both[:128] + both[128:] + dot(high, low_ref[...])
    price_ref[...] = price.T


def unit_prices(core, mine, other, high, low):
    units = high.shape[1]
    return pl.pallas_call(
        price_kernel,
        in_specs=[SMEM] + [VMEM] * 4,
        out_specs=VMEM,
        out_shape=jax.ShapeDtypeStruct((units, 128), F32),
        scratch_shapes=[pltpu.VMEM((ROWS, 128), F32)],
        compiler_params=params(8),
        cost_estimate=cost_of(3 * 2 * ROWS * 512 * 128, 4 * ROWS * 512),
        name="unit_prices",
    )(core, mine, other, high, low)


def joined_kernel(core_ref, mine_ref, other_ref, dual_ref):
    first = core_ref[0] == 0
    mine, other = mine_ref[...], other_ref[...]
    dual_ref[:HALF, :] = jnp.where(first, mine, other)
    rest = LINES_DEV - HALF
    dual_ref[HALF:, :] = jnp.where(first, other[:rest], mine[:rest])


def joined(core, mine, other):
    return pl.pallas_call(
        joined_kernel,
        in_specs=[SMEM, VMEM, VMEM],
        out_specs=VMEM,
        out_shape=jax.ShapeDtypeStruct((LINES_DEV, 128), F32),
        compiler_params=params(8),
        name="joined",
    )(core, mine, other)


def unit_kernel(price_ref, gen_ref, old_ref, state_ref, table_ref, gen_out, extrap_ref, copies_ref):
    cost = table_ref[:, 0:1]
    lower = table_ref[:, 1:2]
    upper = table_ref[:, 2:3]
    gen = gen_ref[...]
    peers = price_ref.shape[0]
    prices = []
    for hours in range(2):
        total = price_ref[hours]
        for peer in range(hours + 2, peers, 2):
            total = total + price_ref[peer]
        prices.append(total)
    gradient = cost + jnp.concatenate(prices, axis=1) + state_ref[...]
    updated = jnp.clip(gen - PRIMAL_STEP * gradient, lower, upper)
    extrap = 2.0 * updated - gen
    gen_out[...] = updated
    extrap_ref[...] = extrap
    change = extrap - old_ref[...]
    for peer in range(peers):
        hours = peer % 2
        copies_ref[peer] = change[:, 128 * hours : 128 * (hours + 1)]


def unit_step(prices, gen, old, state, table):
    wide = jax.ShapeDtypeStruct(gen.shape, F32)
    return pl.pallas_call(
        unit_kernel,
        in_specs=[VMEM] * 5,
        out_specs=[VMEM] * 3,
        out_shape=[wide, wide, jax.ShapeDtypeStruct(prices.shape, F32)],
        compiler_params=params(8),
        name="unit_step",
    )(prices, gen, old, state, table)


def state_kernel(extrap_ref, ramp_ref, store_ref, table_ref, ramp_out, store_out, state_ref):
    ramp_limit = DUAL_STEP * table_ref[:, 3:4]
    storage = table_ref[:, 4:5]
    store_limit = DUAL_STEP * table_ref[:, 5:6]
    extrap = extrap_ref[...]
    hour = lax.broadcasted_iota(jnp.int32, extrap.shape, 1)
    hours = extrap.shape[1]
    previous = pltpu.roll(extrap, 1, 1)
    moved = ramp_ref[...] + jnp.where(hour >= 1, DUAL_STEP * (extrap - previous), 0.0)
    ramp = moved - jnp.clip(moved, -ramp_limit, ramp_limit)
    ramp_out[...] = ramp
    early = lax.broadcasted_iota(jnp.int32, (hours, hours), 0)
    late = lax.broadcasted_iota(jnp.int32, (hours, hours), 1)
    forward = jnp.where(early <= late, 1.0, 0.0)
    backward = jnp.where(early >= late, 1.0, 0.0)
    running = jnp.dot(extrap, forward, precision=lax.Precision.HIGHEST, preferred_element_type=F32)
    moved = store_ref[...] + DUAL_STEP * storage * running
    store = moved - jnp.clip(moved, -store_limit, store_limit)
    store_out[...] = store
    suffix = jnp.dot(store, backward, precision=lax.Precision.HIGHEST, preferred_element_type=F32)
    after = jnp.where(hour < hours - 1, pltpu.roll(ramp, hours - 1, 1), 0.0)
    state_ref[...] = ramp - after + storage * suffix


def state_step(extrap, ramp, store, table):
    wide = jax.ShapeDtypeStruct(ramp.shape, F32)
    return pl.pallas_call(
        state_kernel,
        in_specs=[VMEM] * 4,
        out_specs=[VMEM] * 3,
        out_shape=[wide] * 3,
        compiler_params=params(8),
        cost_estimate=cost_of(12 * 2 * 16 * 256 * 256, 1 << 17),
        name="state_step",
    )(extrap, ramp, store, table)


SWAP = ((0, 1), (1, 0))
NEAR = ((0, 1), (1, 0), (2, 3), (3, 2))
FAR = ((1, 2), (2, 1), (3, 0), (0, 3))


def along_y(value, by_core):
    pairs = [(2 * i + core, 2 * j + core) for core in range(2) for i, j in by_core[core]]
    return lax.ppermute(value, BUS, pairs)


def summed_over_bus(mine, other):
    total = mine + lax.ppermute(other, "c", SWAP)
    total = total + along_y(total, (NEAR, FAR))
    return total, along_y(total, (FAR, NEAR))


def on_device(ptdf, bus_load, unit_bus, unit_type, unit_limit, unit_cost, line_rating):
    line_count = lax.axis_size(LINE)
    hour_dev = bus_load.shape[1]
    local = unit_bus.shape[0]
    core = lax.axis_index("c").astype(jnp.int32)
    half_units = local // 2
    block = (lax.axis_index(BUS) * ptdf.shape[1]).astype(jnp.int32)
    table, first, copies = unit_tables(
        block[None], unit_bus, unit_type, unit_limit, unit_cost, line_count
    )
    unit_rows = lax.all_to_all(copies, LINE, 0, 0, tiled=True)
    unit_rows = unit_rows.reshape(line_count * local, hour_dev)
    load = load_flows(ptdf, bus_load)
    high, low = unit_columns(ptdf, unit_rows)

    own = lax.axis_index("t") * half_units
    table = lax.dynamic_slice_in_dim(table, own, half_units, 0)
    own_first = lax.dynamic_slice_in_dim(first, own, half_units, 0)
    gen = jnp.concatenate([own_first, own_first], axis=1)
    extrap = 2.0 * gen

    pad = jnp.zeros((2 * HALF - LINES_DEV,), F32)
    limits = jnp.concatenate([DUAL_STEP * (line_rating.astype(F32) / 100.0), pad])
    index = core * HALF + jnp.arange(HALF, dtype=jnp.int32)
    weight = 1.0 / (UNITS * 16)
    steps = jnp.where(index < LINES_DEV, DUAL_STEP, jnp.where(index == LINES_DEV, weight, 0.0))
    steps = steps.astype(F32)[:, None]
    limits = lax.dynamic_slice_in_dim(limits, core * HALF, HALF, 0)[:, None]
    core = core[None]
    flow = dual = jnp.zeros((HALF, hour_dev), F32)
    ramp = store = jnp.zeros((half_units, 2 * hour_dev), F32)
    mine, other = unit_flows(core, high, low, unit_rows, load)
    for iteration in range(ITERS):
        last = iteration == ITERS - 1
        if not last:
            ramp, store, state = state_step(extrap, ramp, store, table)
        left, right = summed_over_bus(mine, other)
        if not last:
            right, state, ramp, store = lax.optimization_barrier((right, state, ramp, store))
        flow, dual = dual_step(left, right, flow, dual, steps, limits)
        far = lax.ppermute(dual, "c", SWAP)
        if last:
            break
        prices = unit_prices(core, dual, far, high, low)
        prices = prices.reshape(2 * line_count, half_units, hour_dev)
        prices = lax.all_to_all(prices, LINE_TM, 0, 0, tiled=True)
        gen, extrap, copies = unit_step(prices, gen, extrap, state, table)
        changes = lax.all_to_all(copies, LINE_TM, 0, 0, tiled=True)
        mine, other = unit_flows(core, high, low, changes.reshape(-1, hour_dev))
    first_hours = lax.axis_index("t") == 0
    sent = jnp.where(first_hours, gen[:, hour_dev:], gen[:, :hour_dev])
    kept = jnp.where(first_hours, gen[:, :hour_dev], gen[:, hour_dev:])
    got = lax.ppermute(sent, "t", SWAP)
    upper_half = jnp.where(first_hours, kept, got)
    lower_half = jnp.where(first_hours, got, kept)
    return jnp.concatenate([upper_half, lower_half], axis=0), joined(core, dual, far)


def solution(mesh):
    finer = Mesh(
        mesh.devices.reshape(8, 2, 4, 2, mesh.shape["tm"]),
        ("z", "xl", "y", "c", "t"),
    )
    return jax.shard_map(
        on_device,
        mesh=finer,
        in_specs=(
            P(LINE, BUS),
            P(BUS, "t"),
            P(LINE_BUS),
            P(LINE_BUS),
            P(LINE_BUS),
            P(LINE_BUS),
            P(LINE),
        ),
        out_specs=(P(LINE_BUS, "t"), P(LINE, "t")),
        check_vma=False,
    )
```

time: 398 us -> 209 us (0.53)
  blocking collectives: 145 us -> 90.2 us
  matrix products: 45.4 us -> 0 us
  starting transfers between devices: 79.6 us -> 46 us
  waiting for transfers between devices: 72.2 us -> 45.5 us
  Pallas kernels: 0 us -> 21.2 us
  other arithmetic: 20.5 us -> 0.95 us
  local copies, waits for them, and re-layouts: 19.1 us -> 3.99 us
  between operations: 14.3 us -> 0.87 us
    psum x12 -> x0, blocking collectives: 106 us -> none  [over_axes(): value = lax.psum(value, axis)]
    all_to_all x3 -> x6, blocking collectives: 38.8 us -> 90.2 us  [the longest x3 45.9 us: on_device(): prices = lax.all_to_all(prices, LINE_TM, 0, 0, tiled=True)]
    all_to_all x12 -> x1, starting transfers between devices: 58.2 us -> 10 us  [on_device(): unit_rows = lax.all_to_all(copies, LINE, 0, 0, tiled=True)]
    dot_general x16 -> x0, matrix products: 45.4 us -> none  [the longest x12 31.3 us: products(): jnp.dot(left, right, precision=lax.Precision.HIGHEST, preferred_element_t...]
    ppermute x7 -> x17, waiting for transfers between devices: 0.83 us -> 40.7 us  [the longest x8 32.2 us: along_y(): return lax.ppermute(value, BUS, pairs)]
    all_to_all x12 -> x1, waiting for transfers between devices: 40 us -> 4.71 us  [on_device(): unit_rows = lax.all_to_all(copies, LINE, 0, 0, tiled=True)]
    all_gather x4 -> x0, waiting for transfers between devices: 31.3 us -> none  [gathered_total(): return lax.all_gather(value, axis).sum(0)]
    pallas_call x0 -> x21, Pallas kernels: none -> 21.2 us  [the longest x1 4.95 us: unit_columns(): pl.pallas_call(columns_kernel, grid=(ROWS // BLOCK,), in_specs=[pl.BlockS...]
  transfers between devices with their start and end apart: 23 -> 18, of which waited for: 7 -> 17; matrix products, arithmetic and copies ran while one was open for 14% -> 0% of each run, Pallas kernels for 0% -> 4%
where the time goes in v1:
time: 209 us
  blocking collectives  90.2 us (43%)
  starting transfers between devices  46 us (22%)
  waiting for transfers between devices  45.5 us (22%)
  Pallas kernels  21.2 us (10%)
  local copies, waits for them, and re-layouts  3.99 us (2%)
    all_to_all x3, blocking collectives, on_device(): prices = lax.all_to_all(prices, LINE_TM, 0, 0, tiled=True)  45.9 us
    all_to_all x3, blocking collectives, on_device(): changes = lax.all_to_all(copies, LINE_TM, 0, 0, tiled=True)  44.4 us
    ppermute x8, waiting for transfers between devices, along_y(): return lax.ppermute(value, BUS, pairs)  32.2 us
    ppermute x4, starting transfers between devices, summed_over_bus(): total = mine + lax.ppermute(other, 'c', SWAP)  13.1 us
    ppermute x8, starting transfers between devices, along_y(): return lax.ppermute(value, BUS, pairs)  12 us
    all_to_all x1, starting transfers between devices, on_device(): unit_rows = lax.all_to_all(copies, LINE, 0, 0, tiled=True)  10 us
    ppermute x4, starting transfers between devices, on_device(): far = lax.ppermute(dual, 'c', SWAP)  9.51 us
    pallas_call x1, Pallas kernels, unit_columns(): pl.pallas_call(columns_kernel, grid=(ROWS // BLOCK,), in_specs=[pl.BlockS...  4.95 us
  transfers between devices with their start and end apart: 18, of which 17 were waited for; matrix products, arithmetic and copies ran while one was open for 0% of the time, Pallas kernels for 4%

profile of v1, /device:TPU:1, one launch (start us, length us, event | category | flops | bytes accessed | tf_op | source)
XLA Modules:
  0.0 208.7 jit_solution(4486016729594956857)
XLA Ops:
  4.1 10.0 %all-to-all-start = ((f32[16,32,128]{2,1,0:T(8,128)}), f32[16,32,128]{2,1,0:T(8,128)S(1)}, u32[]{:S(2)}, u32[]{:S(2)}) async-start(f32[16,32,128]{2,1,0:T(8,128)} %get-tuple-element.47), calls=%async_computation | async-start | bytes 524288 | tf_op jit(solution)/shard_map/all_to_all | solution.py:371
  15.3 4.7 %load_flows.1.refs_0_ = f32[1024,128]{1,0:T(8,128)S(1)} custom-call(f32[960,1536]{1,0:T(8,128)} %ptdf_ref.3, f32[1536,128]{1,0:T(8,128)S(1)} %copy-done), custom_call_target="tpu_custom_call" | custom-call | flops 1207959552 | bytes 6291456 | tf_op jit(solution)/shard_map/load_flows/pallas_call | solution.py:120
  20.0 4.7 %all-to-all-done = f32[16,32,128]{2,1,0:T(8,128)S(1)} async-done(((f32[16,32,128]{2,1,0:T(8,128)}), f32[16,32,128]{2,1,0:T(8,128)S(1)}, u32[]{:S(2)}, u32[]{:S(2)}) %all-to-all-start) | async-done | bytes 262176 | tf_op jit(solution)/shard_map/all_to_all | solution.py:371
  24.7 4.9 %unit_columns.1 = (bf16[1024,512]{1,0:T(8,128)(2,1)S(1)}, bf16[1024,512]{1,0:T(8,128)(2,1)S(1)}) custom-call(f32[960,1536]{1,0:T(8,128)} %ptdf_ref.3, f32[512,128]{1,0:T(8,128)S(1)} %bitcast.14), custom_call_target="tpu_custom_call" | custom-call | flops 1610612736 | bytes 6291456 | tf_op jit(solution)/shard_map/unit_columns/pallas_call | solution.py:165
  34.1 2.8 %collective-permute-start.1 = (f32[496,128]{1,0:T(8,128)S(1)}, f32[496,128]{1,0:T(8,128)S(1)}, u32[]{:S(2)}, u32[]{:S(2)}) collective-permute-start(f32[496,128]{1,0:T(8,128)S(1)} %add.50), channel_id=1, source_target_pairs={{0,4},{4,0},{8,12},{12,8},{6,10},{10,6},{14,2},{2,14},{1,5},{5,1},... | collective-permute-start | bytes 761864 | tf_op jit(solution)/shard_map/ppermute | solution.py:352
  36.9 3.7 %collective-permute-done.1 = f32[496,128]{1,0:T(8,128)S(1)} collective-permute-done((f32[496,128]{1,0:T(8,128)S(1)}, f32[496,128]{1,0:T(8,128)S(1)}, u32[]{:S(2)}, u32[]{:S(2)}) %collective-permute-start.1) | collective-permute-done | bytes 253984 | tf_op jit(solution)/shard_map/ppermute | solution.py:352
  42.0 4.2 %collective-permute-done.2.right_ref = f32[496,128]{1,0:T(8,128)S(1)} collective-permute-done((f32[496,128]{1,0:T(8,128)S(1)}, f32[496,128]{1,0:T(8,128)S(1)}, u32[]{:S(2)}, u32[]{:S(2)}) %collective-permute-start.2) | collective-permute-done | bytes 253984 | tf_op jit(solution)/shard_map/ppermute | solution.py:352
  50.8 16.2 %all_to_all.35.price_ref = f32[32,16,128]{2,1,0:T(8,128)S(1)} all-to-all(f32[32,16,128]{2,1,0:T(8,128)S(1)} %bitcast.19), channel_id=1, replica_groups=mesh['z'=8,'xl'=2,'y'=4,'c'=2,'t'=2] {'z','xl','t'}, dimensions={0} | all-to-all | bytes 524288 | tf_op jit(solution)/shard_map/all_to_all | solution.py:406
  67.1 14.8 %all_to_all.36 = f32[32,16,128]{2,1,0:T(8,128)S(1)} all-to-all(f32[32,16,128]{2,1,0:T(8,128)S(1)} %get-tuple-element.60), channel_id=1, replica_groups=mesh['z'=8,'xl'=2,'y'=4,'c'=2,'t'=2] {'z','xl','t'}, dimensions={0} | all-to-all | bytes 524288 | tf_op jit(solution)/shard_map/all_to_all | solution.py:408
  82.6 3.6 %collective-permute-start.4 = (f32[496,128]{1,0:T(8,128)S(1)}, f32[496,128]{1,0:T(8,128)S(1)}, u32[]{:S(2)}, u32[]{:S(2)}) collective-permute-start(f32[496,128]{1,0:T(8,128)S(1)} %get-tuple-element.62), channel_id=1, source_target_pairs={{0,2},{2,0},{1,3},{3,1},{4,6},{6,4},{5,7},{7,5},{8,10},{10,8},{9,1... | collective-permute-start | bytes 761864 | tf_op jit(solution)/shard_map/ppermute | solution.py:356
  87.3 2.8 %collective-permute-start.5 = (f32[496,128]{1,0:T(8,128)S(1)}, f32[496,128]{1,0:T(8,128)S(1)}, u32[]{:S(2)}, u32[]{:S(2)}) collective-permute-start(f32[496,128]{1,0:T(8,128)S(1)} %add.56), channel_id=1, source_target_pairs={{0,4},{4,0},{8,12},{12,8},{6,10},{10,6},{14,2},{2,14},{1,5},{5,1},... | collective-permute-start | bytes 761864 | tf_op jit(solution)/shard_map/ppermute | solution.py:352
  90.1 3.7 %collective-permute-done.5 = f32[496,128]{1,0:T(8,128)S(1)} collective-permute-done((f32[496,128]{1,0:T(8,128)S(1)}, f32[496,128]{1,0:T(8,128)S(1)}, u32[]{:S(2)}, u32[]{:S(2)}) %collective-permute-start.5) | collective-permute-done | bytes 253984 | tf_op jit(solution)/shard_map/ppermute | solution.py:352
  94.5 4.8 %collective-permute-done.6.right_ref = f32[496,128]{1,0:T(8,128)S(1)} collective-permute-done((f32[496,128]{1,0:T(8,128)S(1)}, f32[496,128]{1,0:T(8,128)S(1)}, u32[]{:S(2)}, u32[]{:S(2)}) %collective-permute-start.6) | collective-permute-done | bytes 253984 | tf_op jit(solution)/shard_map/ppermute | solution.py:352
  104.0 14.8 %all_to_all.37.price_ref = f32[32,16,128]{2,1,0:T(8,128)S(1)} all-to-all(f32[32,16,128]{2,1,0:T(8,128)S(1)} %bitcast.20), channel_id=1, replica_groups=mesh['z'=8,'xl'=2,'y'=4,'c'=2,'t'=2] {'z','xl','t'}, dimensions={0} | all-to-all | bytes 524288 | tf_op jit(solution)/shard_map/all_to_all | solution.py:406
  118.9 14.8 %all_to_all.38 = f32[32,16,128]{2,1,0:T(8,128)S(1)} all-to-all(f32[32,16,128]{2,1,0:T(8,128)S(1)} %get-tuple-element.74), channel_id=1, replica_groups=mesh['z'=8,'xl'=2,'y'=4,'c'=2,'t'=2] {'z','xl','t'}, dimensions={0} | all-to-all | bytes 524288 | tf_op jit(solution)/shard_map/all_to_all | solution.py:408
  134.4 3.6 %collective-permute-start.8 = (f32[496,128]{1,0:T(8,128)S(1)}, f32[496,128]{1,0:T(8,128)S(1)}, u32[]{:S(2)}, u32[]{:S(2)}) collective-permute-start(f32[496,128]{1,0:T(8,128)S(1)} %get-tuple-element.76), channel_id=1, source_target_pairs={{0,2},{2,0},{1,3},{3,1},{4,6},{6,4},{5,7},{7,5},{8,10},{10,8},{9,1... | collective-permute-start | bytes 761864 | tf_op jit(solution)/shard_map/ppermute | solution.py:356
  142.0 3.7 %collective-permute-done.9 = f32[496,128]{1,0:T(8,128)S(1)} collective-permute-done((f32[496,128]{1,0:T(8,128)S(1)}, f32[496,128]{1,0:T(8,128)S(1)}, u32[]{:S(2)}, u32[]{:S(2)}) %collective-permute-start.9) | collective-permute-done | bytes 253984 | tf_op jit(solution)/shard_map/ppermute | solution.py:352
  146.8 4.4 %collective-permute-done.10.right_ref = f32[496,128]{1,0:T(8,128)S(1)} collective-permute-done((f32[496,128]{1,0:T(8,128)S(1)}, f32[496,128]{1,0:T(8,128)S(1)}, u32[]{:S(2)}, u32[]{:S(2)}) %collective-permute-start.10) | collective-permute-done | bytes 253984 | tf_op jit(solution)/shard_map/ppermute | solution.py:352
  155.8 14.8 %all_to_all.39.price_ref = f32[32,16,128]{2,1,0:T(8,128)S(1)} all-to-all(f32[32,16,128]{2,1,0:T(8,128)S(1)} %bitcast.21), channel_id=1, replica_groups=mesh['z'=8,'xl'=2,'y'=4,'c'=2,'t'=2] {'z','xl','t'}, dimensions={0} | all-to-all | bytes 524288 | tf_op jit(solution)/shard_map/all_to_all | solution.py:406
  171.3 14.8 %all_to_all.40 = f32[32,16,128]{2,1,0:T(8,128)S(1)} all-to-all(f32[32,16,128]{2,1,0:T(8,128)S(1)} %get-tuple-element.87), channel_id=1, replica_groups=mesh['z'=8,'xl'=2,'y'=4,'c'=2,'t'=2] {'z','xl','t'}, dimensions={0} | all-to-all | bytes 524288 | tf_op jit(solution)/shard_map/all_to_all | solution.py:408
  186.8 3.6 %collective-permute-start.13 = (f32[496,128]{1,0:T(8,128)S(1)}, f32[496,128]{1,0:T(8,128)S(1)}, u32[]{:S(2)}, u32[]{:S(2)}) collective-permute-start(f32[496,128]{1,0:T(8,128)S(1)} %get-tuple-element.89), channel_id=1, source_target_pairs={{0,2},{2,0},{1,3},{3,1},{4,6},{6,4},{5,7},{7,5},{8,10},{10,8},{9,1... | collective-permute-start | bytes 761864 | tf_op jit(solution)/shard_map/ppermute | solution.py:356
  191.5 2.8 %collective-permute-start.14 = (f32[496,128]{1,0:T(8,128)S(1)}, f32[496,128]{1,0:T(8,128)S(1)}, u32[]{:S(2)}, u32[]{:S(2)}) collective-permute-start(f32[496,128]{1,0:T(8,128)S(1)} %add.60), channel_id=1, source_target_pairs={{0,4},{4,0},{8,12},{12,8},{6,10},{10,6},{14,2},{2,14},{1,5},{5,1},... | collective-permute-start | bytes 761864 | tf_op jit(solution)/shard_map/ppermute | solution.py:352
  194.4 3.7 %collective-permute-done.14 = f32[496,128]{1,0:T(8,128)S(1)} collective-permute-done((f32[496,128]{1,0:T(8,128)S(1)}, f32[496,128]{1,0:T(8,128)S(1)}, u32[]{:S(2)}, u32[]{:S(2)}) %collective-permute-start.14) | collective-permute-done | bytes 253984 | tf_op jit(solution)/shard_map/ppermute | solution.py:352
  199.5 4.1 %collective-permute-done.15.right_ref = f32[496,128]{1,0:T(8,128)S(1)} collective-permute-done((f32[496,128]{1,0:T(8,128)S(1)}, f32[496,128]{1,0:T(8,128)S(1)}, u32[]{:S(2)}, u32[]{:S(2)}) %collective-permute-start.15) | collective-permute-done | bytes 253984 | tf_op jit(solution)/shard_map/ppermute | solution.py:352
  (70 shorter events, 41.9 us)
Async XLA Ops:
  0.6 0.7 copy-start.1
  1.3 0.7 copy-start.2
  2.0 0.7 copy-start.3
  2.6 0.7 copy-start.4
  4.1 20.6 %all-to-all-start = ((f32[16,32,128]{2,1,0:T(8,128)}), f32[16,32,128]{2,1,0:T(8,128)S(1)}, u32[]{:S(2)}, u32[]{:S(2)}) async-start(f32[16,32,128]{2,1,0:T(8,128)} %get-tuple-element.47), calls=%async_computation | async-start | bytes 524288 | tf_op jit(solution)/shard_map/all_to_all | solution.py:371
  14.1 1.1 copy-start
  20.0 16.9 %copy-start.5 = (s32[960]{0:T(1024)S(1)}, s32[960]{0:T(1024)}, u32[]{:S(2)}) copy-start(s32[960]{0:T(1024)} %param.13) | copy-start | bytes 11524
  30.4 3.6 %collective-permute-start = (f32[496,128]{1,0:T(8,128)S(1)}, f32[496,128]{1,0:T(8,128)S(1)}, u32[]{:S(2)}, u32[]{:S(2)}) collective-permute-start(f32[496,128]{1,0:T(8,128)S(1)} %get-tuple-element.51), channel_id=1, source_target_pairs={{0,2},{2,0},{1,3},{3,1},{4,6},{6,4},{5,7},{7,5},{8,10},{10,8},{9,1... | collective-permute-start | bytes 761864 | tf_op jit(solution)/shard_map/ppermute | solution.py:356
  34.1 6.5 %collective-permute-start.1 = (f32[496,128]{1,0:T(8,128)S(1)}, f32[496,128]{1,0:T(8,128)S(1)}, u32[]{:S(2)}, u32[]{:S(2)}) collective-permute-start(f32[496,128]{1,0:T(8,128)S(1)} %add.50), channel_id=1, source_target_pairs={{0,4},{4,0},{8,12},{12,8},{6,10},{10,6},{14,2},{2,14},{1,5},{5,1},... | collective-permute-start | bytes 761864 | tf_op jit(solution)/shard_map/ppermute | solution.py:352
  40.6 5.5 %collective-permute-start.2 = (f32[496,128]{1,0:T(8,128)S(1)}, f32[496,128]{1,0:T(8,128)S(1)}, u32[]{:S(2)}, u32[]{:S(2)}) collective-permute-start(f32[496,128]{1,0:T(8,128)S(1)} %add.51.left_ref), channel_id=1, source_target_pairs={{4,8},{8,4},{12,0},{0,12},{2,6},{6,2},{10,14},{14,10},{5,9},{9,5},... | collective-permute-start | bytes 761864 | tf_op jit(solution)/shard_map/ppermute | solution.py:352
  46.5 3.5 %collective-permute-start.3 = (f32[496,128]{1,0:T(8,128)S(1)}, f32[496,128]{1,0:T(8,128)S(1)}, u32[]{:S(2)}, u32[]{:S(2)}) collective-permute-start(f32[496,128]{1,0:T(8,128)S(1)} %get-tuple-element.58.mine_ref.dual_ref), channel_id=1, source_target_pairs={{0,2},{2,0},{1,3},{3,1},{4,6},{6,4},{5,7},{7,5},{8,10},{10,8},{9,1... | collective-permute-start | bytes 761864 | tf_op jit(solution)/shard_map/ppermute | solution.py:401
  82.6 4.7 %collective-permute-start.4 = (f32[496,128]{1,0:T(8,128)S(1)}, f32[496,128]{1,0:T(8,128)S(1)}, u32[]{:S(2)}, u32[]{:S(2)}) collective-permute-start(f32[496,128]{1,0:T(8,128)S(1)} %get-tuple-element.62), channel_id=1, source_target_pairs={{0,2},{2,0},{1,3},{3,1},{4,6},{6,4},{5,7},{7,5},{8,10},{10,8},{9,1... | collective-permute-start | bytes 761864 | tf_op jit(solution)/shard_map/ppermute | solution.py:356
  87.3 6.5 %collective-permute-start.5 = (f32[496,128]{1,0:T(8,128)S(1)}, f32[496,128]{1,0:T(8,128)S(1)}, u32[]{:S(2)}, u32[]{:S(2)}) collective-permute-start(f32[496,128]{1,0:T(8,128)S(1)} %add.56), channel_id=1, source_target_pairs={{0,4},{4,0},{8,12},{12,8},{6,10},{10,6},{14,2},{2,14},{1,5},{5,1},... | collective-permute-start | bytes 761864 | tf_op jit(solution)/shard_map/ppermute | solution.py:352
  93.8 5.5 %collective-permute-start.6 = (f32[496,128]{1,0:T(8,128)S(1)}, f32[496,128]{1,0:T(8,128)S(1)}, u32[]{:S(2)}, u32[]{:S(2)}) collective-permute-start(f32[496,128]{1,0:T(8,128)S(1)} %add.57.left_ref), channel_id=1, source_target_pairs={{4,8},{8,4},{12,0},{0,12},{2,6},{6,2},{10,14},{14,10},{5,9},{9,5},... | collective-permute-start | bytes 761864 | tf_op jit(solution)/shard_map/ppermute | solution.py:352
  99.6 3.5 %collective-permute-start.7 = (f32[496,128]{1,0:T(8,128)S(1)}, f32[496,128]{1,0:T(8,128)S(1)}, u32[]{:S(2)}, u32[]{:S(2)}) collective-permute-start(f32[496,128]{1,0:T(8,128)S(1)} %get-tuple-element.71.mine_ref.dual_ref), channel_id=1, source_target_pairs={{0,2},{2,0},{1,3},{3,1},{4,6},{6,4},{5,7},{7,5},{8,10},{10,8},{9,1... | collective-permute-start | bytes 761864 | tf_op jit(solution)/shard_map/ppermute | solution.py:401
  134.4 4.7 %collective-permute-start.8 = (f32[496,128]{1,0:T(8,128)S(1)}, f32[496,128]{1,0:T(8,128)S(1)}, u32[]{:S(2)}, u32[]{:S(2)}) collective-permute-start(f32[496,128]{1,0:T(8,128)S(1)} %get-tuple-element.76), channel_id=1, source_target_pairs={{0,2},{2,0},{1,3},{3,1},{4,6},{6,4},{5,7},{7,5},{8,10},{10,8},{9,1... | collective-permute-start | bytes 761864 | tf_op jit(solution)/shard_map/ppermute | solution.py:356
  139.1 6.5 %collective-permute-start.9 = (f32[496,128]{1,0:T(8,128)S(1)}, f32[496,128]{1,0:T(8,128)S(1)}, u32[]{:S(2)}, u32[]{:S(2)}) collective-permute-start(f32[496,128]{1,0:T(8,128)S(1)} %add.58), channel_id=1, source_target_pairs={{0,4},{4,0},{8,12},{12,8},{6,10},{10,6},{14,2},{2,14},{1,5},{5,1},... | collective-permute-start | bytes 761864 | tf_op jit(solution)/shard_map/ppermute | solution.py:352
  145.7 5.5 %collective-permute-start.10 = (f32[496,128]{1,0:T(8,128)S(1)}, f32[496,128]{1,0:T(8,128)S(1)}, u32[]{:S(2)}, u32[]{:S(2)}) collective-permute-start(f32[496,128]{1,0:T(8,128)S(1)} %add.59.left_ref), channel_id=1, source_target_pairs={{4,8},{8,4},{12,0},{0,12},{2,6},{6,2},{10,14},{14,10},{5,9},{9,5},... | collective-permute-start | bytes 761864 | tf_op jit(solution)/shard_map/ppermute | solution.py:352
  151.5 3.6 %collective-permute-start.11 = (f32[496,128]{1,0:T(8,128)S(1)}, f32[496,128]{1,0:T(8,128)S(1)}, u32[]{:S(2)}, u32[]{:S(2)}) collective-permute-start(f32[496,128]{1,0:T(8,128)S(1)} %get-tuple-element.83.mine_ref.dual_ref), channel_id=1, source_target_pairs={{0,2},{2,0},{1,3},{3,1},{4,6},{6,4},{5,7},{7,5},{8,10},{10,8},{9,1... | collective-permute-start | bytes 761864 | tf_op jit(solution)/shard_map/ppermute | solution.py:401
  186.8 4.7 %collective-permute-start.13 = (f32[496,128]{1,0:T(8,128)S(1)}, f32[496,128]{1,0:T(8,128)S(1)}, u32[]{:S(2)}, u32[]{:S(2)}) collective-permute-start(f32[496,128]{1,0:T(8,128)S(1)} %get-tuple-element.89), channel_id=1, source_target_pairs={{0,2},{2,0},{1,3},{3,1},{4,6},{6,4},{5,7},{7,5},{8,10},{10,8},{9,1... | collective-permute-start | bytes 761864 | tf_op jit(solution)/shard_map/ppermute | solution.py:356
  191.5 6.5 %collective-permute-start.14 = (f32[496,128]{1,0:T(8,128)S(1)}, f32[496,128]{1,0:T(8,128)S(1)}, u32[]{:S(2)}, u32[]{:S(2)}) collective-permute-start(f32[496,128]{1,0:T(8,128)S(1)} %add.60), channel_id=1, source_target_pairs={{0,4},{4,0},{8,12},{12,8},{6,10},{10,6},{14,2},{2,14},{1,5},{5,1},... | collective-permute-start | bytes 761864 | tf_op jit(solution)/shard_map/ppermute | solution.py:352
  198.1 5.5 %collective-permute-start.15 = (f32[496,128]{1,0:T(8,128)S(1)}, f32[496,128]{1,0:T(8,128)S(1)}, u32[]{:S(2)}, u32[]{:S(2)}) collective-permute-start(f32[496,128]{1,0:T(8,128)S(1)} %add.61.left_ref), channel_id=1, source_target_pairs={{4,8},{8,4},{12,0},{0,12},{2,6},{6,2},{10,14},{14,10},{5,9},{9,5},... | collective-permute-start | bytes 761864 | tf_op jit(solution)/shard_map/ppermute | solution.py:352
  198.2 8.5 %collective-permute-start.12 = (f32[16,128]{1,0:T(8,128)S(1)}, f32[16,128]{1,0:T(8,128)S(1)}, u32[]{:S(2)}, u32[]{:S(2)}) collective-permute-start(f32[16,128]{1,0:T(8,128)S(1)} %slice_select_fusion), channel_id=1, source_target_pairs={{0,1},{1,0},{2,3},{3,2},{4,5},{5,4},{6,7},{7,6},{8,9},{9,8},{10,11... | collective-permute-start | bytes 24584 | tf_op jit(solution)/shard_map/ppermute | solution.py:413
  204.4 3.5 %collective-permute-start.16 = (f32[496,128]{1,0:T(8,128)S(1)}, f32[496,128]{1,0:T(8,128)S(1)}, u32[]{:S(2)}, u32[]{:S(2)}) collective-permute-start(f32[496,128]{1,0:T(8,128)S(1)} %get-tuple-element.91.mine_ref), channel_id=1, source_target_pairs={{0,2},{2,0},{1,3},{3,1},{4,6},{6,4},{5,7},{7,5},{8,10},{10,8},{9,1... | collective-permute-start | bytes 761864 | tf_op jit(solution)/shard_map/ppermute | solution.py:401

commit v2 on v1

v2 whole, which is shorter than its diff:
```python
import functools

import jax
import jax.numpy as jnp
from jax import lax
from jax.experimental import pallas as pl
from jax.experimental.pallas import tpu as pltpu
from jax.sharding import Mesh
from jax.sharding import PartitionSpec as P

UNITS = 4096
ITERS = 4
LINE = ("z", "xl")
BUS = ("y", "c")
LINE_BUS = ("z", "xl", "y", "c")

RAMP_RATES = (0.1, 0.2, 0.4, 0.5)
COST_FACTORS = (1.0, 1.5, 3.0, 0.05)
PRIMAL_STEP = 0.5
DUAL_STEP = 0.5

LINES_DEV = 960
ROWS = 1024
HALF = 496
BLOCK = 256
PART = 248
BF16 = jnp.bfloat16
F32 = jnp.float32
VMEM = pl.BlockSpec(memory_space=pltpu.VMEM)
SMEM = pl.BlockSpec(memory_space=pltpu.SMEM)


def params(mib):
    return pltpu.CompilerParams(vmem_limit_bytes=mib << 20)


def cost_of(flops, size):
    return pl.CostEstimate(flops=flops, bytes_accessed=size, transcendentals=0)


def halves(value):
    high = value.astype(BF16)
    return high, (value - high.astype(F32)).astype(BF16)


def dot(left, right, dims=((1,), (0,))):
    return lax.dot_general(left, right, (dims, ((), ())), preferred_element_type=F32)


def row_index(shape, first):
    return first + lax.broadcasted_iota(jnp.int32, shape, 0)


def picked(kinds, values):
    total = 0.0
    for kind, value in enumerate(values):
        total = total + jnp.where(kinds == kind, value, 0.0)
    return total


def column(row):
    count = row.shape[1]
    same = lax.broadcasted_iota(jnp.int32, (count, count), 0) == lax.broadcasted_iota(
        jnp.int32, (count, count), 1
    )
    return jnp.sum(jnp.where(same, row, jnp.zeros_like(row)), axis=1, keepdims=True)


def table_kernel(
    place_ref, bus_in, type_in, limit_in, cost_in, load_in, table_ref, first_ref, copies_ref, load_ref,
    bus_ref, type_ref, limit_ref, cost_ref, arrived
):
    pairs = (
        (bus_in, bus_ref.at[0]),
        (type_in, type_ref.at[0]),
        (limit_in, limit_ref.at[0]),
        (cost_in, cost_ref.at[0]),
        (load_in, load_ref),
    )
    copies = [pltpu.make_async_copy(*pair, arrived.at[spot]) for spot, pair in enumerate(pairs)]
    for copy in copies:
        copy.start()
    for copy in copies[:-1]:
        copy.wait()
    kinds = column(type_ref[...])
    capacity = column(limit_ref[...]).astype(F32) / 100.0
    cost = column(cost_ref[...]) * picked(kinds, COST_FACTORS)
    storage = jnp.where(kinds == 3, 1.0, 0.0)
    lower = -capacity * storage
    lane = lax.broadcasted_iota(jnp.int32, table_ref.shape, 1)
    table = jnp.zeros(table_ref.shape, F32)
    parts = (cost, lower, capacity, picked(kinds, RAMP_RATES) * capacity, storage, 2.0 * capacity)
    for spot, part in enumerate(parts):
        table = jnp.where(lane == spot, part, table)
    table_ref[...] = table
    first = jnp.clip(-PRIMAL_STEP * cost, lower, capacity)
    first_ref[...] = jnp.broadcast_to(first, first_ref.shape)
    bus = column(bus_ref[...] - place_ref[0]).astype(F32)
    same = lane == lax.broadcasted_iota(jnp.int32, table_ref.shape, 0)
    bus = jnp.sum(jnp.where(same, bus, 0.0), axis=0, keepdims=True)
    extrap = jnp.sum(jnp.where(same, 2.0 * first, 0.0), axis=0, keepdims=True)
    sent = jnp.where(lax.broadcasted_iota(jnp.int32, (8, 128), 0) == 0, bus, extrap)
    copies_ref[...] = jnp.broadcast_to(sent[None], copies_ref.shape)
    copies[-1].wait()


def unit_tables(place, unit_bus, unit_type, unit_limit, unit_cost, load, line_count):
    units = unit_bus.shape[0]
    rows = (unit_bus, unit_type, unit_limit, unit_cost)
    one = jax.ShapeDtypeStruct((units, 128), F32)
    return pl.pallas_call(
        table_kernel,
        in_specs=[SMEM] + [pl.BlockSpec(memory_space=pltpu.HBM)] * 5,
        out_specs=[VMEM] * 4,
        out_shape=[
            one,
            one,
            jax.ShapeDtypeStruct((line_count, 8, 128), F32),
            jax.ShapeDtypeStruct(load.shape, F32),
        ],
        scratch_shapes=[pltpu.VMEM((1, units), row.dtype) for row in rows]
        + [pltpu.SemaphoreType.DMA((5,))],
        compiler_params=params(16),
        name="unit_tables",
    )(place, *(pltpu.with_memory_space_constraint(x, pltpu.HBM) for x in (*rows, load)))


def first_kernel(core_ref, ptdf_ref, unit_ref, load_ref, mine_ref, other_ref, pair_ref):
    step = pl.program_id(0)

    @pl.when(step == 0)
    def _():
        peers = unit_ref.shape[0]
        span = load_ref.shape[0] // peers
        units = 32
        lane = lax.broadcasted_iota(jnp.int32, (span, 128), 1)
        for peer in range(peers):
            spots = unit_ref[peer][0:1, :].astype(jnp.int32)
            bus = row_index((span, 128), peer * span)
            held = jnp.where((bus == spots) & (lane < units), unit_ref[peer][1:2, :], 0.0)
            rows = slice(peer * span, (peer + 1) * span)
            injection = jnp.sum(held, axis=1, keepdims=True) - load_ref[rows, :]
            high, low = halves(injection)
            pair_ref[rows, :128] = high
            pair_ref[rows, 128:] = low

    rows = row_index(ptdf_ref.shape, step * PART)
    ptdf = jnp.where(rows < LINES_DEV, ptdf_ref[...], jnp.where(rows == LINES_DEV, 1.0, 0.0))
    high, low = halves(ptdf)
    both = dot(high, pair_ref[...])
    flow = both[:, :128] + both[:, 128:] + dot(low, pair_ref[:, :128])
    rows = pl.ds(pl.multiple_of((step % 2) * PART, 8), PART)
    mine = step // 2 == core_ref[0]

    @pl.when(mine)
    def _():
        mine_ref[rows, :] = flow

    @pl.when(jnp.logical_not(mine))
    def _():
        other_ref[rows, :] = flow


def first_flows(core, ptdf, unit_rows, load):
    buses = ptdf.shape[1]
    half = jax.ShapeDtypeStruct((HALF, 128), F32)
    whole = pl.BlockSpec((HALF, 128), lambda i: (0, 0))
    return pl.pallas_call(
        first_kernel,
        grid=(2 * HALF // PART,),
        in_specs=[
            SMEM,
            pl.BlockSpec((PART, buses), lambda i: (i, 0)),
            pl.BlockSpec(unit_rows.shape, lambda i: (0, 0, 0)),
            pl.BlockSpec((buses, 128), lambda i: (0, 0)),
        ],
        out_specs=[whole, whole],
        out_shape=[half, half],
        scratch_shapes=[pltpu.VMEM((buses, 256), BF16)],
        compiler_params=params(48),
        cost_estimate=cost_of(3 * 2 * ROWS * buses * 128, 4 * ROWS * buses),
        name="first_flows",
    )(core, ptdf, unit_rows, load)


def columns_kernel(ptdf_ref, unit_ref, high_ref, low_ref, pick_ref):
    step = pl.program_id(0)
    peers = unit_ref.shape[0]
    span = ptdf_ref.shape[1] // 2
    units = high_ref.shape[1] // 2
    local = units * 2 // peers

    @pl.when(step == 0)
    def _():
        for peer in range(peers):
            group, place = divmod(peer, peers // 2)
            spots = column(unit_ref[peer][0:1, :local]).astype(jnp.int32)
            index = lax.broadcasted_iota(jnp.int32, (local, span), 1) + group * span
            pick = jnp.where(index == spots, 1.0, 0.0).astype(BF16)
            pick_ref[group, place * local : (place + 1) * local, :] = pick

    rows = row_index((BLOCK, units), step * BLOCK)
    inside = row_index((BLOCK, span), step * BLOCK) < LINES_DEV
    for group in range(2):
        ptdf = jnp.where(inside, ptdf_ref[:, group * span : (group + 1) * span], 0.0)
        high, low = halves(ptdf)
        pick = pick_ref[group]
        high = dot(high, pick, ((1,), (1,)))
        low = dot(low, pick, ((1,), (1,)))
        where = slice(group * units, (group + 1) * units)
        high_ref[:, where] = jnp.where(rows == LINES_DEV, 1.0, high).astype(BF16)
        low_ref[:, where] = low.astype(BF16)


def unit_columns(ptdf, unit_rows, units):
    buses = ptdf.shape[1]
    by_row = pl.BlockSpec((BLOCK, units), lambda i: (i, 0))
    return pl.pallas_call(
        columns_kernel,
        grid=(ROWS // BLOCK,),
        in_specs=[
            pl.BlockSpec((BLOCK, buses), lambda i: (i, 0)),
            pl.BlockSpec(unit_rows.shape, lambda i: (0, 0, 0)),
        ],
        out_specs=[by_row, by_row],
        out_shape=[jax.ShapeDtypeStruct((ROWS, units), BF16)] * 2,
        scratch_shapes=[pltpu.VMEM((2, units // 2, buses // 2), BF16)],
        compiler_params=params(48),
        cost_estimate=cost_of(2 * 2 * ROWS * buses * units // 2, 4 * ROWS * buses),
        name="unit_columns",
    )(ptdf, unit_rows)


def flow_kernel(core_ref, high_ref, low_ref, extrap_ref, mine_ref, other_ref):
    core = core_ref[0]
    high, low = halves(extrap_ref[...])
    pair = jnp.concatenate([high, low], axis=1)
    for ref, place in ((other_ref, 1 - core), (mine_ref, core)):
        rows = pl.ds(pl.multiple_of(place * HALF, 16), HALF)
        both = dot(high_ref[rows, :], pair)
        ref[...] = both[:, :128] + both[:, 128:] + dot(low_ref[rows, :], high)


def unit_flows(core, high, low, extrap):
    half = jax.ShapeDtypeStruct((HALF, 128), F32)
    return pl.pallas_call(
        flow_kernel,
        in_specs=[SMEM] + [VMEM] * 3,
        out_specs=[VMEM, VMEM],
        out_shape=[half, half],
        compiler_params=params(8),
        cost_estimate=cost_of(3 * 2 * ROWS * 512 * 128, 4 * ROWS * 512),
        name="unit_flows",
    )(core, high, low, extrap)


def dual_kernel(left_ref, right_ref, flow_ref, dual_ref, step_ref, limit_ref, dual_out, *flow_out):
    flow = flow_ref[...] + (left_ref[...] + right_ref[...])
    for ref in flow_out:
        ref[...] = flow
    moved = dual_ref[...] + step_ref[...] * flow
    limit = limit_ref[...]
    dual_out[...] = moved - jnp.clip(moved, -limit, limit)


def dual_step(left, right, flow, dual, steps, limits, outputs):
    half = jax.ShapeDtypeStruct((HALF, 128), F32)
    return pl.pallas_call(
        dual_kernel,
        in_specs=[VMEM] * 6,
        out_specs=[VMEM] * outputs,
        out_shape=[half] * outputs,
        compiler_params=params(8),
        name="dual_step",
    )(left, right, flow, dual, steps, limits)


def price_kernel(core_ref, mine_ref, other_ref, high_ref, low_ref, price_ref, dual_ref):
    core = core_ref[0]
    for ref, place in ((mine_ref, core), (other_ref, 1 - core)):
        dual_ref[pl.ds(pl.multiple_of(place * HALF, 8), HALF), :] = ref[...]
    dual_ref[2 * HALF :, :] = jnp.zeros((ROWS - 2 * HALF, 128), F32)
    high, low = halves(dual_ref[...].T)
    both = dot(jnp.concatenate([high, low], axis=0), high_ref[...])
    price = both[:128] + both[128:] + dot(high, low_ref[...])
    price_ref[...] = price.T


def unit_prices(core, mine, other, high, low):
    units = high.shape[1]
    return pl.pallas_call(
        price_kernel,
        in_specs=[SMEM] + [VMEM] * 4,
        out_specs=VMEM,
        out_shape=jax.ShapeDtypeStruct((units, 128), F32),
        scratch_shapes=[pltpu.VMEM((ROWS, 128), F32)],
        compiler_params=params(8),
        cost_estimate=cost_of(3 * 2 * ROWS * 512 * 128, 4 * ROWS * 512),
        name="unit_prices",
    )(core, mine, other, high, low)


def joined_kernel(core_ref, mine_ref, other_ref, dual_ref):
    first = core_ref[0] == 0
    mine, other = mine_ref[...], other_ref[...]
    dual_ref[:HALF, :] = jnp.where(first, mine, other)
    rest = LINES_DEV - HALF
    dual_ref[HALF:, :] = jnp.where(first, other[:rest], mine[:rest])


def joined(core, mine, other):
    return pl.pallas_call(
        joined_kernel,
        in_specs=[SMEM, VMEM, VMEM],
        out_specs=VMEM,
        out_shape=jax.ShapeDtypeStruct((LINES_DEV, 128), F32),
        compiler_params=params(8),
        name="joined",
    )(core, mine, other)


def unit_kernel(price_ref, gen_ref, old_ref, state_ref, table_ref, gen_out, extrap_ref, copies_ref):
    cost = table_ref[:, 0:1]
    lower = table_ref[:, 1:2]
    upper = table_ref[:, 2:3]
    gen = gen_ref[...]
    gradient = cost + jnp.sum(price_ref[...], axis=0) + state_ref[...]
    updated = jnp.clip(gen - PRIMAL_STEP * gradient, lower, upper)
    extrap = 2.0 * updated - gen
    gen_out[...] = updated
    extrap_ref[...] = extrap
    copies_ref[...] = jnp.broadcast_to((extrap - old_ref[...])[None], copies_ref.shape)


def unit_step(prices, gen, old, state, table):
    one = jax.ShapeDtypeStruct(gen.shape, F32)
    return pl.pallas_call(
        unit_kernel,
        in_specs=[VMEM] * 5,
        out_specs=[VMEM] * 3,
        out_shape=[one, one, jax.ShapeDtypeStruct(prices.shape, F32)],
        compiler_params=params(8),
        name="unit_step",
    )(prices, gen, old, state, table)


def state_kernel(place_ref, own_ref, far_ref, ramp_ref, store_ref, table_ref, ramp_out, store_out, state_ref):
    ramp_limit = DUAL_STEP * table_ref[:, 3:4]
    storage = table_ref[:, 4:5]
    store_limit = DUAL_STEP * table_ref[:, 5:6]
    first = place_ref[0] == 0
    own, far = own_ref[...], far_ref[...]
    extrap = jnp.concatenate([jnp.where(first, own, far), jnp.where(first, far, own)], axis=1)
    hour = lax.broadcasted_iota(jnp.int32, extrap.shape, 1)
    hours = extrap.shape[1]
    previous = pltpu.roll(extrap, 1, 1)
    moved = ramp_ref[...] + jnp.where(hour >= 1, DUAL_STEP * (extrap - previous), 0.0)
    ramp = moved - jnp.clip(moved, -ramp_limit, ramp_limit)
    ramp_out[...] = ramp
    early = lax.broadcasted_iota(jnp.int32, (hours, hours), 0)
    late = lax.broadcasted_iota(jnp.int32, (hours, hours), 1)
    forward = jnp.where(early <= late, 1.0, 0.0)
    backward = jnp.where(early >= late, 1.0, 0.0)
    running = jnp.dot(extrap, forward, precision=lax.Precision.HIGHEST, preferred_element_type=F32)
    moved = store_ref[...] + DUAL_STEP * storage * running
    store = moved - jnp.clip(moved, -store_limit, store_limit)
    store_out[...] = store
    suffix = jnp.dot(store, backward, precision=lax.Precision.HIGHEST, preferred_element_type=F32)
    after = jnp.where(hour < hours - 1, pltpu.roll(ramp, hours - 1, 1), 0.0)
    state = ramp - after + storage * suffix
    state_ref[...] = jnp.where(first, state[:, :128], state[:, 128:])


def state_step(place, own, far, ramp, store, table):
    wide = jax.ShapeDtypeStruct(ramp.shape, F32)
    return pl.pallas_call(
        state_kernel,
        in_specs=[SMEM] + [VMEM] * 5,
        out_specs=[VMEM] * 3,
        out_shape=[wide, wide, jax.ShapeDtypeStruct(own.shape, F32)],
        compiler_params=params(8),
        cost_estimate=cost_of(12 * 2 * 32 * 256 * 256, 1 << 18),
        name="state_step",
    )(place, own, far, ramp, store, table)


SWAP = ((0, 1), (1, 0))
NEAR = ((0, 1), (1, 0), (2, 3), (3, 2))
FAR = ((1, 2), (2, 1), (3, 0), (0, 3))


def along_y(value, by_core):
    pairs = [(2 * i + core, 2 * j + core) for core in range(2) for i, j in by_core[core]]
    return lax.ppermute(value, BUS, pairs)


def on_device(ptdf, bus_load, unit_bus, unit_type, unit_limit, unit_cost, line_rating):
    line_count = lax.axis_size(LINE)
    hour_dev = bus_load.shape[1]
    local = unit_bus.shape[0]
    core = lax.axis_index("c").astype(jnp.int32)
    place = lax.axis_index("t").astype(jnp.int32)[None]
    block = (lax.axis_index(BUS) * ptdf.shape[1]).astype(jnp.int32)
    table, gen, copies, load = unit_tables(
        block[None], unit_bus, unit_type, unit_limit, unit_cost, bus_load, line_count
    )
    unit_rows = lax.all_to_all(copies, LINE, 0, 0, tiled=True)
    mine, other = first_flows(core[None], ptdf, unit_rows, load)
    extrap = far = 2.0 * gen

    pad = jnp.zeros((2 * HALF - LINES_DEV,), F32)
    limits = jnp.concatenate([DUAL_STEP * (line_rating.astype(F32) / 100.0), pad])
    index = core * HALF + jnp.arange(HALF, dtype=jnp.int32)
    weight = 1.0 / (UNITS * 16)
    steps = jnp.where(index < LINES_DEV, DUAL_STEP, jnp.where(index == LINES_DEV, weight, 0.0))
    steps = steps.astype(F32)[:, None]
    limits = lax.dynamic_slice_in_dim(limits, core * HALF, HALF, 0)[:, None]
    core = core[None]
    flow = dual = jnp.zeros((HALF, hour_dev), F32)
    ramp = store = jnp.zeros((local, 2 * hour_dev), F32)
    high = low = None
    for iteration in range(ITERS):
        last = iteration == ITERS - 1
        total = mine + lax.ppermute(other, "c", SWAP)
        if iteration == 0:
            total, tied, rows = lax.optimization_barrier((total, ptdf, unit_rows))
            high, low = unit_columns(tied, rows, line_count * local)
        elif not last:
            total, tied = lax.optimization_barrier((total, extrap))
            far = lax.ppermute(tied, "t", SWAP)
        total = total + along_y(total, (NEAR, FAR))
        if not last:
            ramp, store, state = state_step(place, extrap, far, ramp, store, table)
        right = along_y(total, (FAR, NEAR))
        if iteration == 0:
            right, high, low = lax.optimization_barrier((right, high, low))
        if last:
            (dual,) = dual_step(total, right, flow, dual, steps, limits, 1)
            return gen, joined(core, dual, lax.ppermute(dual, "c", SWAP))
        right, state, ramp, store = lax.optimization_barrier((right, state, ramp, store))
        dual, flow = dual_step(total, right, flow, dual, steps, limits, 2)
        prices = unit_prices(core, dual, lax.ppermute(dual, "c", SWAP), high, low)
        prices = prices.reshape(line_count, local, hour_dev)
        prices = lax.all_to_all(prices, LINE, 0, 0, tiled=True)
        gen, extrap, copies = unit_step(prices, gen, extrap, state, table)
        changes = lax.all_to_all(copies, LINE, 0, 0, tiled=True)
        mine, other = unit_flows(core, high, low, changes.reshape(-1, hour_dev))


def solution(mesh):
    finer = Mesh(
        mesh.devices.reshape(8, 2, 4, 2, mesh.shape["tm"]),
        ("z", "xl", "y", "c", "t"),
    )
    return jax.shard_map(
        on_device,
        mesh=finer,
        in_specs=(
            P(LINE, BUS),
            P(BUS, "t"),
            P(LINE_BUS),
            P(LINE_BUS),
            P(LINE_BUS),
            P(LINE_BUS),
            P(LINE),
        ),
        out_specs=(P(LINE_BUS, "t"), P(LINE, "t")),
        check_vma=False,
    )
```

time: 209 us -> 195 us (0.933)
  waiting for transfers between devices: 45.5 us -> 35.8 us
  blocking collectives: 90.2 us -> 99.5 us
  starting transfers between devices: 46 us -> 36.8 us
  local copies, waits for them, and re-layouts: 3.99 us -> 0.24 us
    all_to_all x1 -> x0, starting transfers between devices: 10 us -> none  [on_device(): unit_rows = lax.all_to_all(copies, LINE, 0, 0, tiled=True)]
    all_to_all x6 -> x7, blocking collectives: 90.2 us -> 99.5 us  [the longest x3 41.8 us: on_device(): prices = lax.all_to_all(prices, LINE, 0, 0, tiled=True)]
    ppermute x8, waiting for transfers between devices: 32.2 us -> 23.3 us  [along_y(): return lax.ppermute(value, BUS, pairs)]
    all_to_all x1 -> x0, waiting for transfers between devices: 4.71 us -> none  [on_device(): unit_rows = lax.all_to_all(copies, LINE, 0, 0, tiled=True)]
    ppermute x9 -> x10, starting transfers between devices: 24 us -> 28.2 us  [the longest x4 11.6 us: on_device(): total = mine + lax.ppermute(other, 'c', SWAP)]
    ppermute x9 -> x10, waiting for transfers between devices: 8.59 us -> 12.5 us  [the longest x4 4.6 us: on_device(): total = mine + lax.ppermute(other, 'c', SWAP)]
    unnamed x12 -> x2, local copies, waits for them, and re-layouts: 3.75 us -> 0.01 us
    ppermute x8, starting transfers between devices: 12 us -> 8.58 us  [along_y(): return lax.ppermute(value, BUS, pairs)]
  transfers between devices with their start and end apart: 18 -> 18, of which waited for: 17 -> 18; matrix products, arithmetic and copies ran while one was open for 0% -> 0% of each run, Pallas kernels for 4% -> 4%
where the time goes in v2:
time: 195 us; the launch traced here: 194 us
  blocking collectives  99.5 us (51%)
  starting transfers between devices  36.8 us (19%)
  waiting for transfers between devices  35.8 us (18%)
  Pallas kernels  20.7 us (11%)
    all_to_all x3, blocking collectives, on_device(): prices = lax.all_to_all(prices, LINE, 0, 0, tiled=True)  41.8 us
    all_to_all x3, blocking collectives, on_device(): changes = lax.all_to_all(copies, LINE, 0, 0, tiled=True)  40 us
    ppermute x8, waiting for transfers between devices, along_y(): return lax.ppermute(value, BUS, pairs)  23.3 us
    all_to_all x1, blocking collectives, on_device(): unit_rows = lax.all_to_all(copies, LINE, 0, 0, tiled=True)  17.7 us
    ppermute x4, starting transfers between devices, on_device(): total = mine + lax.ppermute(other, 'c', SWAP)  11.6 us
    ppermute x3, starting transfers between devices, on_device(): prices = unit_prices(core, dual, lax.ppermute(dual, 'c', SWAP), high, low)  9.13 us
    ppermute x8, starting transfers between devices, along_y(): return lax.ppermute(value, BUS, pairs)  8.58 us
    ppermute x2, starting transfers between devices, on_device(): far = lax.ppermute(tied, 't', SWAP)  5.06 us
  transfers between devices with their start and end apart: 18, of which 18 were waited for; matrix products, arithmetic and copies ran while one was open for 0% of the time, Pallas kernels for 4%

profile of v2, /device:TPU:1, one launch (start us, length us, event | category | flops | bytes accessed | tf_op | source)
XLA Modules:
  0.0 194.2 jit_solution(12927793756339926064)
XLA Ops:
  1.9 17.7 %all_to_all.35.unit_ref = f32[16,8,128]{2,1,0:T(8,128)S(1)} all-to-all(f32[16,8,128]{2,1,0:T(8,128)S(1)} %get-tuple-element.57), channel_id=1, replica_groups=mesh['z'=8,'xl'=2,'y'=4,'c'=2,'t'=2] {'z','xl'}, dimensions={0} | all-to-all | bytes 131072 | tf_op jit(solution)/shard_map/all_to_all | solution.py:407
  19.6 4.9 %first_flows.1 = (f32[496,128]{1,0:T(8,128)S(1)}, f32[496,128]{1,0:T(8,128)S(1)}) custom-call(s32[1]{0:T(128)} %bitcast.core_ref, f32[960,1536]{1,0:T(8,128)} %ptdf_ref.2, f32[16,8,128]{2,1,0:T(8,128)S(1)} %all_to_all.35.unit_ref, f32[1536,128]{1,0:T(8,128)S(1)} %get-tuple-element.58.load_ref), custom_call_target="tpu_custom_call" | custom-call | flops 1207959552 | bytes 6291456 | tf_op jit(solution)/shard_map/first_flows/pallas_call | solution.py:168
  27.9 2.8 %collective-permute-start.1 = (f32[496,128]{1,0:T(8,128)S(1)}, f32[496,128]{1,0:T(8,128)S(1)}, u32[]{:S(2)}, u32[]{:S(2)}) collective-permute-start(f32[496,128]{1,0:T(8,128)S(1)} %add.46), channel_id=1, source_target_pairs={{0,4},{4,0},{8,12},{12,8},{6,10},{10,6},{14,2},{2,14},{1,5},{5,1},... | collective-permute-start | bytes 761864 | tf_op jit(solution)/shard_map/ppermute | solution.py:394
  31.6 2.8 %collective-permute-done.1 = f32[496,128]{1,0:T(8,128)S(1)} collective-permute-done((f32[496,128]{1,0:T(8,128)S(1)}, f32[496,128]{1,0:T(8,128)S(1)}, u32[]{:S(2)}, u32[]{:S(2)}) %collective-permute-start.1) | collective-permute-done | bytes 253984 | tf_op jit(solution)/shard_map/ppermute | solution.py:394
  34.9 5.0 %unit_columns.1 = (bf16[1024,512]{1,0:T(8,128)(2,1)S(1)}, bf16[1024,512]{1,0:T(8,128)(2,1)S(1)}) custom-call(f32[960,1536]{1,0:T(8,128)} %ptdf_ref.2, f32[16,8,128]{2,1,0:T(8,128)S(1)} %all_to_all.35.unit_ref), custom_call_target="tpu_custom_call" | custom-call | flops 1610612736 | bytes 6291456 | tf_op jit(solution)/shard_map/unit_columns/pallas_call | solution.py:218
  40.3 3.0 %collective-permute-start.3 = (f32[496,128]{1,0:T(8,128)S(1)}, f32[496,128]{1,0:T(8,128)S(1)}, u32[]{:S(2)}, u32[]{:S(2)}) collective-permute-start(f32[496,128]{1,0:T(8,128)S(1)} %get-tuple-element.75.mine_ref.dual_ref), channel_id=1, source_target_pairs={{0,2},{2,0},{1,3},{3,1},{4,6},{6,4},{5,7},{7,5},{8,10},{10,8},{9,1... | collective-permute-start | bytes 761864 | tf_op jit(solution)/shard_map/ppermute | solution.py:442
  45.2 13.9 %all_to_all.36.price_ref = f32[16,32,128]{2,1,0:T(8,128)S(1)} all-to-all(f32[16,32,128]{2,1,0:T(8,128)S(1)} %bitcast.13), channel_id=1, replica_groups=mesh['z'=8,'xl'=2,'y'=4,'c'=2,'t'=2] {'z','xl'}, dimensions={0} | all-to-all | bytes 524288 | tf_op jit(solution)/shard_map/all_to_all | solution.py:444
  59.2 13.3 %all_to_all.37 = f32[16,32,128]{2,1,0:T(8,128)S(1)} all-to-all(f32[16,32,128]{2,1,0:T(8,128)S(1)} %get-tuple-element.77), channel_id=1, replica_groups=mesh['z'=8,'xl'=2,'y'=4,'c'=2,'t'=2] {'z','xl'}, dimensions={0} | all-to-all | bytes 524288 | tf_op jit(solution)/shard_map/all_to_all | solution.py:446
  73.3 3.1 %collective-permute-start.4 = (f32[496,128]{1,0:T(8,128)S(1)}, f32[496,128]{1,0:T(8,128)S(1)}, u32[]{:S(2)}, u32[]{:S(2)}) collective-permute-start(f32[496,128]{1,0:T(8,128)S(1)} %get-tuple-element.79), channel_id=1, source_target_pairs={{0,2},{2,0},{1,3},{3,1},{4,6},{6,4},{5,7},{7,5},{8,10},{10,8},{9,1... | collective-permute-start | bytes 761864 | tf_op jit(solution)/shard_map/ppermute | solution.py:424
  79.7 4.2 %collective-permute-done.5 = f32[496,128]{1,0:T(8,128)S(1)} collective-permute-done((f32[496,128]{1,0:T(8,128)S(1)}, f32[496,128]{1,0:T(8,128)S(1)}, u32[]{:S(2)}, u32[]{:S(2)}) %collective-permute-start.5) | collective-permute-done | bytes 253984 | tf_op jit(solution)/shard_map/ppermute | solution.py:394
  84.1 2.5 %collective-permute-start.7 = (f32[32,128]{1,0:T(8,128)S(1)}, f32[32,128]{1,0:T(8,128)S(1)}, u32[]{:S(2)}, u32[]{:S(2)}) collective-permute-start(f32[32,128]{1,0:T(8,128)S(1)} %get-tuple-element.82.own_ref.old_ref), channel_id=1, source_target_pairs={{0,1},{1,0},{2,3},{3,2},{4,5},{5,4},{6,7},{7,6},{8,9},{9,8},{10,11... | collective-permute-start | bytes 49160 | tf_op jit(solution)/shard_map/ppermute | solution.py:430
  89.8 3.3 %collective-permute-start.8 = (f32[496,128]{1,0:T(8,128)S(1)}, f32[496,128]{1,0:T(8,128)S(1)}, u32[]{:S(2)}, u32[]{:S(2)}) collective-permute-start(f32[496,128]{1,0:T(8,128)S(1)} %get-tuple-element.90.mine_ref.dual_ref), channel_id=1, source_target_pairs={{0,2},{2,0},{1,3},{3,1},{4,6},{6,4},{5,7},{7,5},{8,10},{10,8},{9,1... | collective-permute-start | bytes 761864 | tf_op jit(solution)/shard_map/ppermute | solution.py:442
  95.0 13.9 %all_to_all.38.price_ref = f32[16,32,128]{2,1,0:T(8,128)S(1)} all-to-all(f32[16,32,128]{2,1,0:T(8,128)S(1)} %bitcast.14), channel_id=1, replica_groups=mesh['z'=8,'xl'=2,'y'=4,'c'=2,'t'=2] {'z','xl'}, dimensions={0} | all-to-all | bytes 524288 | tf_op jit(solution)/shard_map/all_to_all | solution.py:444
  109.0 13.3 %all_to_all.39 = f32[16,32,128]{2,1,0:T(8,128)S(1)} all-to-all(f32[16,32,128]{2,1,0:T(8,128)S(1)} %get-tuple-element.93), channel_id=1, replica_groups=mesh['z'=8,'xl'=2,'y'=4,'c'=2,'t'=2] {'z','xl'}, dimensions={0} | all-to-all | bytes 524288 | tf_op jit(solution)/shard_map/all_to_all | solution.py:446
  123.1 3.2 %collective-permute-start.9 = (f32[496,128]{1,0:T(8,128)S(1)}, f32[496,128]{1,0:T(8,128)S(1)}, u32[]{:S(2)}, u32[]{:S(2)}) collective-permute-start(f32[496,128]{1,0:T(8,128)S(1)} %get-tuple-element.95), channel_id=1, source_target_pairs={{0,2},{2,0},{1,3},{3,1},{4,6},{6,4},{5,7},{7,5},{8,10},{10,8},{9,1... | collective-permute-start | bytes 761864 | tf_op jit(solution)/shard_map/ppermute | solution.py:424
  128.9 5.0 %collective-permute-done.10 = f32[496,128]{1,0:T(8,128)S(1)} collective-permute-done((f32[496,128]{1,0:T(8,128)S(1)}, f32[496,128]{1,0:T(8,128)S(1)}, u32[]{:S(2)}, u32[]{:S(2)}) %collective-permute-start.10) | collective-permute-done | bytes 253984 | tf_op jit(solution)/shard_map/ppermute | solution.py:394
  134.1 2.5 %collective-permute-start.12 = (f32[32,128]{1,0:T(8,128)S(1)}, f32[32,128]{1,0:T(8,128)S(1)}, u32[]{:S(2)}, u32[]{:S(2)}) collective-permute-start(f32[32,128]{1,0:T(8,128)S(1)} %get-tuple-element.98.own_ref.old_ref), channel_id=1, source_target_pairs={{0,1},{1,0},{2,3},{3,2},{4,5},{5,4},{6,7},{7,6},{8,9},{9,8},{10,11... | collective-permute-start | bytes 49160 | tf_op jit(solution)/shard_map/ppermute | solution.py:430
  139.8 2.9 %collective-permute-start.13 = (f32[496,128]{1,0:T(8,128)S(1)}, f32[496,128]{1,0:T(8,128)S(1)}, u32[]{:S(2)}, u32[]{:S(2)}) collective-permute-start(f32[496,128]{1,0:T(8,128)S(1)} %get-tuple-element.104.mine_ref.dual_ref), channel_id=1, source_target_pairs={{0,2},{2,0},{1,3},{3,1},{4,6},{6,4},{5,7},{7,5},{8,10},{10,8},{9,1... | collective-permute-start | bytes 761864 | tf_op jit(solution)/shard_map/ppermute | solution.py:442
  144.6 13.9 %all_to_all.40.price_ref = f32[16,32,128]{2,1,0:T(8,128)S(1)} all-to-all(f32[16,32,128]{2,1,0:T(8,128)S(1)} %bitcast.15), channel_id=1, replica_groups=mesh['z'=8,'xl'=2,'y'=4,'c'=2,'t'=2] {'z','xl'}, dimensions={0} | all-to-all | bytes 524288 | tf_op jit(solution)/shard_map/all_to_all | solution.py:444
  159.2 13.3 %all_to_all.41 = f32[16,32,128]{2,1,0:T(8,128)S(1)} all-to-all(f32[16,32,128]{2,1,0:T(8,128)S(1)} %get-tuple-element.108), channel_id=1, replica_groups=mesh['z'=8,'xl'=2,'y'=4,'c'=2,'t'=2] {'z','xl'}, dimensions={0} | all-to-all | bytes 524288 | tf_op jit(solution)/shard_map/all_to_all | solution.py:446
  173.2 3.1 %collective-permute-start.14 = (f32[496,128]{1,0:T(8,128)S(1)}, f32[496,128]{1,0:T(8,128)S(1)}, u32[]{:S(2)}, u32[]{:S(2)}) collective-permute-start(f32[496,128]{1,0:T(8,128)S(1)} %get-tuple-element.110), channel_id=1, source_target_pairs={{0,2},{2,0},{1,3},{3,1},{4,6},{6,4},{5,7},{7,5},{8,10},{10,8},{9,1... | collective-permute-start | bytes 761864 | tf_op jit(solution)/shard_map/ppermute | solution.py:424
  178.9 5.0 %collective-permute-done.15 = f32[496,128]{1,0:T(8,128)S(1)} collective-permute-done((f32[496,128]{1,0:T(8,128)S(1)}, f32[496,128]{1,0:T(8,128)S(1)}, u32[]{:S(2)}, u32[]{:S(2)}) %collective-permute-start.15) | collective-permute-done | bytes 253984 | tf_op jit(solution)/shard_map/ppermute | solution.py:394
  184.0 5.4 %collective-permute-done.16.right_ref = f32[496,128]{1,0:T(8,128)S(1)} collective-permute-done((f32[496,128]{1,0:T(8,128)S(1)}, f32[496,128]{1,0:T(8,128)S(1)}, u32[]{:S(2)}, u32[]{:S(2)}) %collective-permute-start.16) | collective-permute-done | bytes 253984 | tf_op jit(solution)/shard_map/ppermute | solution.py:394
  189.8 2.5 %collective-permute-start.17 = (f32[496,128]{1,0:T(8,128)S(1)}, f32[496,128]{1,0:T(8,128)S(1)}, u32[]{:S(2)}, u32[]{:S(2)}) collective-permute-start(f32[496,128]{1,0:T(8,128)S(1)} %dual_step.7.mine_ref), channel_id=1, source_target_pairs={{0,2},{2,0},{1,3},{3,1},{4,6},{6,4},{5,7},{7,5},{8,10},{10,8},{9,1... | collective-permute-start | bytes 761864 | tf_op jit(solution)/shard_map/ppermute | solution.py:439
  (56 shorter events, 32.7 us)
Async XLA Ops:
  0.6 26.1 %copy-start = (s32[960]{0:T(1024)S(1)}, s32[960]{0:T(1024)}, u32[]{:S(2)}) copy-start(s32[960]{0:T(1024)} %param.13) | copy-start | bytes 11524
  24.5 3.3 %collective-permute-start = (f32[496,128]{1,0:T(8,128)S(1)}, f32[496,128]{1,0:T(8,128)S(1)}, u32[]{:S(2)}, u32[]{:S(2)}) collective-permute-start(f32[496,128]{1,0:T(8,128)S(1)} %get-tuple-element.60), channel_id=1, source_target_pairs={{0,2},{2,0},{1,3},{3,1},{4,6},{6,4},{5,7},{7,5},{8,10},{10,8},{9,1... | collective-permute-start | bytes 761864 | tf_op jit(solution)/shard_map/ppermute | solution.py:424
  27.9 6.5 %collective-permute-start.1 = (f32[496,128]{1,0:T(8,128)S(1)}, f32[496,128]{1,0:T(8,128)S(1)}, u32[]{:S(2)}, u32[]{:S(2)}) collective-permute-start(f32[496,128]{1,0:T(8,128)S(1)} %add.46), channel_id=1, source_target_pairs={{0,4},{4,0},{8,12},{12,8},{6,10},{10,6},{14,2},{2,14},{1,5},{5,1},... | collective-permute-start | bytes 761864 | tf_op jit(solution)/shard_map/ppermute | solution.py:394
  34.4 5.5 %collective-permute-start.2 = (f32[496,128]{1,0:T(8,128)S(1)}, f32[496,128]{1,0:T(8,128)S(1)}, u32[]{:S(2)}, u32[]{:S(2)}) collective-permute-start(f32[496,128]{1,0:T(8,128)S(1)} %add.47.left_ref), channel_id=1, source_target_pairs={{4,8},{8,4},{12,0},{0,12},{2,6},{6,2},{10,14},{14,10},{5,9},{9,5},... | collective-permute-start | bytes 761864 | tf_op jit(solution)/shard_map/ppermute | solution.py:394
  40.3 4.1 %collective-permute-start.3 = (f32[496,128]{1,0:T(8,128)S(1)}, f32[496,128]{1,0:T(8,128)S(1)}, u32[]{:S(2)}, u32[]{:S(2)}) collective-permute-start(f32[496,128]{1,0:T(8,128)S(1)} %get-tuple-element.75.mine_ref.dual_ref), channel_id=1, source_target_pairs={{0,2},{2,0},{1,3},{3,1},{4,6},{6,4},{5,7},{7,5},{8,10},{10,8},{9,1... | collective-permute-start | bytes 761864 | tf_op jit(solution)/shard_map/ppermute | solution.py:442
  73.3 4.2 %collective-permute-start.4 = (f32[496,128]{1,0:T(8,128)S(1)}, f32[496,128]{1,0:T(8,128)S(1)}, u32[]{:S(2)}, u32[]{:S(2)}) collective-permute-start(f32[496,128]{1,0:T(8,128)S(1)} %get-tuple-element.79), channel_id=1, source_target_pairs={{0,2},{2,0},{1,3},{3,1},{4,6},{6,4},{5,7},{7,5},{8,10},{10,8},{9,1... | collective-permute-start | bytes 761864 | tf_op jit(solution)/shard_map/ppermute | solution.py:424
  77.5 6.4 %collective-permute-start.5 = (f32[496,128]{1,0:T(8,128)S(1)}, f32[496,128]{1,0:T(8,128)S(1)}, u32[]{:S(2)}, u32[]{:S(2)}) collective-permute-start(f32[496,128]{1,0:T(8,128)S(1)} %add.51), channel_id=1, source_target_pairs={{0,4},{4,0},{8,12},{12,8},{6,10},{10,6},{14,2},{2,14},{1,5},{5,1},... | collective-permute-start | bytes 761864 | tf_op jit(solution)/shard_map/ppermute | solution.py:394
  84.0 5.5 %collective-permute-start.6 = (f32[496,128]{1,0:T(8,128)S(1)}, f32[496,128]{1,0:T(8,128)S(1)}, u32[]{:S(2)}, u32[]{:S(2)}) collective-permute-start(f32[496,128]{1,0:T(8,128)S(1)} %add.52.left_ref), channel_id=1, source_target_pairs={{4,8},{8,4},{12,0},{0,12},{2,6},{6,2},{10,14},{14,10},{5,9},{9,5},... | collective-permute-start | bytes 761864 | tf_op jit(solution)/shard_map/ppermute | solution.py:394
  84.1 4.2 %collective-permute-start.7 = (f32[32,128]{1,0:T(8,128)S(1)}, f32[32,128]{1,0:T(8,128)S(1)}, u32[]{:S(2)}, u32[]{:S(2)}) collective-permute-start(f32[32,128]{1,0:T(8,128)S(1)} %get-tuple-element.82.own_ref.old_ref), channel_id=1, source_target_pairs={{0,1},{1,0},{2,3},{3,2},{4,5},{5,4},{6,7},{7,6},{8,9},{9,8},{10,11... | collective-permute-start | bytes 49160 | tf_op jit(solution)/shard_map/ppermute | solution.py:430
  89.8 4.4 %collective-permute-start.8 = (f32[496,128]{1,0:T(8,128)S(1)}, f32[496,128]{1,0:T(8,128)S(1)}, u32[]{:S(2)}, u32[]{:S(2)}) collective-permute-start(f32[496,128]{1,0:T(8,128)S(1)} %get-tuple-element.90.mine_ref.dual_ref), channel_id=1, source_target_pairs={{0,2},{2,0},{1,3},{3,1},{4,6},{6,4},{5,7},{7,5},{8,10},{10,8},{9,1... | collective-permute-start | bytes 761864 | tf_op jit(solution)/shard_map/ppermute | solution.py:442
  123.1 4.4 %collective-permute-start.9 = (f32[496,128]{1,0:T(8,128)S(1)}, f32[496,128]{1,0:T(8,128)S(1)}, u32[]{:S(2)}, u32[]{:S(2)}) collective-permute-start(f32[496,128]{1,0:T(8,128)S(1)} %get-tuple-element.95), channel_id=1, source_target_pairs={{0,2},{2,0},{1,3},{3,1},{4,6},{6,4},{5,7},{7,5},{8,10},{10,8},{9,1... | collective-permute-start | bytes 761864 | tf_op jit(solution)/shard_map/ppermute | solution.py:424
  127.5 6.4 %collective-permute-start.10 = (f32[496,128]{1,0:T(8,128)S(1)}, f32[496,128]{1,0:T(8,128)S(1)}, u32[]{:S(2)}, u32[]{:S(2)}) collective-permute-start(f32[496,128]{1,0:T(8,128)S(1)} %add.53), channel_id=1, source_target_pairs={{0,4},{4,0},{8,12},{12,8},{6,10},{10,6},{14,2},{2,14},{1,5},{5,1},... | collective-permute-start | bytes 761864 | tf_op jit(solution)/shard_map/ppermute | solution.py:394
  134.0 5.5 %collective-permute-start.11 = (f32[496,128]{1,0:T(8,128)S(1)}, f32[496,128]{1,0:T(8,128)S(1)}, u32[]{:S(2)}, u32[]{:S(2)}) collective-permute-start(f32[496,128]{1,0:T(8,128)S(1)} %add.54.left_ref), channel_id=1, source_target_pairs={{4,8},{8,4},{12,0},{0,12},{2,6},{6,2},{10,14},{14,10},{5,9},{9,5},... | collective-permute-start | bytes 761864 | tf_op jit(solution)/shard_map/ppermute | solution.py:394
  134.1 4.2 %collective-permute-start.12 = (f32[32,128]{1,0:T(8,128)S(1)}, f32[32,128]{1,0:T(8,128)S(1)}, u32[]{:S(2)}, u32[]{:S(2)}) collective-permute-start(f32[32,128]{1,0:T(8,128)S(1)} %get-tuple-element.98.own_ref.old_ref), channel_id=1, source_target_pairs={{0,1},{1,0},{2,3},{3,2},{4,5},{5,4},{6,7},{7,6},{8,9},{9,8},{10,11... | collective-permute-start | bytes 49160 | tf_op jit(solution)/shard_map/ppermute | solution.py:430
  139.8 4.0 %collective-permute-start.13 = (f32[496,128]{1,0:T(8,128)S(1)}, f32[496,128]{1,0:T(8,128)S(1)}, u32[]{:S(2)}, u32[]{:S(2)}) collective-permute-start(f32[496,128]{1,0:T(8,128)S(1)} %get-tuple-element.104.mine_ref.dual_ref), channel_id=1, source_target_pairs={{0,2},{2,0},{1,3},{3,1},{4,6},{6,4},{5,7},{7,5},{8,10},{10,8},{9,1... | collective-permute-start | bytes 761864 | tf_op jit(solution)/shard_map/ppermute | solution.py:442
  173.2 4.2 %collective-permute-start.14 = (f32[496,128]{1,0:T(8,128)S(1)}, f32[496,128]{1,0:T(8,128)S(1)}, u32[]{:S(2)}, u32[]{:S(2)}) collective-permute-start(f32[496,128]{1,0:T(8,128)S(1)} %get-tuple-element.110), channel_id=1, source_target_pairs={{0,2},{2,0},{1,3},{3,1},{4,6},{6,4},{5,7},{7,5},{8,10},{10,8},{9,1... | collective-permute-start | bytes 761864 | tf_op jit(solution)/shard_map/ppermute | solution.py:424
  177.5 6.4 %collective-permute-start.15 = (f32[496,128]{1,0:T(8,128)S(1)}, f32[496,128]{1,0:T(8,128)S(1)}, u32[]{:S(2)}, u32[]{:S(2)}) collective-permute-start(f32[496,128]{1,0:T(8,128)S(1)} %add.55), channel_id=1, source_target_pairs={{0,4},{4,0},{8,12},{12,8},{6,10},{10,6},{14,2},{2,14},{1,5},{5,1},... | collective-permute-start | bytes 761864 | tf_op jit(solution)/shard_map/ppermute | solution.py:394
  183.9 5.5 %collective-permute-start.16 = (f32[496,128]{1,0:T(8,128)S(1)}, f32[496,128]{1,0:T(8,128)S(1)}, u32[]{:S(2)}, u32[]{:S(2)}) collective-permute-start(f32[496,128]{1,0:T(8,128)S(1)} %add.56.left_ref), channel_id=1, source_target_pairs={{4,8},{8,4},{12,0},{0,12},{2,6},{6,2},{10,14},{14,10},{5,9},{9,5},... | collective-permute-start | bytes 761864 | tf_op jit(solution)/shard_map/ppermute | solution.py:394
  189.8 3.6 %collective-permute-start.17 = (f32[496,128]{1,0:T(8,128)S(1)}, f32[496,128]{1,0:T(8,128)S(1)}, u32[]{:S(2)}, u32[]{:S(2)}) collective-permute-start(f32[496,128]{1,0:T(8,128)S(1)} %dual_step.7.mine_ref), channel_id=1, source_target_pairs={{0,2},{2,0},{1,3},{3,1},{4,6},{6,4},{5,7},{7,5},{8,10},{10,8},{9,1... | collective-permute-start | bytes 761864 | tf_op jit(solution)/shard_map/ppermute | solution.py:439

commit v3 on v2

--- a/solution.py
+++ b/solution.py
@@ -1,5 +1,3 @@
-import functools
-
 import jax
 import jax.numpy as jnp
 from jax import lax
@@ -24,6 +22,7 @@
 HALF = 496
 BLOCK = 256
 PART = 248
+CHUNKS = ((0, 240), (240, HALF))
 BF16 = jnp.bfloat16
 F32 = jnp.float32
 VMEM = pl.BlockSpec(memory_space=pltpu.VMEM)
@@ -231,73 +230,74 @@
     )(ptdf, unit_rows)
 
 
-def flow_kernel(core_ref, high_ref, low_ref, extrap_ref, mine_ref, other_ref):
-    core = core_ref[0]
+def flow_kernel(place_ref, high_ref, low_ref, extrap_ref, flow_ref):
     high, low = halves(extrap_ref[...])
     pair = jnp.concatenate([high, low], axis=1)
-    for ref, place in ((other_ref, 1 - core), (mine_ref, core)):
-        rows = pl.ds(pl.multiple_of(place * HALF, 16), HALF)
-        both = dot(high_ref[rows, :], pair)
-        ref[...] = both[:, :128] + both[:, 128:] + dot(low_ref[rows, :], high)
-
-
-def unit_flows(core, high, low, extrap):
-    half = jax.ShapeDtypeStruct((HALF, 128), F32)
+    rows = pl.ds(pl.multiple_of(place_ref[0] * HALF, 16), HALF)
+    both = dot(high_ref[rows, :], pair)
+    flow_ref[...] = both[:, :128] + both[:, 128:] + dot(low_ref[rows, :], high)
+
+
+def unit_flows(place, high, low, extrap):
     return pl.pallas_call(
         flow_kernel,
         in_specs=[SMEM] + [VMEM] * 3,
-        out_specs=[VMEM, VMEM],
-        out_shape=[half, half],
-        compiler_params=params(8),
-        cost_estimate=cost_of(3 * 2 * ROWS * 512 * 128, 4 * ROWS * 512),
+        out_specs=VMEM,
+        out_shape=jax.ShapeDtypeStruct((HALF, 128), F32),
+        compiler_params=params(8),
+        cost_estimate=cost_of(3 * 2 * HALF * 512 * 128, 4 * HALF * 512),
         name="unit_flows",
-    )(core, high, low, extrap)
-
-
-def dual_kernel(left_ref, right_ref, flow_ref, dual_ref, step_ref, limit_ref, dual_out, *flow_out):
-    flow = flow_ref[...] + (left_ref[...] + right_ref[...])
-    for ref in flow_out:
-        ref[...] = flow
-    moved = dual_ref[...] + step_ref[...] * flow
-    limit = limit_ref[...]
-    dual_out[...] = moved - jnp.clip(moved, -limit, limit)
-
-
-def dual_step(left, right, flow, dual, steps, limits, outputs):
+    )(place, high, low, extrap)
+
+
+def dual_kernel(*refs):
+    count = len(CHUNKS)
+    lefts, rights = refs[:count], refs[count : 2 * count]
+    flow_ref, dual_ref, step_ref, limit_ref, dual_out, *flow_out = refs[2 * count :]
+    for chunk, ends in enumerate(CHUNKS):
+        rows = slice(*ends)
+        flow = flow_ref[rows, :] + (lefts[chunk][...] + rights[chunk][...])
+        for ref in flow_out:
+            ref[rows, :] = flow
+        moved = dual_ref[rows, :] + step_ref[rows, :] * flow
+        limit = limit_ref[rows, :]
+        dual_out[rows, :] = moved - jnp.clip(moved, -limit, limit)
+
+
+def dual_step(lefts, rights, flow, dual, steps, limits, outputs):
     half = jax.ShapeDtypeStruct((HALF, 128), F32)
     return pl.pallas_call(
         dual_kernel,
-        in_specs=[VMEM] * 6,
+        in_specs=[VMEM] * (4 + 2 * len(lefts)),
         out_specs=[VMEM] * outputs,
         out_shape=[half] * outputs,
         compiler_params=params(8),
         name="dual_step",
-    )(left, right, flow, dual, steps, limits)
-
-
-def price_kernel(core_ref, mine_ref, other_ref, high_ref, low_ref, price_ref, dual_ref):
-    core = core_ref[0]
-    for ref, place in ((mine_ref, core), (other_ref, 1 - core)):
-        dual_ref[pl.ds(pl.multiple_of(place * HALF, 8), HALF), :] = ref[...]
-    dual_ref[2 * HALF :, :] = jnp.zeros((ROWS - 2 * HALF, 128), F32)
+    )(*lefts, *rights, flow, dual, steps, limits)
+
+
+def price_kernel(place_ref, dual_ref, high_ref, low_ref, *refs):
+    rows = pl.ds(pl.multiple_of(place_ref[0] * HALF, 16), HALF)
     high, low = halves(dual_ref[...].T)
-    both = dot(jnp.concatenate([high, low], axis=0), high_ref[...])
-    price = both[:128] + both[128:] + dot(high, low_ref[...])
-    price_ref[...] = price.T
-
-
-def unit_prices(core, mine, other, high, low):
+    both = dot(jnp.concatenate([high, low], axis=0), high_ref[rows, :])
+    price = both[:128] + both[128:] + dot(high, low_ref[rows, :])
+    if len(refs) == 2:
+        refs[1][...] = (refs[0][...] + price).T
+    else:
+        refs[0][...] = price
+
+
+def unit_prices(place, dual, high, low, *part):
     units = high.shape[1]
     return pl.pallas_call(
         price_kernel,
-        in_specs=[SMEM] + [VMEM] * 4,
+        in_specs=[SMEM] + [VMEM] * (3 + len(part)),
         out_specs=VMEM,
-        out_shape=jax.ShapeDtypeStruct((units, 128), F32),
-        scratch_shapes=[pltpu.VMEM((ROWS, 128), F32)],
-        compiler_params=params(8),
-        cost_estimate=cost_of(3 * 2 * ROWS * 512 * 128, 4 * ROWS * 512),
+        out_shape=jax.ShapeDtypeStruct((units, 128) if part else (128, units), F32),
+        compiler_params=params(8),
+        cost_estimate=cost_of(3 * 2 * HALF * 512 * 128, 4 * HALF * 512),
         name="unit_prices",
-    )(core, mine, other, high, low)
+    )(place, dual, high, low, *part)
 
 
 def joined_kernel(core_ref, mine_ref, other_ref, dual_ref):
@@ -415,7 +415,7 @@
     steps = jnp.where(index < LINES_DEV, DUAL_STEP, jnp.where(index == LINES_DEV, weight, 0.0))
     steps = steps.astype(F32)[:, None]
     limits = lax.dynamic_slice_in_dim(limits, core * HALF, HALF, 0)[:, None]
-    core = core[None]
+    core, partner = core[None], 1 - core[None]
     flow = dual = jnp.zeros((HALF, hour_dev), F32)
     ramp = store = jnp.zeros((local, 2 * hour_dev), F32)
     high = low = None
@@ -428,23 +428,28 @@
         elif not last:
             total, tied = lax.optimization_barrier((total, extrap))
             far = lax.ppermute(tied, "t", SWAP)
-        total = total + along_y(total, (NEAR, FAR))
+        lefts = [total[start:stop] for start, stop in CHUNKS]
+        lefts = [left + along_y(left, (NEAR, FAR)) for left in lefts]
+        if 0 < iteration < ITERS - 1:
+            lefts[0], far = lax.optimization_barrier((lefts[0], far))
         if not last:
             ramp, store, state = state_step(place, extrap, far, ramp, store, table)
-        right = along_y(total, (FAR, NEAR))
+        rights = [along_y(left, (FAR, NEAR)) for left in lefts]
         if iteration == 0:
-            right, high, low = lax.optimization_barrier((right, high, low))
+            rights[-1], high, low = lax.optimization_barrier((rights[-1], high, low))
         if last:
-            (dual,) = dual_step(total, right, flow, dual, steps, limits, 1)
+            (dual,) = dual_step(lefts, rights, flow, dual, steps, limits, 1)
             return gen, joined(core, dual, lax.ppermute(dual, "c", SWAP))
-        right, state, ramp, store = lax.optimization_barrier((right, state, ramp, store))
-        dual, flow = dual_step(total, right, flow, dual, steps, limits, 2)
-        prices = unit_prices(core, dual, lax.ppermute(dual, "c", SWAP), high, low)
+        rights[-1], state, ramp, store = lax.optimization_barrier((rights[-1], state, ramp, store))
+        dual, flow = dual_step(lefts, rights, flow, dual, steps, limits, 2)
+        prices = unit_prices(core, dual, high, low)
+        prices = unit_prices(partner, lax.ppermute(dual, "c", SWAP), high, low, prices)
         prices = prices.reshape(line_count, local, hour_dev)
         prices = lax.all_to_all(prices, LINE, 0, 0, tiled=True)
         gen, extrap, copies = unit_step(prices, gen, extrap, state, table)
-        changes = lax.all_to_all(copies, LINE, 0, 0, tiled=True)
-        mine, other = unit_flows(core, high, low, changes.reshape(-1, hour_dev))
+        changes = lax.all_to_all(copies, LINE, 0, 0, tiled=True).reshape(-1, hour_dev)
+        other = unit_flows(partner, high, low, changes)
+        mine = unit_flows(core, high, low, changes)
 
 
 def solution(mesh):

time: 195 us -> 192 us (0.985)
  blocking collectives: 99.5 us -> 81.8 us
  starting transfers between devices: 36.8 us -> 46 us
  waiting for transfers between devices: 35.8 us -> 39.3 us
    all_to_all x4 -> x3, blocking collectives: 57.7 us -> 40.1 us  [on_device(): lax.all_to_all(copies, LINE, 0, 0, tiled=True).reshape(-1, hour_dev)]
    all_to_all x0 -> x1, starting transfers between devices: none -> 10 us  [on_device(): unit_rows = lax.all_to_all(copies, LINE, 0, 0, tiled=True)]
    all_to_all x0 -> x1, waiting for transfers between devices: none -> 7.2 us  [on_device(): unit_rows = lax.all_to_all(copies, LINE, 0, 0, tiled=True)]
    ppermute x8 -> x16, starting transfers between devices: 8.58 us -> 11.9 us  [along_y(): return lax.ppermute(value, BUS, pairs)]
    ppermute x2, waiting for transfers between devices: 3.3 us -> 0.01 us  [on_device(): far = lax.ppermute(tied, 't', SWAP)]
    ppermute x3, starting transfers between devices: 9.13 us -> 6.71 us  [on_device(): lax.ppermute(dual, 'c', SWAP)]
    ppermute x8 -> x16, waiting for transfers between devices: 23.3 us -> 25.6 us  [along_y(): return lax.ppermute(value, BUS, pairs)]
    pallas_call x10 -> x16, Pallas kernels: 5.52 us -> 6.46 us  [the longest x6 2.75 us: unit_prices(): pl.pallas_call(price_kernel, in_specs=[SMEM] + [VMEM] * (3 + len(part)),...]
  transfers between devices with their start and end apart: 18 -> 27, of which waited for: 18 -> 21; matrix products, arithmetic and copies ran while one was open for 0% -> 1% of each run, Pallas kernels for 4% -> 5%
where the time goes in v3:
time: 192 us
  blocking collectives  81.8 us (43%)
  starting transfers between devices  46 us (24%)
  waiting for transfers between devices  39.3 us (20%)
  Pallas kernels  22.2 us (12%)
    all_to_all x3, blocking collectives, on_device(): prices = lax.all_to_all(prices, LINE, 0, 0, tiled=True)  41.8 us
    all_to_all x3, blocking collectives, on_device(): lax.all_to_all(copies, LINE, 0, 0, tiled=True).reshape(-1, hour_dev)  40.1 us
    ppermute x16, waiting for transfers between devices, along_y(): return lax.ppermute(value, BUS, pairs)  25.6 us
    ppermute x16, starting transfers between devices, along_y(): return lax.ppermute(value, BUS, pairs)  11.9 us
    ppermute x4, starting transfers between devices, on_device(): total = mine + lax.ppermute(other, 'c', SWAP)  11.4 us
    all_to_all x1, starting transfers between devices, on_device(): unit_rows = lax.all_to_all(copies, LINE, 0, 0, tiled=True)  10 us
    all_to_all x1, waiting for transfers between devices, on_device(): unit_rows = lax.all_to_all(copies, LINE, 0, 0, tiled=True)  7.2 us
    ppermute x3, starting transfers between devices, on_device(): lax.ppermute(dual, 'c', SWAP)  6.71 us
  transfers between devices with their start and end apart: 27, of which 21 were waited for; matrix products, arithmetic and copies ran while one was open for 1% of the time, Pallas kernels for 5%

profile of v3, /device:TPU:1, one launch (start us, length us, event | category | flops | bytes accessed | tf_op | source)
XLA Modules:
  0.0 191.7 jit_solution(9519374415954547216)
XLA Ops:
  2.5 10.0 %all-to-all-start = ((f32[16,8,128]{2,1,0:T(8,128)}), f32[16,8,128]{2,1,0:T(8,128)S(1)}, u32[]{:S(2)}, u32[]{:S(2)}) async-start(f32[16,8,128]{2,1,0:T(8,128)} %get-tuple-element.55), calls=%async_computation | async-start | bytes 131072 | tf_op jit(solution)/shard_map/all_to_all | solution.py:407
  13.3 7.2 %all-to-all-done.unit_ref = f32[16,8,128]{2,1,0:T(8,128)S(1)} async-done(((f32[16,8,128]{2,1,0:T(8,128)}), f32[16,8,128]{2,1,0:T(8,128)S(1)}, u32[]{:S(2)}, u32[]{:S(2)}) %all-to-all-start) | async-done | bytes 65568 | tf_op jit(solution)/shard_map/all_to_all | solution.py:407
  20.5 4.9 %first_flows.1 = (f32[496,128]{1,0:T(8,128)S(1)}, f32[496,128]{1,0:T(8,128)S(1)}) custom-call(s32[1]{0:T(128)} %bitcast.core_ref.place_ref, f32[960,1536]{1,0:T(8,128)} %ptdf_ref.2, f32[16,8,128]{2,1,0:T(8,128)S(1)} %all-to-all-done.unit_ref, f32[1536,128]{1,0:T(8,128)S(1)} %get-tuple-element.56.load_ref), custom_call_target="tpu_custom_call" | custom-call | flops 1207959552 | bytes 6291456 | tf_op jit(solution)/shard_map/first_flows/pallas_call | solution.py:167
  25.4 2.2 %collective-permute-start = (f32[496,128]{1,0:T(8,128)S(1)}, f32[496,128]{1,0:T(8,128)S(1)}, u32[]{:S(2)}, u32[]{:S(2)}) collective-permute-start(f32[496,128]{1,0:T(8,128)S(1)} %get-tuple-element.58), channel_id=1, source_target_pairs={{0,2},{2,0},{1,3},{3,1},{4,6},{6,4},{5,7},{7,5},{8,10},{10,8},{9,1... | collective-permute-start | bytes 761864 | tf_op jit(solution)/shard_map/ppermute | solution.py:424
  28.8 2.8 %collective-permute-start.3 = (f32[240,128]{1,0:T(8,128)S(1)}, f32[240,128]{1,0:T(8,128)S(1)}, u32[]{:S(2)}, u32[]{:S(2)}) collective-permute-start(f32[240,128]{1,0:T(8,128)S(1)} %slice.25), channel_id=1, source_target_pairs={{0,4},{4,0},{8,12},{12,8},{6,10},{10,6},{14,2},{2,14},{1,5},{5,1},... | collective-permute-start | bytes 368648 | tf_op jit(solution)/shard_map/ppermute | solution.py:394
  34.3 3.1 %collective-permute-done.1 = f32[256,128]{1,0:T(8,128)S(1)} collective-permute-done((f32[256,128]{1,0:T(8,128)S(1)}, f32[256,128]{1,0:T(8,128)S(1)}, u32[]{:S(2)}, u32[]{:S(2)}) %collective-permute-start.1) | collective-permute-done | bytes 131104 | tf_op jit(solution)/shard_map/ppermute | solution.py:394
  37.5 5.0 %unit_columns.1 = (bf16[1024,512]{1,0:T(8,128)(2,1)S(1)}, bf16[1024,512]{1,0:T(8,128)(2,1)S(1)}) custom-call(f32[960,1536]{1,0:T(8,128)} %ptdf_ref.2, f32[16,8,128]{2,1,0:T(8,128)S(1)} %all-to-all-done.unit_ref), custom_call_target="tpu_custom_call" | custom-call | flops 1610612736 | bytes 6291456 | tf_op jit(solution)/shard_map/unit_columns/pallas_call | solution.py:217
  45.9 13.9 %all_to_all.35.price_ref = f32[16,32,128]{2,1,0:T(8,128)S(1)} all-to-all(f32[16,32,128]{2,1,0:T(8,128)S(1)} %bitcast.16), channel_id=1, replica_groups=mesh['z'=8,'xl'=2,'y'=4,'c'=2,'t'=2] {'z','xl'}, dimensions={0} | all-to-all | bytes 524288 | tf_op jit(solution)/shard_map/all_to_all | solution.py:448
  60.0 13.4 %all_to_all.36 = f32[16,32,128]{2,1,0:T(8,128)S(1)} all-to-all(f32[16,32,128]{2,1,0:T(8,128)S(1)} %get-tuple-element.75), channel_id=1, replica_groups=mesh['z'=8,'xl'=2,'y'=4,'c'=2,'t'=2] {'z','xl'}, dimensions={0} | all-to-all | bytes 524288 | tf_op jit(solution)/shard_map/all_to_all | solution.py:450
  73.8 3.1 %collective-permute-start.6 = (f32[496,128]{1,0:T(8,128)S(1)}, f32[496,128]{1,0:T(8,128)S(1)}, u32[]{:S(2)}, u32[]{:S(2)}) collective-permute-start(f32[496,128]{1,0:T(8,128)S(1)} %unit_flows.7), channel_id=1, source_target_pairs={{0,2},{2,0},{1,3},{3,1},{4,6},{6,4},{5,7},{7,5},{8,10},{10,8},{9,1... | collective-permute-start | bytes 761864 | tf_op jit(solution)/shard_map/ppermute | solution.py:424
  79.6 2.5 %collective-permute-start.8 = (f32[32,128]{1,0:T(8,128)S(1)}, f32[32,128]{1,0:T(8,128)S(1)}, u32[]{:S(2)}, u32[]{:S(2)}) collective-permute-start(f32[32,128]{1,0:T(8,128)S(1)} %get-tuple-element.78.own_ref.old_ref), channel_id=1, source_target_pairs={{0,1},{1,0},{2,3},{3,2},{4,5},{5,4},{6,7},{7,6},{8,9},{9,8},{10,11... | collective-permute-start | bytes 49160 | tf_op jit(solution)/shard_map/ppermute | solution.py:430
  83.5 3.6 %collective-permute-done.7 = f32[240,128]{1,0:T(8,128)S(1)} collective-permute-done((f32[240,128]{1,0:T(8,128)S(1)}, f32[240,128]{1,0:T(8,128)S(1)}, u32[]{:S(2)}, u32[]{:S(2)}) %collective-permute-start.7) | collective-permute-done | bytes 122912 | tf_op jit(solution)/shard_map/ppermute | solution.py:394
  88.0 2.9 %collective-permute-done.10.refs_2_ = f32[240,128]{1,0:T(8,128)S(1)} collective-permute-done((f32[240,128]{1,0:T(8,128)S(1)}, f32[240,128]{1,0:T(8,128)S(1)}, u32[]{:S(2)}, u32[]{:S(2)}) %collective-permute-start.10) | collective-permute-done | bytes 122912 | tf_op jit(solution)/shard_map/ppermute | solution.py:394
  91.1 3.0 %collective-permute-start.12 = (f32[496,128]{1,0:T(8,128)S(1)}, f32[496,128]{1,0:T(8,128)S(1)}, u32[]{:S(2)}, u32[]{:S(2)}) collective-permute-start(f32[496,128]{1,0:T(8,128)S(1)} %get-tuple-element.88.dual_ref.refs_5_), channel_id=1, source_target_pairs={{0,2},{2,0},{1,3},{3,1},{4,6},{6,4},{5,7},{7,5},{8,10},{10,8},{9,1... | collective-permute-start | bytes 761864 | tf_op jit(solution)/shard_map/ppermute | solution.py:446
  95.8 13.9 %all_to_all.37.price_ref = f32[16,32,128]{2,1,0:T(8,128)S(1)} all-to-all(f32[16,32,128]{2,1,0:T(8,128)S(1)} %bitcast.17), channel_id=1, replica_groups=mesh['z'=8,'xl'=2,'y'=4,'c'=2,'t'=2] {'z','xl'}, dimensions={0} | all-to-all | bytes 524288 | tf_op jit(solution)/shard_map/all_to_all | solution.py:448
  109.9 13.4 %all_to_all.38 = f32[16,32,128]{2,1,0:T(8,128)S(1)} all-to-all(f32[16,32,128]{2,1,0:T(8,128)S(1)} %get-tuple-element.91), channel_id=1, replica_groups=mesh['z'=8,'xl'=2,'y'=4,'c'=2,'t'=2] {'z','xl'}, dimensions={0} | all-to-all | bytes 524288 | tf_op jit(solution)/shard_map/all_to_all | solution.py:450
  123.7 3.1 %collective-permute-start.13 = (f32[496,128]{1,0:T(8,128)S(1)}, f32[496,128]{1,0:T(8,128)S(1)}, u32[]{:S(2)}, u32[]{:S(2)}) collective-permute-start(f32[496,128]{1,0:T(8,128)S(1)} %unit_flows.9), channel_id=1, source_target_pairs={{0,2},{2,0},{1,3},{3,1},{4,6},{6,4},{5,7},{7,5},{8,10},{10,8},{9,1... | collective-permute-start | bytes 761864 | tf_op jit(solution)/shard_map/ppermute | solution.py:424
  139.0 2.3 %collective-permute-start.19 = (f32[496,128]{1,0:T(8,128)S(1)}, f32[496,128]{1,0:T(8,128)S(1)}, u32[]{:S(2)}, u32[]{:S(2)}) collective-permute-start(f32[496,128]{1,0:T(8,128)S(1)} %get-tuple-element.102.dual_ref.refs_5_), channel_id=1, source_target_pairs={{0,2},{2,0},{1,3},{3,1},{4,6},{6,4},{5,7},{7,5},{8,10},{10,8},{9,1... | collective-permute-start | bytes 761864 | tf_op jit(solution)/shard_map/ppermute | solution.py:446
  143.0 13.9 %all_to_all.39.price_ref = f32[16,32,128]{2,1,0:T(8,128)S(1)} all-to-all(f32[16,32,128]{2,1,0:T(8,128)S(1)} %bitcast.18), channel_id=1, replica_groups=mesh['z'=8,'xl'=2,'y'=4,'c'=2,'t'=2] {'z','xl'}, dimensions={0} | all-to-all | bytes 524288 | tf_op jit(solution)/shard_map/all_to_all | solution.py:448
  157.7 13.4 %all_to_all.40 = f32[16,32,128]{2,1,0:T(8,128)S(1)} all-to-all(f32[16,32,128]{2,1,0:T(8,128)S(1)} %get-tuple-element.106), channel_id=1, replica_groups=mesh['z'=8,'xl'=2,'y'=4,'c'=2,'t'=2] {'z','xl'}, dimensions={0} | all-to-all | bytes 524288 | tf_op jit(solution)/shard_map/all_to_all | solution.py:450
  171.5 3.1 %collective-permute-start.20 = (f32[496,128]{1,0:T(8,128)S(1)}, f32[496,128]{1,0:T(8,128)S(1)}, u32[]{:S(2)}, u32[]{:S(2)}) collective-permute-start(f32[496,128]{1,0:T(8,128)S(1)} %unit_flows.11), channel_id=1, source_target_pairs={{0,2},{2,0},{1,3},{3,1},{4,6},{6,4},{5,7},{7,5},{8,10},{10,8},{9,1... | collective-permute-start | bytes 761864 | tf_op jit(solution)/shard_map/ppermute | solution.py:424
  178.6 2.3 %collective-permute-done.22 = f32[256,128]{1,0:T(8,128)S(1)} collective-permute-done((f32[256,128]{1,0:T(8,128)S(1)}, f32[256,128]{1,0:T(8,128)S(1)}, u32[]{:S(2)}, u32[]{:S(2)}) %collective-permute-start.22) | collective-permute-done | bytes 131104 | tf_op jit(solution)/shard_map/ppermute | solution.py:394
  182.6 4.0 %collective-permute-done.23.refs_2_ = f32[240,128]{1,0:T(8,128)S(1)} collective-permute-done((f32[240,128]{1,0:T(8,128)S(1)}, f32[240,128]{1,0:T(8,128)S(1)}, u32[]{:S(2)}, u32[]{:S(2)}) %collective-permute-start.23) | collective-permute-done | bytes 122912 | tf_op jit(solution)/shard_map/ppermute | solution.py:394
  186.9 2.8 %collective-permute-start.25 = (f32[496,128]{1,0:T(8,128)S(1)}, f32[496,128]{1,0:T(8,128)S(1)}, u32[]{:S(2)}, u32[]{:S(2)}) collective-permute-start(f32[496,128]{1,0:T(8,128)S(1)} %dual_step.7.mine_ref), channel_id=1, source_target_pairs={{0,2},{2,0},{1,3},{3,1},{4,6},{6,4},{5,7},{7,5},{8,10},{10,8},{9,1... | collective-permute-start | bytes 761864 | tf_op jit(solution)/shard_map/ppermute | solution.py:442
  (89 shorter events, 41.0 us)
Async XLA Ops:
  2.5 18.0 %all-to-all-start = ((f32[16,8,128]{2,1,0:T(8,128)}), f32[16,8,128]{2,1,0:T(8,128)S(1)}, u32[]{:S(2)}, u32[]{:S(2)}) async-start(f32[16,8,128]{2,1,0:T(8,128)} %get-tuple-element.55), calls=%async_computation | async-start | bytes 131072 | tf_op jit(solution)/shard_map/all_to_all | solution.py:407
  28.8 5.1 %collective-permute-start.3 = (f32[240,128]{1,0:T(8,128)S(1)}, f32[240,128]{1,0:T(8,128)S(1)}, u32[]{:S(2)}, u32[]{:S(2)}) collective-permute-start(f32[240,128]{1,0:T(8,128)S(1)} %slice.25), channel_id=1, source_target_pairs={{0,4},{4,0},{8,12},{12,8},{6,10},{10,6},{14,2},{2,14},{1,5},{5,1},... | collective-permute-start | bytes 368648 | tf_op jit(solution)/shard_map/ppermute | solution.py:394
  32.3 5.1 %collective-permute-start.1 = (f32[256,128]{1,0:T(8,128)S(1)}, f32[256,128]{1,0:T(8,128)S(1)}, u32[]{:S(2)}, u32[]{:S(2)}) collective-permute-start(f32[256,128]{1,0:T(8,128)S(1)} %slice.24), channel_id=1, source_target_pairs={{0,4},{4,0},{8,12},{12,8},{6,10},{10,6},{14,2},{2,14},{1,5},{5,1},... | collective-permute-start | bytes 393224 | tf_op jit(solution)/shard_map/ppermute | solution.py:394
  33.9 8.7 %collective-permute-start.4 = (f32[240,128]{1,0:T(8,128)S(1)}, f32[240,128]{1,0:T(8,128)S(1)}, u32[]{:S(2)}, u32[]{:S(2)}) collective-permute-start(f32[240,128]{1,0:T(8,128)S(1)} %slice_add_fusion.3.refs_0_), channel_id=1, source_target_pairs={{4,8},{8,4},{12,0},{0,12},{2,6},{6,2},{10,14},{14,10},{5,9},{9,5},... | collective-permute-start | bytes 368648 | tf_op jit(solution)/shard_map/ppermute | solution.py:394
  37.5 5.1 %collective-permute-start.2 = (f32[256,128]{1,0:T(8,128)S(1)}, f32[256,128]{1,0:T(8,128)S(1)}, u32[]{:S(2)}, u32[]{:S(2)}) collective-permute-start(f32[256,128]{1,0:T(8,128)S(1)} %slice_add_fusion.7.refs_1_), channel_id=1, source_target_pairs={{4,8},{8,4},{12,0},{0,12},{2,6},{6,2},{10,14},{14,10},{5,9},{9,5},... | collective-permute-start | bytes 393224 | tf_op jit(solution)/shard_map/ppermute | solution.py:394
  73.8 4.2 %collective-permute-start.6 = (f32[496,128]{1,0:T(8,128)S(1)}, f32[496,128]{1,0:T(8,128)S(1)}, u32[]{:S(2)}, u32[]{:S(2)}) collective-permute-start(f32[496,128]{1,0:T(8,128)S(1)} %unit_flows.7), channel_id=1, source_target_pairs={{0,2},{2,0},{1,3},{3,1},{4,6},{6,4},{5,7},{7,5},{8,10},{10,8},{9,1... | collective-permute-start | bytes 761864 | tf_op jit(solution)/shard_map/ppermute | solution.py:424
  78.0 5.3 %collective-permute-start.9 = (f32[256,128]{1,0:T(8,128)S(1)}, f32[256,128]{1,0:T(8,128)S(1)}, u32[]{:S(2)}, u32[]{:S(2)}) collective-permute-start(f32[256,128]{1,0:T(8,128)S(1)} %slice.27), channel_id=1, source_target_pairs={{0,4},{4,0},{8,12},{12,8},{6,10},{10,6},{14,2},{2,14},{1,5},{5,1},... | collective-permute-start | bytes 393224 | tf_op jit(solution)/shard_map/ppermute | solution.py:394
  79.6 7.5 %collective-permute-start.8 = (f32[32,128]{1,0:T(8,128)S(1)}, f32[32,128]{1,0:T(8,128)S(1)}, u32[]{:S(2)}, u32[]{:S(2)}) collective-permute-start(f32[32,128]{1,0:T(8,128)S(1)} %get-tuple-element.78.own_ref.old_ref), channel_id=1, source_target_pairs={{0,1},{1,0},{2,3},{3,2},{4,5},{5,4},{6,7},{7,6},{8,9},{9,8},{10,11... | collective-permute-start | bytes 49160 | tf_op jit(solution)/shard_map/ppermute | solution.py:430
  82.1 4.9 %collective-permute-start.7 = (f32[240,128]{1,0:T(8,128)S(1)}, f32[240,128]{1,0:T(8,128)S(1)}, u32[]{:S(2)}, u32[]{:S(2)}) collective-permute-start(f32[240,128]{1,0:T(8,128)S(1)} %slice.26), channel_id=1, source_target_pairs={{0,4},{4,0},{8,12},{12,8},{6,10},{10,6},{14,2},{2,14},{1,5},{5,1},... | collective-permute-start | bytes 368648 | tf_op jit(solution)/shard_map/ppermute | solution.py:394
  83.4 4.6 %collective-permute-start.11 = (f32[256,128]{1,0:T(8,128)S(1)}, f32[256,128]{1,0:T(8,128)S(1)}, u32[]{:S(2)}, u32[]{:S(2)}) collective-permute-start(f32[256,128]{1,0:T(8,128)S(1)} %slice_add_fusion.6.refs_1_), channel_id=1, source_target_pairs={{4,8},{8,4},{12,0},{0,12},{2,6},{6,2},{10,14},{14,10},{5,9},{9,5},... | collective-permute-start | bytes 393224 | tf_op jit(solution)/shard_map/ppermute | solution.py:394
  87.1 3.8 %collective-permute-start.10 = (f32[240,128]{1,0:T(8,128)S(1)}, f32[240,128]{1,0:T(8,128)S(1)}, u32[]{:S(2)}, u32[]{:S(2)}) collective-permute-start(f32[240,128]{1,0:T(8,128)S(1)} %slice_add_fusion.2.refs_0_), channel_id=1, source_target_pairs={{4,8},{8,4},{12,0},{0,12},{2,6},{6,2},{10,14},{14,10},{5,9},{9,5},... | collective-permute-start | bytes 368648 | tf_op jit(solution)/shard_map/ppermute | solution.py:394
  91.1 4.2 %collective-permute-start.12 = (f32[496,128]{1,0:T(8,128)S(1)}, f32[496,128]{1,0:T(8,128)S(1)}, u32[]{:S(2)}, u32[]{:S(2)}) collective-permute-start(f32[496,128]{1,0:T(8,128)S(1)} %get-tuple-element.88.dual_ref.refs_5_), channel_id=1, source_target_pairs={{0,2},{2,0},{1,3},{3,1},{4,6},{6,4},{5,7},{7,5},{8,10},{10,8},{9,1... | collective-permute-start | bytes 761864 | tf_op jit(solution)/shard_map/ppermute | solution.py:446
  123.7 4.2 %collective-permute-start.13 = (f32[496,128]{1,0:T(8,128)S(1)}, f32[496,128]{1,0:T(8,128)S(1)}, u32[]{:S(2)}, u32[]{:S(2)}) collective-permute-start(f32[496,128]{1,0:T(8,128)S(1)} %unit_flows.9), channel_id=1, source_target_pairs={{0,2},{2,0},{1,3},{3,1},{4,6},{6,4},{5,7},{7,5},{8,10},{10,8},{9,1... | collective-permute-start | bytes 761864 | tf_op jit(solution)/shard_map/ppermute | solution.py:424
  127.9 5.1 %collective-permute-start.16 = (f32[256,128]{1,0:T(8,128)S(1)}, f32[256,128]{1,0:T(8,128)S(1)}, u32[]{:S(2)}, u32[]{:S(2)}) collective-permute-start(f32[256,128]{1,0:T(8,128)S(1)} %slice.29), channel_id=1, source_target_pairs={{0,4},{4,0},{8,12},{12,8},{6,10},{10,6},{14,2},{2,14},{1,5},{5,1},... | collective-permute-start | bytes 393224 | tf_op jit(solution)/shard_map/ppermute | solution.py:394
  129.0 5.6 %collective-permute-start.15 = (f32[32,128]{1,0:T(8,128)S(1)}, f32[32,128]{1,0:T(8,128)S(1)}, u32[]{:S(2)}, u32[]{:S(2)}) collective-permute-start(f32[32,128]{1,0:T(8,128)S(1)} %get-tuple-element.94.own_ref.old_ref), channel_id=1, source_target_pairs={{0,1},{1,0},{2,3},{3,2},{4,5},{5,4},{6,7},{7,6},{8,9},{9,8},{10,11... | collective-permute-start | bytes 49160 | tf_op jit(solution)/shard_map/ppermute | solution.py:430
  129.7 4.9 %collective-permute-start.14 = (f32[240,128]{1,0:T(8,128)S(1)}, f32[240,128]{1,0:T(8,128)S(1)}, u32[]{:S(2)}, u32[]{:S(2)}) collective-permute-start(f32[240,128]{1,0:T(8,128)S(1)} %slice.28), channel_id=1, source_target_pairs={{0,4},{4,0},{8,12},{12,8},{6,10},{10,6},{14,2},{2,14},{1,5},{5,1},... | collective-permute-start | bytes 368648 | tf_op jit(solution)/shard_map/ppermute | solution.py:394
  133.1 3.9 %collective-permute-start.18 = (f32[256,128]{1,0:T(8,128)S(1)}, f32[256,128]{1,0:T(8,128)S(1)}, u32[]{:S(2)}, u32[]{:S(2)}) collective-permute-start(f32[256,128]{1,0:T(8,128)S(1)} %slice_add_fusion.5.refs_1_), channel_id=1, source_target_pairs={{4,8},{8,4},{12,0},{0,12},{2,6},{6,2},{10,14},{14,10},{5,9},{9,5},... | collective-permute-start | bytes 393224 | tf_op jit(solution)/shard_map/ppermute | solution.py:394
  134.6 4.1 %collective-permute-start.17 = (f32[240,128]{1,0:T(8,128)S(1)}, f32[240,128]{1,0:T(8,128)S(1)}, u32[]{:S(2)}, u32[]{:S(2)}) collective-permute-start(f32[240,128]{1,0:T(8,128)S(1)} %slice_add_fusion.1.refs_0_), channel_id=1, source_target_pairs={{4,8},{8,4},{12,0},{0,12},{2,6},{6,2},{10,14},{14,10},{5,9},{9,5},... | collective-permute-start | bytes 368648 | tf_op jit(solution)/shard_map/ppermute | solution.py:394
  171.5 4.2 %collective-permute-start.20 = (f32[496,128]{1,0:T(8,128)S(1)}, f32[496,128]{1,0:T(8,128)S(1)}, u32[]{:S(2)}, u32[]{:S(2)}) collective-permute-start(f32[496,128]{1,0:T(8,128)S(1)} %unit_flows.11), channel_id=1, source_target_pairs={{0,2},{2,0},{1,3},{3,1},{4,6},{6,4},{5,7},{7,5},{8,10},{10,8},{9,1... | collective-permute-start | bytes 761864 | tf_op jit(solution)/shard_map/ppermute | solution.py:424
  175.7 5.1 %collective-permute-start.22 = (f32[256,128]{1,0:T(8,128)S(1)}, f32[256,128]{1,0:T(8,128)S(1)}, u32[]{:S(2)}, u32[]{:S(2)}) collective-permute-start(f32[256,128]{1,0:T(8,128)S(1)} %slice.33), channel_id=1, source_target_pairs={{0,4},{4,0},{8,12},{12,8},{6,10},{10,6},{14,2},{2,14},{1,5},{5,1},... | collective-permute-start | bytes 393224 | tf_op jit(solution)/shard_map/ppermute | solution.py:394
  177.5 5.0 %collective-permute-start.21 = (f32[240,128]{1,0:T(8,128)S(1)}, f32[240,128]{1,0:T(8,128)S(1)}, u32[]{:S(2)}, u32[]{:S(2)}) collective-permute-start(f32[240,128]{1,0:T(8,128)S(1)} %slice.32), channel_id=1, source_target_pairs={{0,4},{4,0},{8,12},{12,8},{6,10},{10,6},{14,2},{2,14},{1,5},{5,1},... | collective-permute-start | bytes 368648 | tf_op jit(solution)/shard_map/ppermute | solution.py:394
  180.9 5.8 %collective-permute-start.24 = (f32[256,128]{1,0:T(8,128)S(1)}, f32[256,128]{1,0:T(8,128)S(1)}, u32[]{:S(2)}, u32[]{:S(2)}) collective-permute-start(f32[256,128]{1,0:T(8,128)S(1)} %slice_add_fusion.4.refs_1_), channel_id=1, source_target_pairs={{4,8},{8,4},{12,0},{0,12},{2,6},{6,2},{10,14},{14,10},{5,9},{9,5},... | collective-permute-start | bytes 393224 | tf_op jit(solution)/shard_map/ppermute | solution.py:394
  182.5 4.1 %collective-permute-start.23 = (f32[240,128]{1,0:T(8,128)S(1)}, f32[240,128]{1,0:T(8,128)S(1)}, u32[]{:S(2)}, u32[]{:S(2)}) collective-permute-start(f32[240,128]{1,0:T(8,128)S(1)} %slice_add_fusion.refs_0_), channel_id=1, source_target_pairs={{4,8},{8,4},{12,0},{0,12},{2,6},{6,2},{10,14},{14,10},{5,9},{9,5},... | collective-permute-start | bytes 368648 | tf_op jit(solution)/shard_map/ppermute | solution.py:394
  186.9 4.0 %collective-permute-start.25 = (f32[496,128]{1,0:T(8,128)S(1)}, f32[496,128]{1,0:T(8,128)S(1)}, u32[]{:S(2)}, u32[]{:S(2)}) collective-permute-start(f32[496,128]{1,0:T(8,128)S(1)} %dual_step.7.mine_ref), channel_id=1, source_target_pairs={{0,2},{2,0},{1,3},{3,1},{4,6},{6,4},{5,7},{7,5},{8,10},{10,8},{9,1... | collective-permute-start | bytes 761864 | tf_op jit(solution)/shard_map/ppermute | solution.py:442
  (3 other events, 9.3 us)

commit v4 on v3

--- a/solution.py
+++ b/solution.py
@@ -1,3 +1,5 @@
+import functools
+
 import jax
 import jax.numpy as jnp
 from jax import lax
@@ -22,6 +24,7 @@
 HALF = 496
 BLOCK = 256
 PART = 248
+KEPT = 400
 CHUNKS = ((0, 240), (240, HALF))
 BF16 = jnp.bfloat16
 F32 = jnp.float32
@@ -66,7 +69,7 @@
 
 
 def table_kernel(
-    place_ref, bus_in, type_in, limit_in, cost_in, load_in, table_ref, first_ref, copies_ref, load_ref,
+    place_ref, bus_in, type_in, limit_in, cost_in, table_ref, first_ref, copies_ref,
     bus_ref, type_ref, limit_ref, cost_ref, arrived
 ):
     pairs = (
@@ -74,12 +77,11 @@
         (type_in, type_ref.at[0]),
         (limit_in, limit_ref.at[0]),
         (cost_in, cost_ref.at[0]),
-        (load_in, load_ref),
     )
     copies = [pltpu.make_async_copy(*pair, arrived.at[spot]) for spot, pair in enumerate(pairs)]
     for copy in copies:
         copy.start()
-    for copy in copies[:-1]:
+    for copy in copies:
         copy.wait()
     kinds = column(type_ref[...])
     capacity = column(limit_ref[...]).astype(F32) / 100.0
@@ -100,93 +102,138 @@
     extrap = jnp.sum(jnp.where(same, 2.0 * first, 0.0), axis=0, keepdims=True)
     sent = jnp.where(lax.broadcasted_iota(jnp.int32, (8, 128), 0) == 0, bus, extrap)
     copies_ref[...] = jnp.broadcast_to(sent[None], copies_ref.shape)
-    copies[-1].wait()
-
-
-def unit_tables(place, unit_bus, unit_type, unit_limit, unit_cost, load, line_count):
+
+
+def unit_tables(place, unit_bus, unit_type, unit_limit, unit_cost, line_count):
     units = unit_bus.shape[0]
     rows = (unit_bus, unit_type, unit_limit, unit_cost)
     one = jax.ShapeDtypeStruct((units, 128), F32)
     return pl.pallas_call(
         table_kernel,
-        in_specs=[SMEM] + [pl.BlockSpec(memory_space=pltpu.HBM)] * 5,
-        out_specs=[VMEM] * 4,
+        in_specs=[SMEM] + [pl.BlockSpec(memory_space=pltpu.HBM)] * 4,
+        out_specs=[VMEM] * 3,
         out_shape=[
             one,
             one,
             jax.ShapeDtypeStruct((line_count, 8, 128), F32),
-            jax.ShapeDtypeStruct(load.shape, F32),
         ],
         scratch_shapes=[pltpu.VMEM((1, units), row.dtype) for row in rows]
-        + [pltpu.SemaphoreType.DMA((5,))],
+        + [pltpu.SemaphoreType.DMA((4,))],
         compiler_params=params(16),
         name="unit_tables",
-    )(place, *(pltpu.with_memory_space_constraint(x, pltpu.HBM) for x in (*rows, load)))
-
-
-def first_kernel(core_ref, ptdf_ref, unit_ref, load_ref, mine_ref, other_ref, pair_ref):
+    )(place, *(pltpu.with_memory_space_constraint(x, pltpu.HBM) for x in rows))
+
+
+def load_kernel(ptdf_ref, load_ref, flow_ref, kept_ref, pair_ref):
     step = pl.program_id(0)
 
     @pl.when(step == 0)
     def _():
-        peers = unit_ref.shape[0]
-        span = load_ref.shape[0] // peers
-        units = 32
-        lane = lax.broadcasted_iota(jnp.int32, (span, 128), 1)
-        for peer in range(peers):
-            spots = unit_ref[peer][0:1, :].astype(jnp.int32)
-            bus = row_index((span, 128), peer * span)
-            held = jnp.where((bus == spots) & (lane < units), unit_ref[peer][1:2, :], 0.0)
-            rows = slice(peer * span, (peer + 1) * span)
-            injection = jnp.sum(held, axis=1, keepdims=True) - load_ref[rows, :]
-            high, low = halves(injection)
-            pair_ref[rows, :128] = high
-            pair_ref[rows, 128:] = low
+        high, low = halves(load_ref[...])
+        pair_ref[:, :128] = high
+        pair_ref[:, 128:] = low
+
+    for start in range(0, KEPT, PART):
+        count = min(PART, KEPT - start)
+
+        @pl.when(step == start // PART)
+        def _(start=start, count=count):
+            kept_ref[start : start + count, :] = ptdf_ref[:count, :]
 
     rows = row_index(ptdf_ref.shape, step * PART)
     ptdf = jnp.where(rows < LINES_DEV, ptdf_ref[...], jnp.where(rows == LINES_DEV, 1.0, 0.0))
     high, low = halves(ptdf)
     both = dot(high, pair_ref[...])
-    flow = both[:, :128] + both[:, 128:] + dot(low, pair_ref[:, :128])
-    rows = pl.ds(pl.multiple_of((step % 2) * PART, 8), PART)
-    mine = step // 2 == core_ref[0]
-
-    @pl.when(mine)
-    def _():
-        mine_ref[rows, :] = flow
-
-    @pl.when(jnp.logical_not(mine))
-    def _():
-        other_ref[rows, :] = flow
-
-
-def first_flows(core, ptdf, unit_rows, load):
+    flow_ref[...] = both[:, :128] + both[:, 128:] + dot(low, pair_ref[:, :128])
+
+
+def load_flows(ptdf, load):
     buses = ptdf.shape[1]
-    half = jax.ShapeDtypeStruct((HALF, 128), F32)
-    whole = pl.BlockSpec((HALF, 128), lambda i: (0, 0))
-    return pl.pallas_call(
-        first_kernel,
+    return pl.pallas_call(
+        load_kernel,
         grid=(2 * HALF // PART,),
         in_specs=[
-            SMEM,
             pl.BlockSpec((PART, buses), lambda i: (i, 0)),
-            pl.BlockSpec(unit_rows.shape, lambda i: (0, 0, 0)),
             pl.BlockSpec((buses, 128), lambda i: (0, 0)),
         ],
-        out_specs=[whole, whole],
+        out_specs=[
+            pl.BlockSpec((PART, 128), lambda i: (i, 0)),
+            pl.BlockSpec((KEPT, buses), lambda i: (0, 0)),
+        ],
+        out_shape=[
+            jax.ShapeDtypeStruct((2 * HALF, 128), F32),
+            jax.ShapeDtypeStruct((KEPT, buses), F32),
+        ],
+        scratch_shapes=[pltpu.VMEM((buses, 256), BF16)],
+        compiler_params=params(40),
+        cost_estimate=cost_of(3 * 2 * ROWS * buses * 128, 4 * ROWS * buses),
+        name="load_flows",
+    )(*(pltpu.with_memory_space_constraint(x, pltpu.HBM) for x in (ptdf, load)))
+
+
+def first_kernel(
+    core_ref, ptdf_in, load_in, kept_ref, unit_ref, mine_ref, other_ref, rest_ref, load_ref, flow_ref, arrived
+):
+    load = pltpu.make_async_copy(load_in, load_ref, arrived.at[0])
+    load.start()
+    rest_rows = ptdf_in.at[pl.ds(KEPT, LINES_DEV - KEPT), :]
+    copy = pltpu.make_async_copy(rest_rows, rest_ref, arrived.at[1])
+    copy.start()
+    peers, buses = unit_ref.shape[0], ptdf_in.shape[1]
+    span, units = buses // peers, 32
+    lane = lax.broadcasted_iota(jnp.int32, (units, 128), 1)
+    tiles = [jnp.zeros((units, 128), F32)] * (buses // 128)
+    for peer in range(peers):
+        spots = column(unit_ref[peer][0:1, :units]).astype(jnp.int32)
+        extrap = column(unit_ref[peer][1:2, :units])
+        for tile in range(peer * span // 128, ((peer + 1) * span - 1) // 128 + 1):
+            tiles[tile] += jnp.where(lane + tile * 128 == spots, extrap, 0.0)
+    injection = jnp.concatenate(
+        [jnp.sum(tile, axis=0, keepdims=True) for tile in tiles], axis=1
+    )
+    load.wait()
+    flow_ref[:KEPT, :] = jnp.sum(kept_ref[...] * injection, axis=1, keepdims=True) - load_ref[:KEPT, :]
+    total = jnp.sum(injection, axis=1, keepdims=True)
+    end = row_index((2 * HALF - LINES_DEV, 128), LINES_DEV)
+    flow_ref[LINES_DEV:, :] = jnp.where(end == LINES_DEV, total, 0.0) - load_ref[LINES_DEV:, :]
+    copy.wait()
+    rest = jnp.sum(rest_ref[...] * injection, axis=1, keepdims=True)
+    flow_ref[KEPT:LINES_DEV, :] = rest - load_ref[KEPT:LINES_DEV, :]
+    core = core_ref[0]
+    for ref, place in ((other_ref, 1 - core), (mine_ref, core)):
+        ref[...] = flow_ref[pl.ds(pl.multiple_of(place * HALF, 8), HALF), :]
+
+
+def first_flows(core, ptdf, kept, unit_rows, load):
+    half = jax.ShapeDtypeStruct((HALF, 128), F32)
+    return pl.pallas_call(
+        first_kernel,
+        in_specs=[SMEM] + [pl.BlockSpec(memory_space=pltpu.HBM)] * 2 + [VMEM, VMEM],
+        out_specs=[VMEM, VMEM],
         out_shape=[half, half],
-        scratch_shapes=[pltpu.VMEM((buses, 256), BF16)],
-        compiler_params=params(48),
-        cost_estimate=cost_of(3 * 2 * ROWS * buses * 128, 4 * ROWS * buses),
+        scratch_shapes=[
+            pltpu.VMEM((LINES_DEV - KEPT, ptdf.shape[1]), F32),
+            pltpu.VMEM((2 * HALF, 128), F32),
+            pltpu.VMEM((2 * HALF, 128), F32),
+            pltpu.SemaphoreType.DMA((2,)),
+        ],
+        compiler_params=params(24),
+        cost_estimate=cost_of(2 * ROWS * ptdf.shape[1], 4 * ROWS * ptdf.shape[1]),
         name="first_flows",
-    )(core, ptdf, unit_rows, load)
-
-
-def columns_kernel(ptdf_ref, unit_ref, high_ref, low_ref, pick_ref):
+    )(
+        core,
+        pltpu.with_memory_space_constraint(ptdf, pltpu.HBM),
+        pltpu.with_memory_space_constraint(load, pltpu.HBM),
+        kept,
+        unit_rows,
+    )
+
+
+def columns_kernel(part, ptdf_ref, unit_ref, out_ref, pick_ref):
     step = pl.program_id(0)
     peers = unit_ref.shape[0]
     span = ptdf_ref.shape[1] // 2
-    units = high_ref.shape[1] // 2
+    units = out_ref.shape[1] // 2
     local = units * 2 // peers
 
     @pl.when(step == 0)
@@ -202,30 +249,26 @@
     inside = row_index((BLOCK, span), step * BLOCK) < LINES_DEV
     for group in range(2):
         ptdf = jnp.where(inside, ptdf_ref[:, group * span : (group + 1) * span], 0.0)
-        high, low = halves(ptdf)
-        pick = pick_ref[group]
-        high = dot(high, pick, ((1,), (1,)))
-        low = dot(low, pick, ((1,), (1,)))
-        where = slice(group * units, (group + 1) * units)
-        high_ref[:, where] = jnp.where(rows == LINES_DEV, 1.0, high).astype(BF16)
-        low_ref[:, where] = low.astype(BF16)
-
-
-def unit_columns(ptdf, unit_rows, units):
+        value = dot(halves(ptdf)[part], pick_ref[group], ((1,), (1,)))
+        if part == 0:
+            value = jnp.where(rows == LINES_DEV, 1.0, value)
+        out_ref[:, group * units : (group + 1) * units] = value.astype(BF16)
+
+
+def unit_columns(part, ptdf, unit_rows, units):
     buses = ptdf.shape[1]
-    by_row = pl.BlockSpec((BLOCK, units), lambda i: (i, 0))
-    return pl.pallas_call(
-        columns_kernel,
+    return pl.pallas_call(
+        functools.partial(columns_kernel, part),
         grid=(ROWS // BLOCK,),
         in_specs=[
             pl.BlockSpec((BLOCK, buses), lambda i: (i, 0)),
             pl.BlockSpec(unit_rows.shape, lambda i: (0, 0, 0)),
         ],
-        out_specs=[by_row, by_row],
-        out_shape=[jax.ShapeDtypeStruct((ROWS, units), BF16)] * 2,
+        out_specs=pl.BlockSpec((BLOCK, units), lambda i: (i, 0)),
+        out_shape=jax.ShapeDtypeStruct((ROWS, units), BF16),
         scratch_shapes=[pltpu.VMEM((2, units // 2, buses // 2), BF16)],
         compiler_params=params(48),
-        cost_estimate=cost_of(2 * 2 * ROWS * buses * units // 2, 4 * ROWS * buses),
+        cost_estimate=cost_of(2 * ROWS * buses * units // 2, 4 * ROWS * buses),
         name="unit_columns",
     )(ptdf, unit_rows)
 
@@ -401,11 +444,12 @@
     core = lax.axis_index("c").astype(jnp.int32)
     place = lax.axis_index("t").astype(jnp.int32)[None]
     block = (lax.axis_index(BUS) * ptdf.shape[1]).astype(jnp.int32)
-    table, gen, copies, load = unit_tables(
-        block[None], unit_bus, unit_type, unit_limit, unit_cost, bus_load, line_count
+    table, gen, copies = unit_tables(
+        block[None], unit_bus, unit_type, unit_limit, unit_cost, line_count
     )
     unit_rows = lax.all_to_all(copies, LINE, 0, 0, tiled=True)
-    mine, other = first_flows(core[None], ptdf, unit_rows, load)
+    load, kept = load_flows(ptdf, bus_load)
+    mine, other = first_flows(core[None], ptdf, kept, unit_rows, load)
     extrap = far = 2.0 * gen
 
     pad = jnp.zeros((2 * HALF - LINES_DEV,), F32)
@@ -424,19 +468,23 @@
         total = mine + lax.ppermute(other, "c", SWAP)
         if iteration == 0:
             total, tied, rows = lax.optimization_barrier((total, ptdf, unit_rows))
-            high, low = unit_columns(tied, rows, line_count * local)
+            high = unit_columns(0, tied, rows, line_count * local)
         elif not last:
             total, tied = lax.optimization_barrier((total, extrap))
             far = lax.ppermute(tied, "t", SWAP)
         lefts = [total[start:stop] for start, stop in CHUNKS]
         lefts = [left + along_y(left, (NEAR, FAR)) for left in lefts]
-        if 0 < iteration < ITERS - 1:
+        if iteration == 0:
+            lefts[1], high = lax.optimization_barrier((lefts[1], high))
+            lefts[0], tied, rows = lax.optimization_barrier((lefts[0], tied, rows))
+            low = unit_columns(1, tied, rows, line_count * local)
+        elif not last:
             lefts[0], far = lax.optimization_barrier((lefts[0], far))
         if not last:
             ramp, store, state = state_step(place, extrap, far, ramp, store, table)
         rights = [along_y(left, (FAR, NEAR)) for left in lefts]
         if iteration == 0:
-            rights[-1], high, low = lax.optimization_barrier((rights[-1], high, low))
+            rights[-1], low = lax.optimization_barrier((rights[-1], low))
         if last:
             (dual,) = dual_step(lefts, rights, flow, dual, steps, limits, 1)
             return gen, joined(core, dual, lax.ppermute(dual, "c", SWAP))

time: 192 us -> 192 us (level)
  waiting for transfers between devices: 39.3 us -> 26.9 us
  Pallas kernels: 22.2 us -> 28.3 us
  starting transfers between devices: 46 us -> 50.3 us
    ppermute x16, waiting for transfers between devices: 25.6 us -> 18.2 us  [along_y(): return lax.ppermute(value, BUS, pairs)]
    pallas_call x2 -> x4, Pallas kernels: 9.89 us -> 16.4 us  [the longest x2 8.68 us: unit_columns(): pl.pallas_call(functools.partial(columns_kernel, part), grid=(ROWS // BLO...]
    all_to_all x1, waiting for transfers between devices: 7.2 us -> 2.04 us  [on_device(): unit_rows = lax.all_to_all(copies, LINE, 0, 0, tiled=True)]
  transfers between devices with their start and end apart: 27 -> 27, of which waited for: 21 -> 19; matrix products, arithmetic and copies ran while one was open for 1% -> 0% of each run, Pallas kernels for 5% -> 10%
where the time goes in v4:
time: 192 us; the launch traced here: 191 us
  blocking collectives  83.3 us (43%)
  starting transfers between devices  50.3 us (26%)
  Pallas kernels  28.3 us (15%)
  waiting for transfers between devices  26.9 us (14%)
    all_to_all x3, blocking collectives, on_device(): prices = lax.all_to_all(prices, LINE, 0, 0, tiled=True)  43.3 us
    all_to_all x3, blocking collectives, on_device(): lax.all_to_all(copies, LINE, 0, 0, tiled=True).reshape(-1, hour_dev)  40 us
    ppermute x16, waiting for transfers between devices, along_y(): return lax.ppermute(value, BUS, pairs)  18.2 us
    ppermute x16, starting transfers between devices, along_y(): return lax.ppermute(value, BUS, pairs)  13.3 us
    ppermute x4, starting transfers between devices, on_device(): total = mine + lax.ppermute(other, 'c', SWAP)  11.4 us
    all_to_all x1, starting transfers between devices, on_device(): unit_rows = lax.all_to_all(copies, LINE, 0, 0, tiled=True)  10 us
    pallas_call x2, Pallas kernels, unit_columns(): pl.pallas_call(functools.partial(columns_kernel, part), grid=(ROWS // BLO...  8.68 us
    ppermute x3, starting transfers between devices, on_device(): lax.ppermute(dual, 'c', SWAP)  7.79 us
  transfers between devices with their start and end apart: 27, of which 19 were waited for; matrix products, arithmetic and copies ran while one was open for 0% of the time, Pallas kernels for 10%

profile of v4, /device:TPU:1, one launch (start us, length us, event | category | flops | bytes accessed | tf_op | source)
XLA Modules:
  0.0 191.3 jit_solution(16238585188959254498)
XLA Ops:
  2.1 10.0 %all-to-all-start = ((f32[16,8,128]{2,1,0:T(8,128)}), f32[16,8,128]{2,1,0:T(8,128)S(1)}, u32[]{:S(2)}, u32[]{:S(2)}) async-start(f32[16,8,128]{2,1,0:T(8,128)} %get-tuple-element.60), calls=%async_computation | async-start | bytes 131072 | tf_op jit(solution)/shard_map/all_to_all | solution.py:450
  12.2 5.1 %load_flows.1 = (f32[992,128]{1,0:T(8,128)S(1)}, f32[400,1536]{1,0:T(8,128)S(1)}) custom-call(f32[960,1536]{1,0:T(8,128)} %ptdf_ref.3, f32[1536,128]{1,0:T(8,128)} %load_ref.1), custom_call_target="tpu_custom_call" | custom-call | flops 1207959552 | bytes 6291456 | tf_op jit(solution)/shard_map/load_flows/pallas_call | solution.py:152
  20.1 2.6 %first_flows.1 = (f32[496,128]{1,0:T(8,128)S(1)}, f32[496,128]{1,0:T(8,128)S(1)}) custom-call(s32[1]{0:T(128)} %bitcast.core_ref.place_ref, f32[960,1536]{1,0:T(8,128)} %ptdf_ref.3, f32[992,128]{1,0:T(8,128)} %copy-done, f32[400,1536]{1,0:T(8,128)S(1)} %get-tuple-element.59.kept_ref, f32[16,8,128]{2,1,0:T(8,128)S(1)} %all-to-all-done.unit_ref), custom_call_target="tpu_custom_call" | custom-call | flops 3145728 | bytes 6291456 | tf_op jit(solution)/shard_map/first_flows/pallas_call | solution.py:209
  26.1 2.8 %collective-permute-start.3 = (f32[240,128]{1,0:T(8,128)S(1)}, f32[240,128]{1,0:T(8,128)S(1)}, u32[]{:S(2)}, u32[]{:S(2)}) collective-permute-start(f32[240,128]{1,0:T(8,128)S(1)} %slice.25), channel_id=1, source_target_pairs={{0,4},{4,0},{8,12},{12,8},{6,10},{10,6},{14,2},{2,14},{1,5},{5,1},... | collective-permute-start | bytes 368648 | tf_op jit(solution)/shard_map/ppermute | solution.py:437
  29.1 4.3 %unit_columns.2.high_ref = bf16[1024,512]{1,0:T(8,128)(2,1)S(1)} custom-call(f32[960,1536]{1,0:T(8,128)} %ptdf_ref.3, f32[16,8,128]{2,1,0:T(8,128)S(1)} %all-to-all-done.unit_ref), custom_call_target="tpu_custom_call" | custom-call | flops 805306368 | bytes 6291456 | tf_op jit(solution)/shard_map/unit_columns/pallas_call | solution.py:260
  36.0 4.3 %unit_columns.3.low_ref = bf16[1024,512]{1,0:T(8,128)(2,1)S(1)} custom-call(f32[960,1536]{1,0:T(8,128)} %ptdf_ref.3, f32[16,8,128]{2,1,0:T(8,128)S(1)} %all-to-all-done.unit_ref), custom_call_target="tpu_custom_call" | custom-call | flops 805306368 | bytes 6291456 | tf_op jit(solution)/shard_map/unit_columns/pallas_call | solution.py:260
  40.7 2.2 %collective-permute-start.5 = (f32[496,128]{1,0:T(8,128)S(1)}, f32[496,128]{1,0:T(8,128)S(1)}, u32[]{:S(2)}, u32[]{:S(2)}) collective-permute-start(f32[496,128]{1,0:T(8,128)S(1)} %get-tuple-element.79.dual_ref.refs_5_), channel_id=1, source_target_pairs={{0,2},{2,0},{1,3},{3,1},{4,6},{6,4},{5,7},{7,5},{8,10},{10,8},{9,1... | collective-permute-start | bytes 761864 | tf_op jit(solution)/shard_map/ppermute | solution.py:494
  44.6 15.5 %all_to_all.35.price_ref = f32[16,32,128]{2,1,0:T(8,128)S(1)} all-to-all(f32[16,32,128]{2,1,0:T(8,128)S(1)} %bitcast.16), channel_id=1, replica_groups=mesh['z'=8,'xl'=2,'y'=4,'c'=2,'t'=2] {'z','xl'}, dimensions={0} | all-to-all | bytes 524288 | tf_op jit(solution)/shard_map/all_to_all | solution.py:496
  60.1 13.4 %all_to_all.36 = f32[16,32,128]{2,1,0:T(8,128)S(1)} all-to-all(f32[16,32,128]{2,1,0:T(8,128)S(1)} %get-tuple-element.81), channel_id=1, replica_groups=mesh['z'=8,'xl'=2,'y'=4,'c'=2,'t'=2] {'z','xl'}, dimensions={0} | all-to-all | bytes 524288 | tf_op jit(solution)/shard_map/all_to_all | solution.py:498
  74.0 3.0 %collective-permute-start.6 = (f32[496,128]{1,0:T(8,128)S(1)}, f32[496,128]{1,0:T(8,128)S(1)}, u32[]{:S(2)}, u32[]{:S(2)}) collective-permute-start(f32[496,128]{1,0:T(8,128)S(1)} %unit_flows.7), channel_id=1, source_target_pairs={{0,2},{2,0},{1,3},{3,1},{4,6},{6,4},{5,7},{7,5},{8,10},{10,8},{9,1... | collective-permute-start | bytes 761864 | tf_op jit(solution)/shard_map/ppermute | solution.py:468
  81.1 2.5 %collective-permute-start.8 = (f32[32,128]{1,0:T(8,128)S(1)}, f32[32,128]{1,0:T(8,128)S(1)}, u32[]{:S(2)}, u32[]{:S(2)}) collective-permute-start(f32[32,128]{1,0:T(8,128)S(1)} %get-tuple-element.84.own_ref.old_ref), channel_id=1, source_target_pairs={{0,1},{1,0},{2,3},{3,2},{4,5},{5,4},{6,7},{7,6},{8,9},{9,8},{10,11... | collective-permute-start | bytes 49160 | tf_op jit(solution)/shard_map/ppermute | solution.py:474
  87.4 2.2 %collective-permute-done.10.refs_2_ = f32[240,128]{1,0:T(8,128)S(1)} collective-permute-done((f32[240,128]{1,0:T(8,128)S(1)}, f32[240,128]{1,0:T(8,128)S(1)}, u32[]{:S(2)}, u32[]{:S(2)}) %collective-permute-start.10) | collective-permute-done | bytes 122912 | tf_op jit(solution)/shard_map/ppermute | solution.py:437
  89.9 2.8 %collective-permute-start.12 = (f32[496,128]{1,0:T(8,128)S(1)}, f32[496,128]{1,0:T(8,128)S(1)}, u32[]{:S(2)}, u32[]{:S(2)}) collective-permute-start(f32[496,128]{1,0:T(8,128)S(1)} %get-tuple-element.94.dual_ref.refs_5_), channel_id=1, source_target_pairs={{0,2},{2,0},{1,3},{3,1},{4,6},{6,4},{5,7},{7,5},{8,10},{10,8},{9,1... | collective-permute-start | bytes 761864 | tf_op jit(solution)/shard_map/ppermute | solution.py:494
  94.5 13.9 %all_to_all.37.price_ref = f32[16,32,128]{2,1,0:T(8,128)S(1)} all-to-all(f32[16,32,128]{2,1,0:T(8,128)S(1)} %bitcast.17), channel_id=1, replica_groups=mesh['z'=8,'xl'=2,'y'=4,'c'=2,'t'=2] {'z','xl'}, dimensions={0} | all-to-all | bytes 524288 | tf_op jit(solution)/shard_map/all_to_all | solution.py:496
  108.5 13.3 %all_to_all.38 = f32[16,32,128]{2,1,0:T(8,128)S(1)} all-to-all(f32[16,32,128]{2,1,0:T(8,128)S(1)} %get-tuple-element.97), channel_id=1, replica_groups=mesh['z'=8,'xl'=2,'y'=4,'c'=2,'t'=2] {'z','xl'}, dimensions={0} | all-to-all | bytes 524288 | tf_op jit(solution)/shard_map/all_to_all | solution.py:498
  122.3 3.1 %collective-permute-start.13 = (f32[496,128]{1,0:T(8,128)S(1)}, f32[496,128]{1,0:T(8,128)S(1)}, u32[]{:S(2)}, u32[]{:S(2)}) collective-permute-start(f32[496,128]{1,0:T(8,128)S(1)} %unit_flows.9), channel_id=1, source_target_pairs={{0,2},{2,0},{1,3},{3,1},{4,6},{6,4},{5,7},{7,5},{8,10},{10,8},{9,1... | collective-permute-start | bytes 761864 | tf_op jit(solution)/shard_map/ppermute | solution.py:468
  129.4 2.5 %collective-permute-start.15 = (f32[32,128]{1,0:T(8,128)S(1)}, f32[32,128]{1,0:T(8,128)S(1)}, u32[]{:S(2)}, u32[]{:S(2)}) collective-permute-start(f32[32,128]{1,0:T(8,128)S(1)} %get-tuple-element.100.own_ref.old_ref), channel_id=1, source_target_pairs={{0,1},{1,0},{2,3},{3,2},{4,5},{5,4},{6,7},{7,6},{8,9},{9,8},{10,11... | collective-permute-start | bytes 49160 | tf_op jit(solution)/shard_map/ppermute | solution.py:474
  138.1 2.7 %collective-permute-start.19 = (f32[496,128]{1,0:T(8,128)S(1)}, f32[496,128]{1,0:T(8,128)S(1)}, u32[]{:S(2)}, u32[]{:S(2)}) collective-permute-start(f32[496,128]{1,0:T(8,128)S(1)} %get-tuple-element.108.dual_ref.refs_5_), channel_id=1, source_target_pairs={{0,2},{2,0},{1,3},{3,1},{4,6},{6,4},{5,7},{7,5},{8,10},{10,8},{9,1... | collective-permute-start | bytes 761864 | tf_op jit(solution)/shard_map/ppermute | solution.py:494
  142.5 13.9 %all_to_all.39.price_ref = f32[16,32,128]{2,1,0:T(8,128)S(1)} all-to-all(f32[16,32,128]{2,1,0:T(8,128)S(1)} %bitcast.18), channel_id=1, replica_groups=mesh['z'=8,'xl'=2,'y'=4,'c'=2,'t'=2] {'z','xl'}, dimensions={0} | all-to-all | bytes 524288 | tf_op jit(solution)/shard_map/all_to_all | solution.py:496
  157.2 13.3 %all_to_all.40 = f32[16,32,128]{2,1,0:T(8,128)S(1)} all-to-all(f32[16,32,128]{2,1,0:T(8,128)S(1)} %get-tuple-element.112), channel_id=1, replica_groups=mesh['z'=8,'xl'=2,'y'=4,'c'=2,'t'=2] {'z','xl'}, dimensions={0} | all-to-all | bytes 524288 | tf_op jit(solution)/shard_map/all_to_all | solution.py:498
  170.9 3.1 %collective-permute-start.20 = (f32[496,128]{1,0:T(8,128)S(1)}, f32[496,128]{1,0:T(8,128)S(1)}, u32[]{:S(2)}, u32[]{:S(2)}) collective-permute-start(f32[496,128]{1,0:T(8,128)S(1)} %unit_flows.11), channel_id=1, source_target_pairs={{0,2},{2,0},{1,3},{3,1},{4,6},{6,4},{5,7},{7,5},{8,10},{10,8},{9,1... | collective-permute-start | bytes 761864 | tf_op jit(solution)/shard_map/ppermute | solution.py:468
  178.0 2.3 %collective-permute-done.22 = f32[256,128]{1,0:T(8,128)S(1)} collective-permute-done((f32[256,128]{1,0:T(8,128)S(1)}, f32[256,128]{1,0:T(8,128)S(1)}, u32[]{:S(2)}, u32[]{:S(2)}) %collective-permute-start.22) | collective-permute-done | bytes 131104 | tf_op jit(solution)/shard_map/ppermute | solution.py:437
  182.1 4.0 %collective-permute-done.23.refs_2_ = f32[240,128]{1,0:T(8,128)S(1)} collective-permute-done((f32[240,128]{1,0:T(8,128)S(1)}, f32[240,128]{1,0:T(8,128)S(1)}, u32[]{:S(2)}, u32[]{:S(2)}) %collective-permute-start.23) | collective-permute-done | bytes 122912 | tf_op jit(solution)/shard_map/ppermute | solution.py:437
  186.5 2.8 %collective-permute-start.25 = (f32[496,128]{1,0:T(8,128)S(1)}, f32[496,128]{1,0:T(8,128)S(1)}, u32[]{:S(2)}, u32[]{:S(2)}) collective-permute-start(f32[496,128]{1,0:T(8,128)S(1)} %dual_step.7.mine_ref), channel_id=1, source_target_pairs={{0,2},{2,0},{1,3},{3,1},{4,6},{6,4},{5,7},{7,5},{8,10},{10,8},{9,1... | collective-permute-start | bytes 761864 | tf_op jit(solution)/shard_map/ppermute | solution.py:490
  (95 shorter events, 44.5 us)
Async XLA Ops:
  2.1 18.0 %all-to-all-start = ((f32[16,8,128]{2,1,0:T(8,128)}), f32[16,8,128]{2,1,0:T(8,128)S(1)}, u32[]{:S(2)}, u32[]{:S(2)}) async-start(f32[16,8,128]{2,1,0:T(8,128)} %get-tuple-element.60), calls=%async_computation | async-start | bytes 131072 | tf_op jit(solution)/shard_map/all_to_all | solution.py:450
  26.1 7.4 %collective-permute-start.3 = (f32[240,128]{1,0:T(8,128)S(1)}, f32[240,128]{1,0:T(8,128)S(1)}, u32[]{:S(2)}, u32[]{:S(2)}) collective-permute-start(f32[240,128]{1,0:T(8,128)S(1)} %slice.25), channel_id=1, source_target_pairs={{0,4},{4,0},{8,12},{12,8},{6,10},{10,6},{14,2},{2,14},{1,5},{5,1},... | collective-permute-start | bytes 368648 | tf_op jit(solution)/shard_map/ppermute | solution.py:437
  29.0 5.1 %collective-permute-start.1 = (f32[256,128]{1,0:T(8,128)S(1)}, f32[256,128]{1,0:T(8,128)S(1)}, u32[]{:S(2)}, u32[]{:S(2)}) collective-permute-start(f32[256,128]{1,0:T(8,128)S(1)} %slice.24), channel_id=1, source_target_pairs={{0,4},{4,0},{8,12},{12,8},{6,10},{10,6},{14,2},{2,14},{1,5},{5,1},... | collective-permute-start | bytes 393224 | tf_op jit(solution)/shard_map/ppermute | solution.py:437
  33.5 6.9 %collective-permute-start.4 = (f32[240,128]{1,0:T(8,128)S(1)}, f32[240,128]{1,0:T(8,128)S(1)}, u32[]{:S(2)}, u32[]{:S(2)}) collective-permute-start(f32[240,128]{1,0:T(8,128)S(1)} %slice_add_fusion.3.refs_0_), channel_id=1, source_target_pairs={{4,8},{8,4},{12,0},{0,12},{2,6},{6,2},{10,14},{14,10},{5,9},{9,5},... | collective-permute-start | bytes 368648 | tf_op jit(solution)/shard_map/ppermute | solution.py:437
  34.1 6.2 %collective-permute-start.2 = (f32[256,128]{1,0:T(8,128)S(1)}, f32[256,128]{1,0:T(8,128)S(1)}, u32[]{:S(2)}, u32[]{:S(2)}) collective-permute-start(f32[256,128]{1,0:T(8,128)S(1)} %slice_add_fusion.7.refs_1_), channel_id=1, source_target_pairs={{4,8},{8,4},{12,0},{0,12},{2,6},{6,2},{10,14},{14,10},{5,9},{9,5},... | collective-permute-start | bytes 393224 | tf_op jit(solution)/shard_map/ppermute | solution.py:437
  74.0 4.2 %collective-permute-start.6 = (f32[496,128]{1,0:T(8,128)S(1)}, f32[496,128]{1,0:T(8,128)S(1)}, u32[]{:S(2)}, u32[]{:S(2)}) collective-permute-start(f32[496,128]{1,0:T(8,128)S(1)} %unit_flows.7), channel_id=1, source_target_pairs={{0,2},{2,0},{1,3},{3,1},{4,6},{6,4},{5,7},{7,5},{8,10},{10,8},{9,1... | collective-permute-start | bytes 761864 | tf_op jit(solution)/shard_map/ppermute | solution.py:468
  78.2 5.3 %collective-permute-start.9 = (f32[256,128]{1,0:T(8,128)S(1)}, f32[256,128]{1,0:T(8,128)S(1)}, u32[]{:S(2)}, u32[]{:S(2)}) collective-permute-start(f32[256,128]{1,0:T(8,128)S(1)} %slice.27), channel_id=1, source_target_pairs={{0,4},{4,0},{8,12},{12,8},{6,10},{10,6},{14,2},{2,14},{1,5},{5,1},... | collective-permute-start | bytes 393224 | tf_op jit(solution)/shard_map/ppermute | solution.py:437
  80.3 5.3 %collective-permute-start.7 = (f32[240,128]{1,0:T(8,128)S(1)}, f32[240,128]{1,0:T(8,128)S(1)}, u32[]{:S(2)}, u32[]{:S(2)}) collective-permute-start(f32[240,128]{1,0:T(8,128)S(1)} %slice.26), channel_id=1, source_target_pairs={{0,4},{4,0},{8,12},{12,8},{6,10},{10,6},{14,2},{2,14},{1,5},{5,1},... | collective-permute-start | bytes 368648 | tf_op jit(solution)/shard_map/ppermute | solution.py:437
  81.1 4.6 %collective-permute-start.8 = (f32[32,128]{1,0:T(8,128)S(1)}, f32[32,128]{1,0:T(8,128)S(1)}, u32[]{:S(2)}, u32[]{:S(2)}) collective-permute-start(f32[32,128]{1,0:T(8,128)S(1)} %get-tuple-element.84.own_ref.old_ref), channel_id=1, source_target_pairs={{0,1},{1,0},{2,3},{3,2},{4,5},{5,4},{6,7},{7,6},{8,9},{9,8},{10,11... | collective-permute-start | bytes 49160 | tf_op jit(solution)/shard_map/ppermute | solution.py:474
  83.5 3.9 %collective-permute-start.11 = (f32[256,128]{1,0:T(8,128)S(1)}, f32[256,128]{1,0:T(8,128)S(1)}, u32[]{:S(2)}, u32[]{:S(2)}) collective-permute-start(f32[256,128]{1,0:T(8,128)S(1)} %slice_add_fusion.6.refs_1_), channel_id=1, source_target_pairs={{4,8},{8,4},{12,0},{0,12},{2,6},{6,2},{10,14},{14,10},{5,9},{9,5},... | collective-permute-start | bytes 393224 | tf_op jit(solution)/shard_map/ppermute | solution.py:437
  85.7 4.0 %collective-permute-start.10 = (f32[240,128]{1,0:T(8,128)S(1)}, f32[240,128]{1,0:T(8,128)S(1)}, u32[]{:S(2)}, u32[]{:S(2)}) collective-permute-start(f32[240,128]{1,0:T(8,128)S(1)} %slice_add_fusion.2.refs_0_), channel_id=1, source_target_pairs={{4,8},{8,4},{12,0},{0,12},{2,6},{6,2},{10,14},{14,10},{5,9},{9,5},... | collective-permute-start | bytes 368648 | tf_op jit(solution)/shard_map/ppermute | solution.py:437
  89.9 4.0 %collective-permute-start.12 = (f32[496,128]{1,0:T(8,128)S(1)}, f32[496,128]{1,0:T(8,128)S(1)}, u32[]{:S(2)}, u32[]{:S(2)}) collective-permute-start(f32[496,128]{1,0:T(8,128)S(1)} %get-tuple-element.94.dual_ref.refs_5_), channel_id=1, source_target_pairs={{0,2},{2,0},{1,3},{3,1},{4,6},{6,4},{5,7},{7,5},{8,10},{10,8},{9,1... | collective-permute-start | bytes 761864 | tf_op jit(solution)/shard_map/ppermute | solution.py:494
  122.3 4.2 %collective-permute-start.13 = (f32[496,128]{1,0:T(8,128)S(1)}, f32[496,128]{1,0:T(8,128)S(1)}, u32[]{:S(2)}, u32[]{:S(2)}) collective-permute-start(f32[496,128]{1,0:T(8,128)S(1)} %unit_flows.9), channel_id=1, source_target_pairs={{0,2},{2,0},{1,3},{3,1},{4,6},{6,4},{5,7},{7,5},{8,10},{10,8},{9,1... | collective-permute-start | bytes 761864 | tf_op jit(solution)/shard_map/ppermute | solution.py:468
  126.5 5.3 %collective-permute-start.16 = (f32[256,128]{1,0:T(8,128)S(1)}, f32[256,128]{1,0:T(8,128)S(1)}, u32[]{:S(2)}, u32[]{:S(2)}) collective-permute-start(f32[256,128]{1,0:T(8,128)S(1)} %slice.29), channel_id=1, source_target_pairs={{0,4},{4,0},{8,12},{12,8},{6,10},{10,6},{14,2},{2,14},{1,5},{5,1},... | collective-permute-start | bytes 393224 | tf_op jit(solution)/shard_map/ppermute | solution.py:437
  128.4 5.3 %collective-permute-start.14 = (f32[240,128]{1,0:T(8,128)S(1)}, f32[240,128]{1,0:T(8,128)S(1)}, u32[]{:S(2)}, u32[]{:S(2)}) collective-permute-start(f32[240,128]{1,0:T(8,128)S(1)} %slice.28), channel_id=1, source_target_pairs={{0,4},{4,0},{8,12},{12,8},{6,10},{10,6},{14,2},{2,14},{1,5},{5,1},... | collective-permute-start | bytes 368648 | tf_op jit(solution)/shard_map/ppermute | solution.py:437
  129.4 4.3 %collective-permute-start.15 = (f32[32,128]{1,0:T(8,128)S(1)}, f32[32,128]{1,0:T(8,128)S(1)}, u32[]{:S(2)}, u32[]{:S(2)}) collective-permute-start(f32[32,128]{1,0:T(8,128)S(1)} %get-tuple-element.100.own_ref.old_ref), channel_id=1, source_target_pairs={{0,1},{1,0},{2,3},{3,2},{4,5},{5,4},{6,7},{7,6},{8,9},{9,8},{10,11... | collective-permute-start | bytes 49160 | tf_op jit(solution)/shard_map/ppermute | solution.py:474
  131.9 3.9 %collective-permute-start.18 = (f32[256,128]{1,0:T(8,128)S(1)}, f32[256,128]{1,0:T(8,128)S(1)}, u32[]{:S(2)}, u32[]{:S(2)}) collective-permute-start(f32[256,128]{1,0:T(8,128)S(1)} %slice_add_fusion.5.refs_1_), channel_id=1, source_target_pairs={{4,8},{8,4},{12,0},{0,12},{2,6},{6,2},{10,14},{14,10},{5,9},{9,5},... | collective-permute-start | bytes 393224 | tf_op jit(solution)/shard_map/ppermute | solution.py:437
  133.7 4.1 %collective-permute-start.17 = (f32[240,128]{1,0:T(8,128)S(1)}, f32[240,128]{1,0:T(8,128)S(1)}, u32[]{:S(2)}, u32[]{:S(2)}) collective-permute-start(f32[240,128]{1,0:T(8,128)S(1)} %slice_add_fusion.1.refs_0_), channel_id=1, source_target_pairs={{4,8},{8,4},{12,0},{0,12},{2,6},{6,2},{10,14},{14,10},{5,9},{9,5},... | collective-permute-start | bytes 368648 | tf_op jit(solution)/shard_map/ppermute | solution.py:437
  170.9 4.2 %collective-permute-start.20 = (f32[496,128]{1,0:T(8,128)S(1)}, f32[496,128]{1,0:T(8,128)S(1)}, u32[]{:S(2)}, u32[]{:S(2)}) collective-permute-start(f32[496,128]{1,0:T(8,128)S(1)} %unit_flows.11), channel_id=1, source_target_pairs={{0,2},{2,0},{1,3},{3,1},{4,6},{6,4},{5,7},{7,5},{8,10},{10,8},{9,1... | collective-permute-start | bytes 761864 | tf_op jit(solution)/shard_map/ppermute | solution.py:468
  175.2 5.1 %collective-permute-start.22 = (f32[256,128]{1,0:T(8,128)S(1)}, f32[256,128]{1,0:T(8,128)S(1)}, u32[]{:S(2)}, u32[]{:S(2)}) collective-permute-start(f32[256,128]{1,0:T(8,128)S(1)} %slice.33), channel_id=1, source_target_pairs={{0,4},{4,0},{8,12},{12,8},{6,10},{10,6},{14,2},{2,14},{1,5},{5,1},... | collective-permute-start | bytes 393224 | tf_op jit(solution)/shard_map/ppermute | solution.py:437
  177.0 5.0 %collective-permute-start.21 = (f32[240,128]{1,0:T(8,128)S(1)}, f32[240,128]{1,0:T(8,128)S(1)}, u32[]{:S(2)}, u32[]{:S(2)}) collective-permute-start(f32[240,128]{1,0:T(8,128)S(1)} %slice.32), channel_id=1, source_target_pairs={{0,4},{4,0},{8,12},{12,8},{6,10},{10,6},{14,2},{2,14},{1,5},{5,1},... | collective-permute-start | bytes 368648 | tf_op jit(solution)/shard_map/ppermute | solution.py:437
  180.3 5.8 %collective-permute-start.24 = (f32[256,128]{1,0:T(8,128)S(1)}, f32[256,128]{1,0:T(8,128)S(1)}, u32[]{:S(2)}, u32[]{:S(2)}) collective-permute-start(f32[256,128]{1,0:T(8,128)S(1)} %slice_add_fusion.4.refs_1_), channel_id=1, source_target_pairs={{4,8},{8,4},{12,0},{0,12},{2,6},{6,2},{10,14},{14,10},{5,9},{9,5},... | collective-permute-start | bytes 393224 | tf_op jit(solution)/shard_map/ppermute | solution.py:437
  182.0 4.1 %collective-permute-start.23 = (f32[240,128]{1,0:T(8,128)S(1)}, f32[240,128]{1,0:T(8,128)S(1)}, u32[]{:S(2)}, u32[]{:S(2)}) collective-permute-start(f32[240,128]{1,0:T(8,128)S(1)} %slice_add_fusion.refs_0_), channel_id=1, source_target_pairs={{4,8},{8,4},{12,0},{0,12},{2,6},{6,2},{10,14},{14,10},{5,9},{9,5},... | collective-permute-start | bytes 368648 | tf_op jit(solution)/shard_map/ppermute | solution.py:437
  186.5 4.0 %collective-permute-start.25 = (f32[496,128]{1,0:T(8,128)S(1)}, f32[496,128]{1,0:T(8,128)S(1)}, u32[]{:S(2)}, u32[]{:S(2)}) collective-permute-start(f32[496,128]{1,0:T(8,128)S(1)} %dual_step.7.mine_ref), channel_id=1, source_target_pairs={{0,2},{2,0},{1,3},{3,1},{4,6},{6,4},{5,7},{7,5},{8,10},{10,8},{9,1... | collective-permute-start | bytes 761864 | tf_op jit(solution)/shard_map/ppermute | solution.py:490
  (5 other events, 18.2 us)

commit v5 on v4

--- a/solution.py
+++ b/solution.py
@@ -22,9 +22,8 @@
 LINES_DEV = 960
 ROWS = 1024
 HALF = 496
-BLOCK = 256
-PART = 248
-KEPT = 400
+BLOCK = 128
+KEPT = 320
 CHUNKS = ((0, 240), (240, HALF))
 BF16 = jnp.bfloat16
 F32 = jnp.float32
@@ -133,14 +132,14 @@
         pair_ref[:, :128] = high
         pair_ref[:, 128:] = low
 
-    for start in range(0, KEPT, PART):
-        count = min(PART, KEPT - start)
-
-        @pl.when(step == start // PART)
+    for start in range(0, KEPT, BLOCK):
+        count = min(BLOCK, KEPT - start)
+
+        @pl.when(step == start // BLOCK)
         def _(start=start, count=count):
             kept_ref[start : start + count, :] = ptdf_ref[:count, :]
 
-    rows = row_index(ptdf_ref.shape, step * PART)
+    rows = row_index(ptdf_ref.shape, step * BLOCK)
     ptdf = jnp.where(rows < LINES_DEV, ptdf_ref[...], jnp.where(rows == LINES_DEV, 1.0, 0.0))
     high, low = halves(ptdf)
     both = dot(high, pair_ref[...])
@@ -151,17 +150,17 @@
     buses = ptdf.shape[1]
     return pl.pallas_call(
         load_kernel,
-        grid=(2 * HALF // PART,),
+        grid=(ROWS // BLOCK,),
         in_specs=[
-            pl.BlockSpec((PART, buses), lambda i: (i, 0)),
+            pl.BlockSpec((BLOCK, buses), lambda i: (i, 0)),
             pl.BlockSpec((buses, 128), lambda i: (0, 0)),
         ],
         out_specs=[
-            pl.BlockSpec((PART, 128), lambda i: (i, 0)),
+            pl.BlockSpec((BLOCK, 128), lambda i: (i, 0)),
             pl.BlockSpec((KEPT, buses), lambda i: (0, 0)),
         ],
         out_shape=[
-            jax.ShapeDtypeStruct((2 * HALF, 128), F32),
+            jax.ShapeDtypeStruct((ROWS, 128), F32),
             jax.ShapeDtypeStruct((KEPT, buses), F32),
         ],
         scratch_shapes=[pltpu.VMEM((buses, 256), BF16)],
@@ -172,12 +171,10 @@
 
 
 def first_kernel(
-    core_ref, ptdf_in, load_in, kept_ref, unit_ref, mine_ref, other_ref, rest_ref, load_ref, flow_ref, arrived
+    core_ref, ptdf_in, load_ref, kept_ref, unit_ref, mine_ref, other_ref, rest_ref, flow_ref, arrived
 ):
-    load = pltpu.make_async_copy(load_in, load_ref, arrived.at[0])
-    load.start()
     rest_rows = ptdf_in.at[pl.ds(KEPT, LINES_DEV - KEPT), :]
-    copy = pltpu.make_async_copy(rest_rows, rest_ref, arrived.at[1])
+    copy = pltpu.make_async_copy(rest_rows, rest_ref, arrived)
     copy.start()
     peers, buses = unit_ref.shape[0], ptdf_in.shape[1]
     span, units = buses // peers, 32
@@ -191,11 +188,10 @@
     injection = jnp.concatenate(
         [jnp.sum(tile, axis=0, keepdims=True) for tile in tiles], axis=1
     )
-    load.wait()
     flow_ref[:KEPT, :] = jnp.sum(kept_ref[...] * injection, axis=1, keepdims=True) - load_ref[:KEPT, :]
     total = jnp.sum(injection, axis=1, keepdims=True)
     end = row_index((2 * HALF - LINES_DEV, 128), LINES_DEV)
-    flow_ref[LINES_DEV:, :] = jnp.where(end == LINES_DEV, total, 0.0) - load_ref[LINES_DEV:, :]
+    flow_ref[LINES_DEV:, :] = jnp.where(end == LINES_DEV, total, 0.0) - load_ref[LINES_DEV : 2 * HALF, :]
     copy.wait()
     rest = jnp.sum(rest_ref[...] * injection, axis=1, keepdims=True)
     flow_ref[KEPT:LINES_DEV, :] = rest - load_ref[KEPT:LINES_DEV, :]
@@ -208,14 +204,13 @@
     half = jax.ShapeDtypeStruct((HALF, 128), F32)
     return pl.pallas_call(
         first_kernel,
-        in_specs=[SMEM] + [pl.BlockSpec(memory_space=pltpu.HBM)] * 2 + [VMEM, VMEM],
+        in_specs=[SMEM, pl.BlockSpec(memory_space=pltpu.HBM)] + [VMEM] * 3,
         out_specs=[VMEM, VMEM],
         out_shape=[half, half],
         scratch_shapes=[
             pltpu.VMEM((LINES_DEV - KEPT, ptdf.shape[1]), F32),
             pltpu.VMEM((2 * HALF, 128), F32),
-            pltpu.VMEM((2 * HALF, 128), F32),
-            pltpu.SemaphoreType.DMA((2,)),
+            pltpu.SemaphoreType.DMA(()),
         ],
         compiler_params=params(24),
         cost_estimate=cost_of(2 * ROWS * ptdf.shape[1], 4 * ROWS * ptdf.shape[1]),
@@ -223,17 +218,18 @@
     )(
         core,
         pltpu.with_memory_space_constraint(ptdf, pltpu.HBM),
-        pltpu.with_memory_space_constraint(load, pltpu.HBM),
+        load,
         kept,
         unit_rows,
     )
 
 
-def columns_kernel(part, ptdf_ref, unit_ref, out_ref, pick_ref):
+def columns_kernel(first, ptdf_ref, unit_ref, *refs):
+    high_ref, low_ref, pick_ref = refs[-3:]
     step = pl.program_id(0)
     peers = unit_ref.shape[0]
     span = ptdf_ref.shape[1] // 2
-    units = out_ref.shape[1] // 2
+    units = high_ref.shape[1] // 2
     local = units * 2 // peers
 
     @pl.when(step == 0)
@@ -245,32 +241,40 @@
             pick = jnp.where(index == spots, 1.0, 0.0).astype(BF16)
             pick_ref[group, place * local : (place + 1) * local, :] = pick
 
-    rows = row_index((BLOCK, units), step * BLOCK)
-    inside = row_index((BLOCK, span), step * BLOCK) < LINES_DEV
+    rows = row_index((BLOCK, units), (first + step) * BLOCK)
+    inside = row_index((BLOCK, span), (first + step) * BLOCK) < LINES_DEV
     for group in range(2):
         ptdf = jnp.where(inside, ptdf_ref[:, group * span : (group + 1) * span], 0.0)
-        value = dot(halves(ptdf)[part], pick_ref[group], ((1,), (1,)))
-        if part == 0:
-            value = jnp.where(rows == LINES_DEV, 1.0, value)
-        out_ref[:, group * units : (group + 1) * units] = value.astype(BF16)
-
-
-def unit_columns(part, ptdf, unit_rows, units):
+        high, low = halves(ptdf)
+        pick = pick_ref[group]
+        high = dot(high, pick, ((1,), (1,)))
+        low = dot(low, pick, ((1,), (1,)))
+        where = slice(group * units, (group + 1) * units)
+        high_ref[:, where] = jnp.where(rows == LINES_DEV, 1.0, high).astype(BF16)
+        low_ref[:, where] = low.astype(BF16)
+
+
+def unit_columns(ptdf, unit_rows, units, *begun):
     buses = ptdf.shape[1]
-    return pl.pallas_call(
-        functools.partial(columns_kernel, part),
-        grid=(ROWS // BLOCK,),
+    count = ROWS // BLOCK // 2
+    first = count if begun else 0
+    by_row = pl.BlockSpec((BLOCK, units), lambda i: (first + i, 0))
+    return pl.pallas_call(
+        functools.partial(columns_kernel, first),
+        grid=(count,),
         in_specs=[
-            pl.BlockSpec((BLOCK, buses), lambda i: (i, 0)),
+            pl.BlockSpec((BLOCK, buses), lambda i: (first + i, 0)),
             pl.BlockSpec(unit_rows.shape, lambda i: (0, 0, 0)),
-        ],
-        out_specs=pl.BlockSpec((BLOCK, units), lambda i: (i, 0)),
-        out_shape=jax.ShapeDtypeStruct((ROWS, units), BF16),
+        ]
+        + [pl.BlockSpec(memory_space=pl.ANY)] * len(begun),
+        out_specs=[by_row, by_row],
+        out_shape=[jax.ShapeDtypeStruct((ROWS, units), BF16)] * 2,
         scratch_shapes=[pltpu.VMEM((2, units // 2, buses // 2), BF16)],
+        input_output_aliases={2: 0, 3: 1} if begun else {},
         compiler_params=params(48),
-        cost_estimate=cost_of(2 * ROWS * buses * units // 2, 4 * ROWS * buses),
+        cost_estimate=cost_of(2 * ROWS * buses * units // 2, 2 * ROWS * buses),
         name="unit_columns",
-    )(ptdf, unit_rows)
+    )(pltpu.with_memory_space_constraint(ptdf, pltpu.HBM), unit_rows, *begun)
 
 
 def flow_kernel(place_ref, high_ref, low_ref, extrap_ref, flow_ref):
@@ -467,24 +471,24 @@
         last = iteration == ITERS - 1
         total = mine + lax.ppermute(other, "c", SWAP)
         if iteration == 0:
-            total, tied, rows = lax.optimization_barrier((total, ptdf, unit_rows))
-            high = unit_columns(0, tied, rows, line_count * local)
+            ramp, store, state = state_step(place, extrap, far, ramp, store, table)
+            total, tied, rows, state = lax.optimization_barrier((total, ptdf, unit_rows, state))
+            high, low = unit_columns(tied, rows, line_count * local)
         elif not last:
             total, tied = lax.optimization_barrier((total, extrap))
             far = lax.ppermute(tied, "t", SWAP)
         lefts = [total[start:stop] for start, stop in CHUNKS]
         lefts = [left + along_y(left, (NEAR, FAR)) for left in lefts]
         if iteration == 0:
-            lefts[1], high = lax.optimization_barrier((lefts[1], high))
-            lefts[0], tied, rows = lax.optimization_barrier((lefts[0], tied, rows))
-            low = unit_columns(1, tied, rows, line_count * local)
+            lefts[0], high, low = lax.optimization_barrier((lefts[0], high, low))
+            high, low = unit_columns(tied, rows, line_count * local, high, low)
         elif not last:
             lefts[0], far = lax.optimization_barrier((lefts[0], far))
-        if not last:
+        if 0 < iteration < ITERS - 1:
             ramp, store, state = state_step(place, extrap, far, ramp, store, table)
         rights = [along_y(left, (FAR, NEAR)) for left in lefts]
         if iteration == 0:
-            rights[-1], low = lax.optimization_barrier((rights[-1], low))
+            rights[-1], high, low = lax.optimization_barrier((rights[-1], high, low))
         if last:
             (dual,) = dual_step(lefts, rights, flow, dual, steps, limits, 1)
             return gen, joined(core, dual, lax.ppermute(dual, "c", SWAP))

time: 192 us -> 193 us (level)
  waiting for transfers between devices: 26.9 us -> 24.1 us
  Pallas kernels: 28.3 us -> 30.6 us
    pallas_call x4, Pallas kernels: 16.4 us -> 18.6 us  [the longest x2 9.03 us: unit_columns(): pl.pallas_call(functools.partial(columns_kernel, first), grid=(count,), i...]
  transfers between devices with their start and end apart: 27 -> 27, of which waited for: 19 -> 21; matrix products, arithmetic and copies ran while one was open for 0% -> 0% of each run, Pallas kernels for 10% -> 11%
where the time goes in v5:
time: 193 us; the launch traced here: 192 us
  blocking collectives  84.5 us (44%)
  starting transfers between devices  51.3 us (27%)
  Pallas kernels  30.6 us (16%)
  waiting for transfers between devices  24.1 us (12%)
    all_to_all x3, blocking collectives, on_device(): prices = lax.all_to_all(prices, LINE, 0, 0, tiled=True)  44.5 us
    all_to_all x3, blocking collectives, on_device(): lax.all_to_all(copies, LINE, 0, 0, tiled=True).reshape(-1, hour_dev)  40 us
    ppermute x16, waiting for transfers between devices, along_y(): return lax.ppermute(value, BUS, pairs)  16.6 us
    ppermute x16, starting transfers between devices, along_y(): return lax.ppermute(value, BUS, pairs)  13.4 us
    ppermute x4, starting transfers between devices, on_device(): total = mine + lax.ppermute(other, 'c', SWAP)  11.4 us
    all_to_all x1, starting transfers between devices, on_device(): unit_rows = lax.all_to_all(copies, LINE, 0, 0, tiled=True)  10 us
    pallas_call x2, Pallas kernels, unit_columns(): pl.pallas_call(functools.partial(columns_kernel, first), grid=(count,), i...  9.03 us
    ppermute x3, starting transfers between devices, on_device(): lax.ppermute(dual, 'c', SWAP)  8.75 us
  transfers between devices with their start and end apart: 27, of which 21 were waited for; matrix products, arithmetic and copies ran while one was open for 0% of the time, Pallas kernels for 11%

profile of v5, /device:TPU:1, one launch (start us, length us, event | category | flops | bytes accessed | tf_op | source)
XLA Modules:
  0.0 192.2 jit_solution(13210994562386162072)
XLA Ops:
  2.1 10.0 %all-to-all-start = ((f32[16,8,128]{2,1,0:T(8,128)}), f32[16,8,128]{2,1,0:T(8,128)S(1)}, u32[]{:S(2)}, u32[]{:S(2)}) async-start(f32[16,8,128]{2,1,0:T(8,128)} %get-tuple-element.64), calls=%async_computation | async-start | bytes 131072 | tf_op jit(solution)/shard_map/all_to_all | solution.py:454
  12.2 7.0 %load_flows.1 = (f32[1024,128]{1,0:T(8,128)S(1)}, f32[320,1536]{1,0:T(8,128)S(1)}) custom-call(f32[960,1536]{1,0:T(8,128)} %ptdf_ref.3, f32[1536,128]{1,0:T(8,128)} %load_ref.1), custom_call_target="tpu_custom_call" | custom-call | flops 1207959552 | bytes 6291456 | tf_op jit(solution)/shard_map/load_flows/pallas_call | solution.py:151
  20.1 2.6 %first_flows.1 = (f32[496,128]{1,0:T(8,128)S(1)}, f32[496,128]{1,0:T(8,128)S(1)}) custom-call(s32[1]{0:T(128)} %bitcast.core_ref.place_ref, f32[960,1536]{1,0:T(8,128)} %ptdf_ref.3, f32[1024,128]{1,0:T(8,128)S(1)} %get-tuple-element.62.load_ref, f32[320,1536]{1,0:T(8,128)S(1)} %get-tuple-element.63.kept_ref, f32[16,8,128]{2,1,0:T(8,128)S(1)} %all-to-all-done.unit_ref), custom_call_target="tpu_custom_call" | custom-call | flops 3145728 | bytes 6291456 | tf_op jit(solution)/shard_map/first_flows/pallas_call | solution.py:205
  22.7 2.2 %collective-permute-start = (f32[496,128]{1,0:T(8,128)S(1)}, f32[496,128]{1,0:T(8,128)S(1)}, u32[]{:S(2)}, u32[]{:S(2)}) collective-permute-start(f32[496,128]{1,0:T(8,128)S(1)} %get-tuple-element.66), channel_id=1, source_target_pairs={{0,2},{2,0},{1,3},{3,1},{4,6},{6,4},{5,7},{7,5},{8,10},{10,8},{9,1... | collective-permute-start | bytes 761864 | tf_op jit(solution)/shard_map/ppermute | solution.py:472
  26.1 2.8 %collective-permute-start.3 = (f32[240,128]{1,0:T(8,128)S(1)}, f32[240,128]{1,0:T(8,128)S(1)}, u32[]{:S(2)}, u32[]{:S(2)}) collective-permute-start(f32[240,128]{1,0:T(8,128)S(1)} %slice.25), channel_id=1, source_target_pairs={{0,4},{4,0},{8,12},{12,8},{6,10},{10,6},{14,2},{2,14},{1,5},{5,1},... | collective-permute-start | bytes 368648 | tf_op jit(solution)/shard_map/ppermute | solution.py:441
  29.1 4.5 %unit_columns.2 = (bf16[1024,512]{1,0:T(8,128)(2,1)S(1)}, bf16[1024,512]{1,0:T(8,128)(2,1)S(1)}) custom-call(f32[960,1536]{1,0:T(8,128)} %ptdf_ref.3, f32[16,8,128]{2,1,0:T(8,128)S(1)} %all-to-all-done.unit_ref), custom_call_target="tpu_custom_call" | custom-call | flops 805306368 | bytes 3145728 | tf_op jit(solution)/shard_map/unit_columns/pallas_call | solution.py:262
  35.6 4.5 %unit_columns.3 = (bf16[1024,512]{1,0:T(8,128)(2,1)S(1)}, bf16[1024,512]{1,0:T(8,128)(2,1)S(1)}) custom-call(f32[960,1536]{1,0:T(8,128)} %ptdf_ref.3, f32[16,8,128]{2,1,0:T(8,128)S(1)} %all-to-all-done.unit_ref, bf16[1024,512]{1,0:T(8,128)(2,1)S(1)} %get-tuple-element.75.refs_0_, ...), custom_call_target="tpu_custom_call", output_to_operand_aliasing={{0}: (2, {}), {1}: (3, {})} | custom-call | flops 805306368 | bytes 3145728 | tf_op jit(solution)/shard_map/unit_columns/pallas_call | solution.py:262
  40.4 2.7 %collective-permute-start.5 = (f32[496,128]{1,0:T(8,128)S(1)}, f32[496,128]{1,0:T(8,128)S(1)}, u32[]{:S(2)}, u32[]{:S(2)}) collective-permute-start(f32[496,128]{1,0:T(8,128)S(1)} %get-tuple-element.87.dual_ref.refs_5_), channel_id=1, source_target_pairs={{0,2},{2,0},{1,3},{3,1},{4,6},{6,4},{5,7},{7,5},{8,10},{10,8},{9,1... | collective-permute-start | bytes 761864 | tf_op jit(solution)/shard_map/ppermute | solution.py:498
  44.8 16.6 %all_to_all.35.price_ref = f32[16,32,128]{2,1,0:T(8,128)S(1)} all-to-all(f32[16,32,128]{2,1,0:T(8,128)S(1)} %bitcast.16), channel_id=1, replica_groups=mesh['z'=8,'xl'=2,'y'=4,'c'=2,'t'=2] {'z','xl'}, dimensions={0} | all-to-all | bytes 524288 | tf_op jit(solution)/shard_map/all_to_all | solution.py:500
  61.5 13.4 %all_to_all.36 = f32[16,32,128]{2,1,0:T(8,128)S(1)} all-to-all(f32[16,32,128]{2,1,0:T(8,128)S(1)} %get-tuple-element.89), channel_id=1, replica_groups=mesh['z'=8,'xl'=2,'y'=4,'c'=2,'t'=2] {'z','xl'}, dimensions={0} | all-to-all | bytes 524288 | tf_op jit(solution)/shard_map/all_to_all | solution.py:502
  75.3 3.0 %collective-permute-start.6 = (f32[496,128]{1,0:T(8,128)S(1)}, f32[496,128]{1,0:T(8,128)S(1)}, u32[]{:S(2)}, u32[]{:S(2)}) collective-permute-start(f32[496,128]{1,0:T(8,128)S(1)} %unit_flows.7), channel_id=1, source_target_pairs={{0,2},{2,0},{1,3},{3,1},{4,6},{6,4},{5,7},{7,5},{8,10},{10,8},{9,1... | collective-permute-start | bytes 761864 | tf_op jit(solution)/shard_map/ppermute | solution.py:472
  82.4 2.4 %collective-permute-start.8 = (f32[32,128]{1,0:T(8,128)S(1)}, f32[32,128]{1,0:T(8,128)S(1)}, u32[]{:S(2)}, u32[]{:S(2)}) collective-permute-start(f32[32,128]{1,0:T(8,128)S(1)} %get-tuple-element.92.own_ref.old_ref), channel_id=1, source_target_pairs={{0,1},{1,0},{2,3},{3,2},{4,5},{5,4},{6,7},{7,6},{8,9},{9,8},{10,11... | collective-permute-start | bytes 49160 | tf_op jit(solution)/shard_map/ppermute | solution.py:479
  90.8 3.0 %collective-permute-start.12 = (f32[496,128]{1,0:T(8,128)S(1)}, f32[496,128]{1,0:T(8,128)S(1)}, u32[]{:S(2)}, u32[]{:S(2)}) collective-permute-start(f32[496,128]{1,0:T(8,128)S(1)} %get-tuple-element.102.dual_ref.refs_5_), channel_id=1, source_target_pairs={{0,2},{2,0},{1,3},{3,1},{4,6},{6,4},{5,7},{7,5},{8,10},{10,8},{9,1... | collective-permute-start | bytes 761864 | tf_op jit(solution)/shard_map/ppermute | solution.py:498
  95.5 13.9 %all_to_all.37.price_ref = f32[16,32,128]{2,1,0:T(8,128)S(1)} all-to-all(f32[16,32,128]{2,1,0:T(8,128)S(1)} %bitcast.17), channel_id=1, replica_groups=mesh['z'=8,'xl'=2,'y'=4,'c'=2,'t'=2] {'z','xl'}, dimensions={0} | all-to-all | bytes 524288 | tf_op jit(solution)/shard_map/all_to_all | solution.py:500
  109.6 13.4 %all_to_all.38 = f32[16,32,128]{2,1,0:T(8,128)S(1)} all-to-all(f32[16,32,128]{2,1,0:T(8,128)S(1)} %get-tuple-element.105), channel_id=1, replica_groups=mesh['z'=8,'xl'=2,'y'=4,'c'=2,'t'=2] {'z','xl'}, dimensions={0} | all-to-all | bytes 524288 | tf_op jit(solution)/shard_map/all_to_all | solution.py:502
  123.4 3.1 %collective-permute-start.13 = (f32[496,128]{1,0:T(8,128)S(1)}, f32[496,128]{1,0:T(8,128)S(1)}, u32[]{:S(2)}, u32[]{:S(2)}) collective-permute-start(f32[496,128]{1,0:T(8,128)S(1)} %unit_flows.9), channel_id=1, source_target_pairs={{0,2},{2,0},{1,3},{3,1},{4,6},{6,4},{5,7},{7,5},{8,10},{10,8},{9,1... | collective-permute-start | bytes 761864 | tf_op jit(solution)/shard_map/ppermute | solution.py:472
  130.5 2.4 %collective-permute-start.15 = (f32[32,128]{1,0:T(8,128)S(1)}, f32[32,128]{1,0:T(8,128)S(1)}, u32[]{:S(2)}, u32[]{:S(2)}) collective-permute-start(f32[32,128]{1,0:T(8,128)S(1)} %get-tuple-element.108.own_ref.old_ref), channel_id=1, source_target_pairs={{0,1},{1,0},{2,3},{3,2},{4,5},{5,4},{6,7},{7,6},{8,9},{9,8},{10,11... | collective-permute-start | bytes 49160 | tf_op jit(solution)/shard_map/ppermute | solution.py:479
  138.9 3.0 %collective-permute-start.19 = (f32[496,128]{1,0:T(8,128)S(1)}, f32[496,128]{1,0:T(8,128)S(1)}, u32[]{:S(2)}, u32[]{:S(2)}) collective-permute-start(f32[496,128]{1,0:T(8,128)S(1)} %get-tuple-element.116.dual_ref.refs_5_), channel_id=1, source_target_pairs={{0,2},{2,0},{1,3},{3,1},{4,6},{6,4},{5,7},{7,5},{8,10},{10,8},{9,1... | collective-permute-start | bytes 761864 | tf_op jit(solution)/shard_map/ppermute | solution.py:498
  143.6 13.9 %all_to_all.39.price_ref = f32[16,32,128]{2,1,0:T(8,128)S(1)} all-to-all(f32[16,32,128]{2,1,0:T(8,128)S(1)} %bitcast.18), channel_id=1, replica_groups=mesh['z'=8,'xl'=2,'y'=4,'c'=2,'t'=2] {'z','xl'}, dimensions={0} | all-to-all | bytes 524288 | tf_op jit(solution)/shard_map/all_to_all | solution.py:500
  158.2 13.3 %all_to_all.40 = f32[16,32,128]{2,1,0:T(8,128)S(1)} all-to-all(f32[16,32,128]{2,1,0:T(8,128)S(1)} %get-tuple-element.120), channel_id=1, replica_groups=mesh['z'=8,'xl'=2,'y'=4,'c'=2,'t'=2] {'z','xl'}, dimensions={0} | all-to-all | bytes 524288 | tf_op jit(solution)/shard_map/all_to_all | solution.py:502
  172.0 3.1 %collective-permute-start.20 = (f32[496,128]{1,0:T(8,128)S(1)}, f32[496,128]{1,0:T(8,128)S(1)}, u32[]{:S(2)}, u32[]{:S(2)}) collective-permute-start(f32[496,128]{1,0:T(8,128)S(1)} %unit_flows.11), channel_id=1, source_target_pairs={{0,2},{2,0},{1,3},{3,1},{4,6},{6,4},{5,7},{7,5},{8,10},{10,8},{9,1... | collective-permute-start | bytes 761864 | tf_op jit(solution)/shard_map/ppermute | solution.py:472
  179.1 2.3 %collective-permute-done.22 = f32[256,128]{1,0:T(8,128)S(1)} collective-permute-done((f32[256,128]{1,0:T(8,128)S(1)}, f32[256,128]{1,0:T(8,128)S(1)}, u32[]{:S(2)}, u32[]{:S(2)}) %collective-permute-start.22) | collective-permute-done | bytes 131104 | tf_op jit(solution)/shard_map/ppermute | solution.py:441
  183.1 4.0 %collective-permute-done.23.refs_2_ = f32[240,128]{1,0:T(8,128)S(1)} collective-permute-done((f32[240,128]{1,0:T(8,128)S(1)}, f32[240,128]{1,0:T(8,128)S(1)}, u32[]{:S(2)}, u32[]{:S(2)}) %collective-permute-start.23) | collective-permute-done | bytes 122912 | tf_op jit(solution)/shard_map/ppermute | solution.py:441
  187.4 2.8 %collective-permute-start.25 = (f32[496,128]{1,0:T(8,128)S(1)}, f32[496,128]{1,0:T(8,128)S(1)}, u32[]{:S(2)}, u32[]{:S(2)}) collective-permute-start(f32[496,128]{1,0:T(8,128)S(1)} %dual_step.7.mine_ref), channel_id=1, source_target_pairs={{0,2},{2,0},{1,3},{3,1},{4,6},{6,4},{5,7},{7,5},{8,10},{10,8},{9,1... | collective-permute-start | bytes 761864 | tf_op jit(solution)/shard_map/ppermute | solution.py:494
  (97 shorter events, 41.1 us)
Async XLA Ops:
  2.1 18.0 %all-to-all-start = ((f32[16,8,128]{2,1,0:T(8,128)}), f32[16,8,128]{2,1,0:T(8,128)S(1)}, u32[]{:S(2)}, u32[]{:S(2)}) async-start(f32[16,8,128]{2,1,0:T(8,128)} %get-tuple-element.64), calls=%async_computation | async-start | bytes 131072 | tf_op jit(solution)/shard_map/all_to_all | solution.py:454
  26.1 7.6 %collective-permute-start.3 = (f32[240,128]{1,0:T(8,128)S(1)}, f32[240,128]{1,0:T(8,128)S(1)}, u32[]{:S(2)}, u32[]{:S(2)}) collective-permute-start(f32[240,128]{1,0:T(8,128)S(1)} %slice.25), channel_id=1, source_target_pairs={{0,4},{4,0},{8,12},{12,8},{6,10},{10,6},{14,2},{2,14},{1,5},{5,1},... | collective-permute-start | bytes 368648 | tf_op jit(solution)/shard_map/ppermute | solution.py:441
  29.0 5.1 %collective-permute-start.1 = (f32[256,128]{1,0:T(8,128)S(1)}, f32[256,128]{1,0:T(8,128)S(1)}, u32[]{:S(2)}, u32[]{:S(2)}) collective-permute-start(f32[256,128]{1,0:T(8,128)S(1)} %slice.24), channel_id=1, source_target_pairs={{0,4},{4,0},{8,12},{12,8},{6,10},{10,6},{14,2},{2,14},{1,5},{5,1},... | collective-permute-start | bytes 393224 | tf_op jit(solution)/shard_map/ppermute | solution.py:441
  33.7 6.4 %collective-permute-start.4 = (f32[240,128]{1,0:T(8,128)S(1)}, f32[240,128]{1,0:T(8,128)S(1)}, u32[]{:S(2)}, u32[]{:S(2)}) collective-permute-start(f32[240,128]{1,0:T(8,128)S(1)} %slice_add_fusion.3.refs_0_), channel_id=1, source_target_pairs={{4,8},{8,4},{12,0},{0,12},{2,6},{6,2},{10,14},{14,10},{5,9},{9,5},... | collective-permute-start | bytes 368648 | tf_op jit(solution)/shard_map/ppermute | solution.py:441
  34.1 5.9 %collective-permute-start.2 = (f32[256,128]{1,0:T(8,128)S(1)}, f32[256,128]{1,0:T(8,128)S(1)}, u32[]{:S(2)}, u32[]{:S(2)}) collective-permute-start(f32[256,128]{1,0:T(8,128)S(1)} %slice_add_fusion.7.refs_1_), channel_id=1, source_target_pairs={{4,8},{8,4},{12,0},{0,12},{2,6},{6,2},{10,14},{14,10},{5,9},{9,5},... | collective-permute-start | bytes 393224 | tf_op jit(solution)/shard_map/ppermute | solution.py:441
  75.3 4.2 %collective-permute-start.6 = (f32[496,128]{1,0:T(8,128)S(1)}, f32[496,128]{1,0:T(8,128)S(1)}, u32[]{:S(2)}, u32[]{:S(2)}) collective-permute-start(f32[496,128]{1,0:T(8,128)S(1)} %unit_flows.7), channel_id=1, source_target_pairs={{0,2},{2,0},{1,3},{3,1},{4,6},{6,4},{5,7},{7,5},{8,10},{10,8},{9,1... | collective-permute-start | bytes 761864 | tf_op jit(solution)/shard_map/ppermute | solution.py:472
  79.6 5.3 %collective-permute-start.9 = (f32[256,128]{1,0:T(8,128)S(1)}, f32[256,128]{1,0:T(8,128)S(1)}, u32[]{:S(2)}, u32[]{:S(2)}) collective-permute-start(f32[256,128]{1,0:T(8,128)S(1)} %slice.27), channel_id=1, source_target_pairs={{0,4},{4,0},{8,12},{12,8},{6,10},{10,6},{14,2},{2,14},{1,5},{5,1},... | collective-permute-start | bytes 393224 | tf_op jit(solution)/shard_map/ppermute | solution.py:441
  81.2 5.0 %collective-permute-start.7 = (f32[240,128]{1,0:T(8,128)S(1)}, f32[240,128]{1,0:T(8,128)S(1)}, u32[]{:S(2)}, u32[]{:S(2)}) collective-permute-start(f32[240,128]{1,0:T(8,128)S(1)} %slice.26), channel_id=1, source_target_pairs={{0,4},{4,0},{8,12},{12,8},{6,10},{10,6},{14,2},{2,14},{1,5},{5,1},... | collective-permute-start | bytes 368648 | tf_op jit(solution)/shard_map/ppermute | solution.py:441
  82.4 4.1 %collective-permute-start.8 = (f32[32,128]{1,0:T(8,128)S(1)}, f32[32,128]{1,0:T(8,128)S(1)}, u32[]{:S(2)}, u32[]{:S(2)}) collective-permute-start(f32[32,128]{1,0:T(8,128)S(1)} %get-tuple-element.92.own_ref.old_ref), channel_id=1, source_target_pairs={{0,1},{1,0},{2,3},{3,2},{4,5},{5,4},{6,7},{7,6},{8,9},{9,8},{10,11... | collective-permute-start | bytes 49160 | tf_op jit(solution)/shard_map/ppermute | solution.py:479
  84.9 3.9 %collective-permute-start.11 = (f32[256,128]{1,0:T(8,128)S(1)}, f32[256,128]{1,0:T(8,128)S(1)}, u32[]{:S(2)}, u32[]{:S(2)}) collective-permute-start(f32[256,128]{1,0:T(8,128)S(1)} %slice_add_fusion.6.refs_1_), channel_id=1, source_target_pairs={{4,8},{8,4},{12,0},{0,12},{2,6},{6,2},{10,14},{14,10},{5,9},{9,5},... | collective-permute-start | bytes 393224 | tf_op jit(solution)/shard_map/ppermute | solution.py:441
  86.5 4.0 %collective-permute-start.10 = (f32[240,128]{1,0:T(8,128)S(1)}, f32[240,128]{1,0:T(8,128)S(1)}, u32[]{:S(2)}, u32[]{:S(2)}) collective-permute-start(f32[240,128]{1,0:T(8,128)S(1)} %slice_add_fusion.2.refs_0_), channel_id=1, source_target_pairs={{4,8},{8,4},{12,0},{0,12},{2,6},{6,2},{10,14},{14,10},{5,9},{9,5},... | collective-permute-start | bytes 368648 | tf_op jit(solution)/shard_map/ppermute | solution.py:441
  90.8 4.2 %collective-permute-start.12 = (f32[496,128]{1,0:T(8,128)S(1)}, f32[496,128]{1,0:T(8,128)S(1)}, u32[]{:S(2)}, u32[]{:S(2)}) collective-permute-start(f32[496,128]{1,0:T(8,128)S(1)} %get-tuple-element.102.dual_ref.refs_5_), channel_id=1, source_target_pairs={{0,2},{2,0},{1,3},{3,1},{4,6},{6,4},{5,7},{7,5},{8,10},{10,8},{9,1... | collective-permute-start | bytes 761864 | tf_op jit(solution)/shard_map/ppermute | solution.py:498
  123.4 4.2 %collective-permute-start.13 = (f32[496,128]{1,0:T(8,128)S(1)}, f32[496,128]{1,0:T(8,128)S(1)}, u32[]{:S(2)}, u32[]{:S(2)}) collective-permute-start(f32[496,128]{1,0:T(8,128)S(1)} %unit_flows.9), channel_id=1, source_target_pairs={{0,2},{2,0},{1,3},{3,1},{4,6},{6,4},{5,7},{7,5},{8,10},{10,8},{9,1... | collective-permute-start | bytes 761864 | tf_op jit(solution)/shard_map/ppermute | solution.py:472
  127.6 5.3 %collective-permute-start.16 = (f32[256,128]{1,0:T(8,128)S(1)}, f32[256,128]{1,0:T(8,128)S(1)}, u32[]{:S(2)}, u32[]{:S(2)}) collective-permute-start(f32[256,128]{1,0:T(8,128)S(1)} %slice.29), channel_id=1, source_target_pairs={{0,4},{4,0},{8,12},{12,8},{6,10},{10,6},{14,2},{2,14},{1,5},{5,1},... | collective-permute-start | bytes 393224 | tf_op jit(solution)/shard_map/ppermute | solution.py:441
  129.3 5.0 %collective-permute-start.14 = (f32[240,128]{1,0:T(8,128)S(1)}, f32[240,128]{1,0:T(8,128)S(1)}, u32[]{:S(2)}, u32[]{:S(2)}) collective-permute-start(f32[240,128]{1,0:T(8,128)S(1)} %slice.28), channel_id=1, source_target_pairs={{0,4},{4,0},{8,12},{12,8},{6,10},{10,6},{14,2},{2,14},{1,5},{5,1},... | collective-permute-start | bytes 368648 | tf_op jit(solution)/shard_map/ppermute | solution.py:441
  130.5 4.1 %collective-permute-start.15 = (f32[32,128]{1,0:T(8,128)S(1)}, f32[32,128]{1,0:T(8,128)S(1)}, u32[]{:S(2)}, u32[]{:S(2)}) collective-permute-start(f32[32,128]{1,0:T(8,128)S(1)} %get-tuple-element.108.own_ref.old_ref), channel_id=1, source_target_pairs={{0,1},{1,0},{2,3},{3,2},{4,5},{5,4},{6,7},{7,6},{8,9},{9,8},{10,11... | collective-permute-start | bytes 49160 | tf_op jit(solution)/shard_map/ppermute | solution.py:479
  134.6 4.0 %collective-permute-start.17 = (f32[240,128]{1,0:T(8,128)S(1)}, f32[240,128]{1,0:T(8,128)S(1)}, u32[]{:S(2)}, u32[]{:S(2)}) collective-permute-start(f32[240,128]{1,0:T(8,128)S(1)} %slice_add_fusion.1.refs_0_), channel_id=1, source_target_pairs={{4,8},{8,4},{12,0},{0,12},{2,6},{6,2},{10,14},{14,10},{5,9},{9,5},... | collective-permute-start | bytes 368648 | tf_op jit(solution)/shard_map/ppermute | solution.py:441
  138.9 4.2 %collective-permute-start.19 = (f32[496,128]{1,0:T(8,128)S(1)}, f32[496,128]{1,0:T(8,128)S(1)}, u32[]{:S(2)}, u32[]{:S(2)}) collective-permute-start(f32[496,128]{1,0:T(8,128)S(1)} %get-tuple-element.116.dual_ref.refs_5_), channel_id=1, source_target_pairs={{0,2},{2,0},{1,3},{3,1},{4,6},{6,4},{5,7},{7,5},{8,10},{10,8},{9,1... | collective-permute-start | bytes 761864 | tf_op jit(solution)/shard_map/ppermute | solution.py:498
  172.0 4.2 %collective-permute-start.20 = (f32[496,128]{1,0:T(8,128)S(1)}, f32[496,128]{1,0:T(8,128)S(1)}, u32[]{:S(2)}, u32[]{:S(2)}) collective-permute-start(f32[496,128]{1,0:T(8,128)S(1)} %unit_flows.11), channel_id=1, source_target_pairs={{0,2},{2,0},{1,3},{3,1},{4,6},{6,4},{5,7},{7,5},{8,10},{10,8},{9,1... | collective-permute-start | bytes 761864 | tf_op jit(solution)/shard_map/ppermute | solution.py:472
  176.3 5.1 %collective-permute-start.22 = (f32[256,128]{1,0:T(8,128)S(1)}, f32[256,128]{1,0:T(8,128)S(1)}, u32[]{:S(2)}, u32[]{:S(2)}) collective-permute-start(f32[256,128]{1,0:T(8,128)S(1)} %slice.33), channel_id=1, source_target_pairs={{0,4},{4,0},{8,12},{12,8},{6,10},{10,6},{14,2},{2,14},{1,5},{5,1},... | collective-permute-start | bytes 393224 | tf_op jit(solution)/shard_map/ppermute | solution.py:441
  177.9 5.0 %collective-permute-start.21 = (f32[240,128]{1,0:T(8,128)S(1)}, f32[240,128]{1,0:T(8,128)S(1)}, u32[]{:S(2)}, u32[]{:S(2)}) collective-permute-start(f32[240,128]{1,0:T(8,128)S(1)} %slice.32), channel_id=1, source_target_pairs={{0,4},{4,0},{8,12},{12,8},{6,10},{10,6},{14,2},{2,14},{1,5},{5,1},... | collective-permute-start | bytes 368648 | tf_op jit(solution)/shard_map/ppermute | solution.py:441
  181.4 5.7 %collective-permute-start.24 = (f32[256,128]{1,0:T(8,128)S(1)}, f32[256,128]{1,0:T(8,128)S(1)}, u32[]{:S(2)}, u32[]{:S(2)}) collective-permute-start(f32[256,128]{1,0:T(8,128)S(1)} %slice_add_fusion.4.refs_1_), channel_id=1, source_target_pairs={{4,8},{8,4},{12,0},{0,12},{2,6},{6,2},{10,14},{14,10},{5,9},{9,5},... | collective-permute-start | bytes 393224 | tf_op jit(solution)/shard_map/ppermute | solution.py:441
  183.0 4.1 %collective-permute-start.23 = (f32[240,128]{1,0:T(8,128)S(1)}, f32[240,128]{1,0:T(8,128)S(1)}, u32[]{:S(2)}, u32[]{:S(2)}) collective-permute-start(f32[240,128]{1,0:T(8,128)S(1)} %slice_add_fusion.refs_0_), channel_id=1, source_target_pairs={{4,8},{8,4},{12,0},{0,12},{2,6},{6,2},{10,14},{14,10},{5,9},{9,5},... | collective-permute-start | bytes 368648 | tf_op jit(solution)/shard_map/ppermute | solution.py:441
  187.4 4.0 %collective-permute-start.25 = (f32[496,128]{1,0:T(8,128)S(1)}, f32[496,128]{1,0:T(8,128)S(1)}, u32[]{:S(2)}, u32[]{:S(2)}) collective-permute-start(f32[496,128]{1,0:T(8,128)S(1)} %dual_step.7.mine_ref), channel_id=1, source_target_pairs={{0,2},{2,0},{1,3},{3,1},{4,6},{6,4},{5,7},{7,5},{8,10},{10,8},{9,1... | collective-permute-start | bytes 761864 | tf_op jit(solution)/shard_map/ppermute | solution.py:494
  (6 other events, 69.2 us)

commit v6 on v5

--- a/solution.py
+++ b/solution.py
@@ -22,7 +22,7 @@
 LINES_DEV = 960
 ROWS = 1024
 HALF = 496
-BLOCK = 128
+BLOCK = 512
 KEPT = 320
 CHUNKS = ((0, 240), (240, HALF))
 BF16 = jnp.bfloat16
@@ -123,47 +123,46 @@
     )(place, *(pltpu.with_memory_space_constraint(x, pltpu.HBM) for x in rows))
 
 
-def load_kernel(ptdf_ref, load_ref, flow_ref, kept_ref, pair_ref):
+def load_kernel(ptdf_ref, load_ref, flow_ref, kept_ref):
     step = pl.program_id(0)
+    ptdf, load = ptdf_ref[...], load_ref[...]
+    kept_ref[...] = ptdf[:KEPT]
+    high, low = halves(load)
+    ptdf_high, ptdf_low = halves(ptdf)
+    both = dot(ptdf_high, jnp.concatenate([high, low], axis=1))
+    flow = both[:, :128] + both[:, 128:] + dot(ptdf_low, high)
+    total = jnp.sum(load, axis=0, keepdims=True)
+    end = row_index((2 * HALF - LINES_DEV, 128), LINES_DEV) == LINES_DEV
+    total = jnp.where(end, total, 0.0)
 
     @pl.when(step == 0)
     def _():
-        high, low = halves(load_ref[...])
-        pair_ref[:, :128] = high
-        pair_ref[:, 128:] = low
-
-    for start in range(0, KEPT, BLOCK):
-        count = min(BLOCK, KEPT - start)
-
-        @pl.when(step == start // BLOCK)
-        def _(start=start, count=count):
-            kept_ref[start : start + count, :] = ptdf_ref[:count, :]
-
-    rows = row_index(ptdf_ref.shape, step * BLOCK)
-    ptdf = jnp.where(rows < LINES_DEV, ptdf_ref[...], jnp.where(rows == LINES_DEV, 1.0, 0.0))
-    high, low = halves(ptdf)
-    both = dot(high, pair_ref[...])
-    flow_ref[...] = both[:, :128] + both[:, 128:] + dot(low, pair_ref[:, :128])
+        flow_ref[:LINES_DEV, :] = flow
+        flow_ref[LINES_DEV:, :] = total
+
+    @pl.when(step > 0)
+    def _():
+        flow_ref[:LINES_DEV, :] += flow
+        flow_ref[LINES_DEV:, :] += total
 
 
 def load_flows(ptdf, load):
-    buses = ptdf.shape[1]
+    lines, buses = ptdf.shape
     return pl.pallas_call(
         load_kernel,
-        grid=(ROWS // BLOCK,),
+        grid=(buses // BLOCK,),
         in_specs=[
-            pl.BlockSpec((BLOCK, buses), lambda i: (i, 0)),
-            pl.BlockSpec((buses, 128), lambda i: (0, 0)),
+            pl.BlockSpec((lines, BLOCK), lambda i: (0, i)),
+            pl.BlockSpec((BLOCK, 128), lambda i: (i, 0)),
         ],
         out_specs=[
-            pl.BlockSpec((BLOCK, 128), lambda i: (i, 0)),
-            pl.BlockSpec((KEPT, buses), lambda i: (0, 0)),
+            pl.BlockSpec((2 * HALF, 128), lambda i: (0, 0)),
+            pl.BlockSpec((KEPT, BLOCK), lambda i: (0, i)),
         ],
         out_shape=[
-            jax.ShapeDtypeStruct((ROWS, 128), F32),
+            jax.ShapeDtypeStruct((2 * HALF, 128), F32),
             jax.ShapeDtypeStruct((KEPT, buses), F32),
         ],
-        scratch_shapes=[pltpu.VMEM((buses, 256), BF16)],
         compiler_params=params(40),
         cost_estimate=cost_of(3 * 2 * ROWS * buses * 128, 4 * ROWS * buses),
         name="load_flows",
@@ -191,7 +190,7 @@
     flow_ref[:KEPT, :] = jnp.sum(kept_ref[...] * injection, axis=1, keepdims=True) - load_ref[:KEPT, :]
     total = jnp.sum(injection, axis=1, keepdims=True)
     end = row_index((2 * HALF - LINES_DEV, 128), LINES_DEV)
-    flow_ref[LINES_DEV:, :] = jnp.where(end == LINES_DEV, total, 0.0) - load_ref[LINES_DEV : 2 * HALF, :]
+    flow_ref[LINES_DEV:, :] = jnp.where(end == LINES_DEV, total, 0.0) - load_ref[LINES_DEV:, :]
     copy.wait()
     rest = jnp.sum(rest_ref[...] * injection, axis=1, keepdims=True)
     flow_ref[KEPT:LINES_DEV, :] = rest - load_ref[KEPT:LINES_DEV, :]
@@ -224,55 +223,47 @@
     )
 
 
-def columns_kernel(first, ptdf_ref, unit_ref, *refs):
+def columns_kernel(group, ptdf_ref, unit_ref, *refs):
     high_ref, low_ref, pick_ref = refs[-3:]
     step = pl.program_id(0)
-    peers = unit_ref.shape[0]
-    span = ptdf_ref.shape[1] // 2
-    units = high_ref.shape[1] // 2
-    local = units * 2 // peers
+    units, span = pick_ref.shape
+    peers = unit_ref.shape[0] // 2
+    local = units // peers
 
     @pl.when(step == 0)
     def _():
         for peer in range(peers):
-            group, place = divmod(peer, peers // 2)
-            spots = column(unit_ref[peer][0:1, :local]).astype(jnp.int32)
+            spots = column(unit_ref[group * peers + peer][0:1, :local]).astype(jnp.int32)
             index = lax.broadcasted_iota(jnp.int32, (local, span), 1) + group * span
             pick = jnp.where(index == spots, 1.0, 0.0).astype(BF16)
-            pick_ref[group, place * local : (place + 1) * local, :] = pick
-
-    rows = row_index((BLOCK, units), (first + step) * BLOCK)
-    inside = row_index((BLOCK, span), (first + step) * BLOCK) < LINES_DEV
-    for group in range(2):
-        ptdf = jnp.where(inside, ptdf_ref[:, group * span : (group + 1) * span], 0.0)
-        high, low = halves(ptdf)
-        pick = pick_ref[group]
-        high = dot(high, pick, ((1,), (1,)))
-        low = dot(low, pick, ((1,), (1,)))
-        where = slice(group * units, (group + 1) * units)
-        high_ref[:, where] = jnp.where(rows == LINES_DEV, 1.0, high).astype(BF16)
-        low_ref[:, where] = low.astype(BF16)
+            pick_ref[peer * local : (peer + 1) * local, :] = pick
+
+    inside = row_index((BLOCK, span), step * BLOCK) < LINES_DEV
+    ptdf = jnp.where(inside, ptdf_ref[...], 0.0)
+    both = dot(jnp.concatenate(halves(ptdf), axis=0), pick_ref[...], ((1,), (1,)))
+    rows = row_index((BLOCK, units), step * BLOCK)
+    high_ref[...] = jnp.where(rows == LINES_DEV, 1.0, both[:BLOCK]).astype(BF16)
+    low_ref[...] = both[BLOCK:].astype(BF16)
 
 
 def unit_columns(ptdf, unit_rows, units, *begun):
-    buses = ptdf.shape[1]
-    count = ROWS // BLOCK // 2
-    first = count if begun else 0
-    by_row = pl.BlockSpec((BLOCK, units), lambda i: (first + i, 0))
-    return pl.pallas_call(
-        functools.partial(columns_kernel, first),
-        grid=(count,),
+    span = ptdf.shape[1] // 2
+    group = 1 if begun else 0
+    by_row = pl.BlockSpec((BLOCK, units // 2), lambda i: (i, group))
+    return pl.pallas_call(
+        functools.partial(columns_kernel, group),
+        grid=(ROWS // BLOCK,),
         in_specs=[
-            pl.BlockSpec((BLOCK, buses), lambda i: (first + i, 0)),
+            pl.BlockSpec((BLOCK, span), lambda i: (i, group)),
             pl.BlockSpec(unit_rows.shape, lambda i: (0, 0, 0)),
         ]
         + [pl.BlockSpec(memory_space=pl.ANY)] * len(begun),
         out_specs=[by_row, by_row],
         out_shape=[jax.ShapeDtypeStruct((ROWS, units), BF16)] * 2,
-        scratch_shapes=[pltpu.VMEM((2, units // 2, buses // 2), BF16)],
+        scratch_shapes=[pltpu.VMEM((units // 2, span), BF16)],
         input_output_aliases={2: 0, 3: 1} if begun else {},
-        compiler_params=params(48),
-        cost_estimate=cost_of(2 * ROWS * buses * units // 2, 2 * ROWS * buses),
+        compiler_params=params(40),
+        cost_estimate=cost_of(2 * ROWS * span * units, 4 * ROWS * span),
         name="unit_columns",
     )(pltpu.with_memory_space_constraint(ptdf, pltpu.HBM), unit_rows, *begun)
 

time: 193 us -> 188 us (0.974)
  Pallas kernels: 30.6 us -> 25.2 us
  waiting for transfers between devices: 24.1 us -> 28 us
  blocking collectives: 84.5 us -> 82.2 us
    pallas_call x3, Pallas kernels: 16 us -> 10.6 us  [the longest x2 5.9 us: unit_columns(): pl.pallas_call(functools.partial(columns_kernel, group), grid=(ROWS // BL...]
    all_to_all x3, blocking collectives: 44.5 us -> 42.1 us  [on_device(): prices = lax.all_to_all(prices, LINE, 0, 0, tiled=True)]
    all_to_all x1, waiting for transfers between devices: 0.91 us -> 3.19 us  [on_device(): unit_rows = lax.all_to_all(copies, LINE, 0, 0, tiled=True)]
  transfers between devices with their start and end apart: 27 -> 27, of which waited for: 21 -> 22; matrix products, arithmetic and copies ran while one was open for 0% -> 0% of each run, Pallas kernels for 11% -> 8%
where the time goes in v6:
time: 188 us
  blocking collectives  82.2 us (44%)
  starting transfers between devices  50.7 us (27%)
  waiting for transfers between devices  28 us (15%)
  Pallas kernels  25.2 us (13%)
    all_to_all x3, blocking collectives, on_device(): prices = lax.all_to_all(prices, LINE, 0, 0, tiled=True)  42.1 us
    all_to_all x3, blocking collectives, on_device(): lax.all_to_all(copies, LINE, 0, 0, tiled=True).reshape(-1, hour_dev)  40.1 us
    ppermute x16, waiting for transfers between devices, along_y(): return lax.ppermute(value, BUS, pairs)  17.8 us
    ppermute x16, starting transfers between devices, along_y(): return lax.ppermute(value, BUS, pairs)  12.7 us
    ppermute x4, starting transfers between devices, on_device(): total = mine + lax.ppermute(other, 'c', SWAP)  11.4 us
    all_to_all x1, starting transfers between devices, on_device(): unit_rows = lax.all_to_all(copies, LINE, 0, 0, tiled=True)  10 us
    ppermute x3, starting transfers between devices, on_device(): lax.ppermute(dual, 'c', SWAP)  9.17 us
    pallas_call x2, Pallas kernels, unit_columns(): pl.pallas_call(functools.partial(columns_kernel, group), grid=(ROWS // BL...  5.9 us
  transfers between devices with their start and end apart: 27, of which 22 were waited for; matrix products, arithmetic and copies ran while one was open for 0% of the time, Pallas kernels for 8%

profile of v6, /device:TPU:1, one launch (start us, length us, event | category | flops | bytes accessed | tf_op | source)
XLA Modules:
  0.0 187.8 jit_solution(7200722757854812882)
XLA Ops:
  2.1 10.0 %all-to-all-start = ((f32[16,8,128]{2,1,0:T(8,128)}), f32[16,8,128]{2,1,0:T(8,128)S(1)}, u32[]{:S(2)}, u32[]{:S(2)}) async-start(f32[16,8,128]{2,1,0:T(8,128)} %get-tuple-element.64), calls=%async_computation | async-start | bytes 131072 | tf_op jit(solution)/shard_map/all_to_all | solution.py:445
  12.2 4.7 %load_flows.1 = (f32[992,128]{1,0:T(8,128)S(1)}, f32[320,1536]{1,0:T(8,128)S(1)}) custom-call(f32[960,1536]{1,0:T(8,128)} %ptdf_ref.3, f32[1536,128]{1,0:T(8,128)} %load_ref.1), custom_call_target="tpu_custom_call" | custom-call | flops 1207959552 | bytes 6291456 | tf_op jit(solution)/shard_map/load_flows/pallas_call | solution.py:151
  16.9 3.2 %all-to-all-done.unit_ref = f32[16,8,128]{2,1,0:T(8,128)S(1)} async-done(((f32[16,8,128]{2,1,0:T(8,128)}), f32[16,8,128]{2,1,0:T(8,128)S(1)}, u32[]{:S(2)}, u32[]{:S(2)}) %all-to-all-start) | async-done | bytes 65568 | tf_op jit(solution)/shard_map/all_to_all | solution.py:445
  20.1 2.6 %first_flows.1 = (f32[496,128]{1,0:T(8,128)S(1)}, f32[496,128]{1,0:T(8,128)S(1)}) custom-call(s32[1]{0:T(128)} %bitcast.core_ref.place_ref, f32[960,1536]{1,0:T(8,128)} %ptdf_ref.3, f32[992,128]{1,0:T(8,128)S(1)} %get-tuple-element.62.load_ref, f32[320,1536]{1,0:T(8,128)S(1)} %get-tuple-element.63.kept_ref, f32[16,8,128]{2,1,0:T(8,128)S(1)} %all-to-all-done.unit_ref), custom_call_target="tpu_custom_call" | custom-call | flops 3145728 | bytes 6291456 | tf_op jit(solution)/shard_map/first_flows/pallas_call | solution.py:204
  26.1 2.8 %collective-permute-start.3 = (f32[240,128]{1,0:T(8,128)S(1)}, f32[240,128]{1,0:T(8,128)S(1)}, u32[]{:S(2)}, u32[]{:S(2)}) collective-permute-start(f32[240,128]{1,0:T(8,128)S(1)} %slice.25), channel_id=1, source_target_pairs={{0,4},{4,0},{8,12},{12,8},{6,10},{10,6},{14,2},{2,14},{1,5},{5,1},... | collective-permute-start | bytes 368648 | tf_op jit(solution)/shard_map/ppermute | solution.py:432
  29.1 2.9 %unit_columns.2 = (bf16[1024,512]{1,0:T(8,128)(2,1)S(1)}, bf16[1024,512]{1,0:T(8,128)(2,1)S(1)}) custom-call(f32[960,1536]{1,0:T(8,128)} %ptdf_ref.3, f32[16,8,128]{2,1,0:T(8,128)S(1)} %all-to-all-done.unit_ref), custom_call_target="tpu_custom_call" | custom-call | flops 805306368 | bytes 3145728 | tf_op jit(solution)/shard_map/unit_columns/pallas_call | solution.py:253
  34.5 3.0 %unit_columns.3 = (bf16[1024,512]{1,0:T(8,128)(2,1)S(1)}, bf16[1024,512]{1,0:T(8,128)(2,1)S(1)}) custom-call(f32[960,1536]{1,0:T(8,128)} %ptdf_ref.3, f32[16,8,128]{2,1,0:T(8,128)S(1)} %all-to-all-done.unit_ref, bf16[1024,512]{1,0:T(8,128)(2,1)S(1)} %get-tuple-element.75.refs_0_, ...), custom_call_target="tpu_custom_call", output_to_operand_aliasing={{0}: (2, {}), {1}: (3, {})} | custom-call | flops 805306368 | bytes 3145728 | tf_op jit(solution)/shard_map/unit_columns/pallas_call | solution.py:253
  38.4 3.2 %collective-permute-start.5 = (f32[496,128]{1,0:T(8,128)S(1)}, f32[496,128]{1,0:T(8,128)S(1)}, u32[]{:S(2)}, u32[]{:S(2)}) collective-permute-start(f32[496,128]{1,0:T(8,128)S(1)} %get-tuple-element.87.dual_ref.refs_5_), channel_id=1, source_target_pairs={{0,2},{2,0},{1,3},{3,1},{4,6},{6,4},{5,7},{7,5},{8,10},{10,8},{9,1... | collective-permute-start | bytes 761864 | tf_op jit(solution)/shard_map/ppermute | solution.py:489
  43.2 14.3 %all_to_all.35.price_ref = f32[16,32,128]{2,1,0:T(8,128)S(1)} all-to-all(f32[16,32,128]{2,1,0:T(8,128)S(1)} %bitcast.16), channel_id=1, replica_groups=mesh['z'=8,'xl'=2,'y'=4,'c'=2,'t'=2] {'z','xl'}, dimensions={0} | all-to-all | bytes 524288 | tf_op jit(solution)/shard_map/all_to_all | solution.py:491
  57.6 13.4 %all_to_all.36 = f32[16,32,128]{2,1,0:T(8,128)S(1)} all-to-all(f32[16,32,128]{2,1,0:T(8,128)S(1)} %get-tuple-element.89), channel_id=1, replica_groups=mesh['z'=8,'xl'=2,'y'=4,'c'=2,'t'=2] {'z','xl'}, dimensions={0} | all-to-all | bytes 524288 | tf_op jit(solution)/shard_map/all_to_all | solution.py:493
  71.4 3.0 %collective-permute-start.6 = (f32[496,128]{1,0:T(8,128)S(1)}, f32[496,128]{1,0:T(8,128)S(1)}, u32[]{:S(2)}, u32[]{:S(2)}) collective-permute-start(f32[496,128]{1,0:T(8,128)S(1)} %unit_flows.7), channel_id=1, source_target_pairs={{0,2},{2,0},{1,3},{3,1},{4,6},{6,4},{5,7},{7,5},{8,10},{10,8},{9,1... | collective-permute-start | bytes 761864 | tf_op jit(solution)/shard_map/ppermute | solution.py:463
  78.5 2.4 %collective-permute-start.8 = (f32[32,128]{1,0:T(8,128)S(1)}, f32[32,128]{1,0:T(8,128)S(1)}, u32[]{:S(2)}, u32[]{:S(2)}) collective-permute-start(f32[32,128]{1,0:T(8,128)S(1)} %get-tuple-element.92.own_ref.old_ref), channel_id=1, source_target_pairs={{0,1},{1,0},{2,3},{3,2},{4,5},{5,4},{6,7},{7,6},{8,9},{9,8},{10,11... | collective-permute-start | bytes 49160 | tf_op jit(solution)/shard_map/ppermute | solution.py:470
  87.0 3.0 %collective-permute-start.12 = (f32[496,128]{1,0:T(8,128)S(1)}, f32[496,128]{1,0:T(8,128)S(1)}, u32[]{:S(2)}, u32[]{:S(2)}) collective-permute-start(f32[496,128]{1,0:T(8,128)S(1)} %get-tuple-element.102.dual_ref.refs_5_), channel_id=1, source_target_pairs={{0,2},{2,0},{1,3},{3,1},{4,6},{6,4},{5,7},{7,5},{8,10},{10,8},{9,1... | collective-permute-start | bytes 761864 | tf_op jit(solution)/shard_map/ppermute | solution.py:489
  91.7 13.9 %all_to_all.37.price_ref = f32[16,32,128]{2,1,0:T(8,128)S(1)} all-to-all(f32[16,32,128]{2,1,0:T(8,128)S(1)} %bitcast.17), channel_id=1, replica_groups=mesh['z'=8,'xl'=2,'y'=4,'c'=2,'t'=2] {'z','xl'}, dimensions={0} | all-to-all | bytes 524288 | tf_op jit(solution)/shard_map/all_to_all | solution.py:491
  105.7 13.4 %all_to_all.38 = f32[16,32,128]{2,1,0:T(8,128)S(1)} all-to-all(f32[16,32,128]{2,1,0:T(8,128)S(1)} %get-tuple-element.105), channel_id=1, replica_groups=mesh['z'=8,'xl'=2,'y'=4,'c'=2,'t'=2] {'z','xl'}, dimensions={0} | all-to-all | bytes 524288 | tf_op jit(solution)/shard_map/all_to_all | solution.py:493
  119.5 3.1 %collective-permute-start.13 = (f32[496,128]{1,0:T(8,128)S(1)}, f32[496,128]{1,0:T(8,128)S(1)}, u32[]{:S(2)}, u32[]{:S(2)}) collective-permute-start(f32[496,128]{1,0:T(8,128)S(1)} %unit_flows.9), channel_id=1, source_target_pairs={{0,2},{2,0},{1,3},{3,1},{4,6},{6,4},{5,7},{7,5},{8,10},{10,8},{9,1... | collective-permute-start | bytes 761864 | tf_op jit(solution)/shard_map/ppermute | solution.py:463
  126.6 2.4 %collective-permute-start.15 = (f32[32,128]{1,0:T(8,128)S(1)}, f32[32,128]{1,0:T(8,128)S(1)}, u32[]{:S(2)}, u32[]{:S(2)}) collective-permute-start(f32[32,128]{1,0:T(8,128)S(1)} %get-tuple-element.108.own_ref.old_ref), channel_id=1, source_target_pairs={{0,1},{1,0},{2,3},{3,2},{4,5},{5,4},{6,7},{7,6},{8,9},{9,8},{10,11... | collective-permute-start | bytes 49160 | tf_op jit(solution)/shard_map/ppermute | solution.py:470
  135.0 3.0 %collective-permute-start.19 = (f32[496,128]{1,0:T(8,128)S(1)}, f32[496,128]{1,0:T(8,128)S(1)}, u32[]{:S(2)}, u32[]{:S(2)}) collective-permute-start(f32[496,128]{1,0:T(8,128)S(1)} %get-tuple-element.116.dual_ref.refs_5_), channel_id=1, source_target_pairs={{0,2},{2,0},{1,3},{3,1},{4,6},{6,4},{5,7},{7,5},{8,10},{10,8},{9,1... | collective-permute-start | bytes 761864 | tf_op jit(solution)/shard_map/ppermute | solution.py:489
  139.7 13.9 %all_to_all.39.price_ref = f32[16,32,128]{2,1,0:T(8,128)S(1)} all-to-all(f32[16,32,128]{2,1,0:T(8,128)S(1)} %bitcast.18), channel_id=1, replica_groups=mesh['z'=8,'xl'=2,'y'=4,'c'=2,'t'=2] {'z','xl'}, dimensions={0} | all-to-all | bytes 524288 | tf_op jit(solution)/shard_map/all_to_all | solution.py:491
  154.4 13.3 %all_to_all.40 = f32[16,32,128]{2,1,0:T(8,128)S(1)} all-to-all(f32[16,32,128]{2,1,0:T(8,128)S(1)} %get-tuple-element.120), channel_id=1, replica_groups=mesh['z'=8,'xl'=2,'y'=4,'c'=2,'t'=2] {'z','xl'}, dimensions={0} | all-to-all | bytes 524288 | tf_op jit(solution)/shard_map/all_to_all | solution.py:493
  168.1 3.1 %collective-permute-start.20 = (f32[496,128]{1,0:T(8,128)S(1)}, f32[496,128]{1,0:T(8,128)S(1)}, u32[]{:S(2)}, u32[]{:S(2)}) collective-permute-start(f32[496,128]{1,0:T(8,128)S(1)} %unit_flows.11), channel_id=1, source_target_pairs={{0,2},{2,0},{1,3},{3,1},{4,6},{6,4},{5,7},{7,5},{8,10},{10,8},{9,1... | collective-permute-start | bytes 761864 | tf_op jit(solution)/shard_map/ppermute | solution.py:463
  175.3 2.3 %collective-permute-done.22 = f32[256,128]{1,0:T(8,128)S(1)} collective-permute-done((f32[256,128]{1,0:T(8,128)S(1)}, f32[256,128]{1,0:T(8,128)S(1)}, u32[]{:S(2)}, u32[]{:S(2)}) %collective-permute-start.22) | collective-permute-done | bytes 131104 | tf_op jit(solution)/shard_map/ppermute | solution.py:432
  179.2 3.9 %collective-permute-done.23.refs_2_ = f32[240,128]{1,0:T(8,128)S(1)} collective-permute-done((f32[240,128]{1,0:T(8,128)S(1)}, f32[240,128]{1,0:T(8,128)S(1)}, u32[]{:S(2)}, u32[]{:S(2)}) %collective-permute-start.23) | collective-permute-done | bytes 122912 | tf_op jit(solution)/shard_map/ppermute | solution.py:432
  183.4 2.5 %collective-permute-start.25 = (f32[496,128]{1,0:T(8,128)S(1)}, f32[496,128]{1,0:T(8,128)S(1)}, u32[]{:S(2)}, u32[]{:S(2)}) collective-permute-start(f32[496,128]{1,0:T(8,128)S(1)} %dual_step.7.mine_ref), channel_id=1, source_target_pairs={{0,2},{2,0},{1,3},{3,1},{4,6},{6,4},{5,7},{7,5},{8,10},{10,8},{9,1... | collective-permute-start | bytes 761864 | tf_op jit(solution)/shard_map/ppermute | solution.py:485
  (97 shorter events, 43.5 us)
Async XLA Ops:
  2.1 18.0 %all-to-all-start = ((f32[16,8,128]{2,1,0:T(8,128)}), f32[16,8,128]{2,1,0:T(8,128)S(1)}, u32[]{:S(2)}, u32[]{:S(2)}) async-start(f32[16,8,128]{2,1,0:T(8,128)} %get-tuple-element.64), calls=%async_computation | async-start | bytes 131072 | tf_op jit(solution)/shard_map/all_to_all | solution.py:445
  26.1 6.0 %collective-permute-start.3 = (f32[240,128]{1,0:T(8,128)S(1)}, f32[240,128]{1,0:T(8,128)S(1)}, u32[]{:S(2)}, u32[]{:S(2)}) collective-permute-start(f32[240,128]{1,0:T(8,128)S(1)} %slice.25), channel_id=1, source_target_pairs={{0,4},{4,0},{8,12},{12,8},{6,10},{10,6},{14,2},{2,14},{1,5},{5,1},... | collective-permute-start | bytes 368648 | tf_op jit(solution)/shard_map/ppermute | solution.py:432
  29.0 5.1 %collective-permute-start.1 = (f32[256,128]{1,0:T(8,128)S(1)}, f32[256,128]{1,0:T(8,128)S(1)}, u32[]{:S(2)}, u32[]{:S(2)}) collective-permute-start(f32[256,128]{1,0:T(8,128)S(1)} %slice.24), channel_id=1, source_target_pairs={{0,4},{4,0},{8,12},{12,8},{6,10},{10,6},{14,2},{2,14},{1,5},{5,1},... | collective-permute-start | bytes 393224 | tf_op jit(solution)/shard_map/ppermute | solution.py:432
  32.1 6.0 %collective-permute-start.4 = (f32[240,128]{1,0:T(8,128)S(1)}, f32[240,128]{1,0:T(8,128)S(1)}, u32[]{:S(2)}, u32[]{:S(2)}) collective-permute-start(f32[240,128]{1,0:T(8,128)S(1)} %slice_add_fusion.3.refs_0_), channel_id=1, source_target_pairs={{4,8},{8,4},{12,0},{0,12},{2,6},{6,2},{10,14},{14,10},{5,9},{9,5},... | collective-permute-start | bytes 368648 | tf_op jit(solution)/shard_map/ppermute | solution.py:432
  34.1 3.9 %collective-permute-start.2 = (f32[256,128]{1,0:T(8,128)S(1)}, f32[256,128]{1,0:T(8,128)S(1)}, u32[]{:S(2)}, u32[]{:S(2)}) collective-permute-start(f32[256,128]{1,0:T(8,128)S(1)} %slice_add_fusion.7.refs_1_), channel_id=1, source_target_pairs={{4,8},{8,4},{12,0},{0,12},{2,6},{6,2},{10,14},{14,10},{5,9},{9,5},... | collective-permute-start | bytes 393224 | tf_op jit(solution)/shard_map/ppermute | solution.py:432
  38.4 4.3 %collective-permute-start.5 = (f32[496,128]{1,0:T(8,128)S(1)}, f32[496,128]{1,0:T(8,128)S(1)}, u32[]{:S(2)}, u32[]{:S(2)}) collective-permute-start(f32[496,128]{1,0:T(8,128)S(1)} %get-tuple-element.87.dual_ref.refs_5_), channel_id=1, source_target_pairs={{0,2},{2,0},{1,3},{3,1},{4,6},{6,4},{5,7},{7,5},{8,10},{10,8},{9,1... | collective-permute-start | bytes 761864 | tf_op jit(solution)/shard_map/ppermute | solution.py:489
  71.4 4.2 %collective-permute-start.6 = (f32[496,128]{1,0:T(8,128)S(1)}, f32[496,128]{1,0:T(8,128)S(1)}, u32[]{:S(2)}, u32[]{:S(2)}) collective-permute-start(f32[496,128]{1,0:T(8,128)S(1)} %unit_flows.7), channel_id=1, source_target_pairs={{0,2},{2,0},{1,3},{3,1},{4,6},{6,4},{5,7},{7,5},{8,10},{10,8},{9,1... | collective-permute-start | bytes 761864 | tf_op jit(solution)/shard_map/ppermute | solution.py:463
  75.7 5.3 %collective-permute-start.9 = (f32[256,128]{1,0:T(8,128)S(1)}, f32[256,128]{1,0:T(8,128)S(1)}, u32[]{:S(2)}, u32[]{:S(2)}) collective-permute-start(f32[256,128]{1,0:T(8,128)S(1)} %slice.27), channel_id=1, source_target_pairs={{0,4},{4,0},{8,12},{12,8},{6,10},{10,6},{14,2},{2,14},{1,5},{5,1},... | collective-permute-start | bytes 393224 | tf_op jit(solution)/shard_map/ppermute | solution.py:432
  76.7 5.4 %collective-permute-start.7 = (f32[240,128]{1,0:T(8,128)S(1)}, f32[240,128]{1,0:T(8,128)S(1)}, u32[]{:S(2)}, u32[]{:S(2)}) collective-permute-start(f32[240,128]{1,0:T(8,128)S(1)} %slice.26), channel_id=1, source_target_pairs={{0,4},{4,0},{8,12},{12,8},{6,10},{10,6},{14,2},{2,14},{1,5},{5,1},... | collective-permute-start | bytes 368648 | tf_op jit(solution)/shard_map/ppermute | solution.py:432
  78.5 4.1 %collective-permute-start.8 = (f32[32,128]{1,0:T(8,128)S(1)}, f32[32,128]{1,0:T(8,128)S(1)}, u32[]{:S(2)}, u32[]{:S(2)}) collective-permute-start(f32[32,128]{1,0:T(8,128)S(1)} %get-tuple-element.92.own_ref.old_ref), channel_id=1, source_target_pairs={{0,1},{1,0},{2,3},{3,2},{4,5},{5,4},{6,7},{7,6},{8,9},{9,8},{10,11... | collective-permute-start | bytes 49160 | tf_op jit(solution)/shard_map/ppermute | solution.py:470
  81.0 4.1 %collective-permute-start.11 = (f32[256,128]{1,0:T(8,128)S(1)}, f32[256,128]{1,0:T(8,128)S(1)}, u32[]{:S(2)}, u32[]{:S(2)}) collective-permute-start(f32[256,128]{1,0:T(8,128)S(1)} %slice_add_fusion.6.refs_1_), channel_id=1, source_target_pairs={{4,8},{8,4},{12,0},{0,12},{2,6},{6,2},{10,14},{14,10},{5,9},{9,5},... | collective-permute-start | bytes 393224 | tf_op jit(solution)/shard_map/ppermute | solution.py:432
  82.6 4.1 %collective-permute-start.10 = (f32[240,128]{1,0:T(8,128)S(1)}, f32[240,128]{1,0:T(8,128)S(1)}, u32[]{:S(2)}, u32[]{:S(2)}) collective-permute-start(f32[240,128]{1,0:T(8,128)S(1)} %slice_add_fusion.2.refs_0_), channel_id=1, source_target_pairs={{4,8},{8,4},{12,0},{0,12},{2,6},{6,2},{10,14},{14,10},{5,9},{9,5},... | collective-permute-start | bytes 368648 | tf_op jit(solution)/shard_map/ppermute | solution.py:432
  87.0 4.1 %collective-permute-start.12 = (f32[496,128]{1,0:T(8,128)S(1)}, f32[496,128]{1,0:T(8,128)S(1)}, u32[]{:S(2)}, u32[]{:S(2)}) collective-permute-start(f32[496,128]{1,0:T(8,128)S(1)} %get-tuple-element.102.dual_ref.refs_5_), channel_id=1, source_target_pairs={{0,2},{2,0},{1,3},{3,1},{4,6},{6,4},{5,7},{7,5},{8,10},{10,8},{9,1... | collective-permute-start | bytes 761864 | tf_op jit(solution)/shard_map/ppermute | solution.py:489
  119.5 4.2 %collective-permute-start.13 = (f32[496,128]{1,0:T(8,128)S(1)}, f32[496,128]{1,0:T(8,128)S(1)}, u32[]{:S(2)}, u32[]{:S(2)}) collective-permute-start(f32[496,128]{1,0:T(8,128)S(1)} %unit_flows.9), channel_id=1, source_target_pairs={{0,2},{2,0},{1,3},{3,1},{4,6},{6,4},{5,7},{7,5},{8,10},{10,8},{9,1... | collective-permute-start | bytes 761864 | tf_op jit(solution)/shard_map/ppermute | solution.py:463
  123.8 5.3 %collective-permute-start.16 = (f32[256,128]{1,0:T(8,128)S(1)}, f32[256,128]{1,0:T(8,128)S(1)}, u32[]{:S(2)}, u32[]{:S(2)}) collective-permute-start(f32[256,128]{1,0:T(8,128)S(1)} %slice.29), channel_id=1, source_target_pairs={{0,4},{4,0},{8,12},{12,8},{6,10},{10,6},{14,2},{2,14},{1,5},{5,1},... | collective-permute-start | bytes 393224 | tf_op jit(solution)/shard_map/ppermute | solution.py:432
  124.8 5.4 %collective-permute-start.14 = (f32[240,128]{1,0:T(8,128)S(1)}, f32[240,128]{1,0:T(8,128)S(1)}, u32[]{:S(2)}, u32[]{:S(2)}) collective-permute-start(f32[240,128]{1,0:T(8,128)S(1)} %slice.28), channel_id=1, source_target_pairs={{0,4},{4,0},{8,12},{12,8},{6,10},{10,6},{14,2},{2,14},{1,5},{5,1},... | collective-permute-start | bytes 368648 | tf_op jit(solution)/shard_map/ppermute | solution.py:432
  126.6 4.1 %collective-permute-start.15 = (f32[32,128]{1,0:T(8,128)S(1)}, f32[32,128]{1,0:T(8,128)S(1)}, u32[]{:S(2)}, u32[]{:S(2)}) collective-permute-start(f32[32,128]{1,0:T(8,128)S(1)} %get-tuple-element.108.own_ref.old_ref), channel_id=1, source_target_pairs={{0,1},{1,0},{2,3},{3,2},{4,5},{5,4},{6,7},{7,6},{8,9},{9,8},{10,11... | collective-permute-start | bytes 49160 | tf_op jit(solution)/shard_map/ppermute | solution.py:470
  130.7 4.0 %collective-permute-start.17 = (f32[240,128]{1,0:T(8,128)S(1)}, f32[240,128]{1,0:T(8,128)S(1)}, u32[]{:S(2)}, u32[]{:S(2)}) collective-permute-start(f32[240,128]{1,0:T(8,128)S(1)} %slice_add_fusion.1.refs_0_), channel_id=1, source_target_pairs={{4,8},{8,4},{12,0},{0,12},{2,6},{6,2},{10,14},{14,10},{5,9},{9,5},... | collective-permute-start | bytes 368648 | tf_op jit(solution)/shard_map/ppermute | solution.py:432
  135.0 4.2 %collective-permute-start.19 = (f32[496,128]{1,0:T(8,128)S(1)}, f32[496,128]{1,0:T(8,128)S(1)}, u32[]{:S(2)}, u32[]{:S(2)}) collective-permute-start(f32[496,128]{1,0:T(8,128)S(1)} %get-tuple-element.116.dual_ref.refs_5_), channel_id=1, source_target_pairs={{0,2},{2,0},{1,3},{3,1},{4,6},{6,4},{5,7},{7,5},{8,10},{10,8},{9,1... | collective-permute-start | bytes 761864 | tf_op jit(solution)/shard_map/ppermute | solution.py:489
  168.1 4.2 %collective-permute-start.20 = (f32[496,128]{1,0:T(8,128)S(1)}, f32[496,128]{1,0:T(8,128)S(1)}, u32[]{:S(2)}, u32[]{:S(2)}) collective-permute-start(f32[496,128]{1,0:T(8,128)S(1)} %unit_flows.11), channel_id=1, source_target_pairs={{0,2},{2,0},{1,3},{3,1},{4,6},{6,4},{5,7},{7,5},{8,10},{10,8},{9,1... | collective-permute-start | bytes 761864 | tf_op jit(solution)/shard_map/ppermute | solution.py:463
  172.4 5.1 %collective-permute-start.22 = (f32[256,128]{1,0:T(8,128)S(1)}, f32[256,128]{1,0:T(8,128)S(1)}, u32[]{:S(2)}, u32[]{:S(2)}) collective-permute-start(f32[256,128]{1,0:T(8,128)S(1)} %slice.33), channel_id=1, source_target_pairs={{0,4},{4,0},{8,12},{12,8},{6,10},{10,6},{14,2},{2,14},{1,5},{5,1},... | collective-permute-start | bytes 393224 | tf_op jit(solution)/shard_map/ppermute | solution.py:432
  173.5 5.4 %collective-permute-start.21 = (f32[240,128]{1,0:T(8,128)S(1)}, f32[240,128]{1,0:T(8,128)S(1)}, u32[]{:S(2)}, u32[]{:S(2)}) collective-permute-start(f32[240,128]{1,0:T(8,128)S(1)} %slice.32), channel_id=1, source_target_pairs={{0,4},{4,0},{8,12},{12,8},{6,10},{10,6},{14,2},{2,14},{1,5},{5,1},... | collective-permute-start | bytes 368648 | tf_op jit(solution)/shard_map/ppermute | solution.py:432
  177.5 5.5 %collective-permute-start.24 = (f32[256,128]{1,0:T(8,128)S(1)}, f32[256,128]{1,0:T(8,128)S(1)}, u32[]{:S(2)}, u32[]{:S(2)}) collective-permute-start(f32[256,128]{1,0:T(8,128)S(1)} %slice_add_fusion.4.refs_1_), channel_id=1, source_target_pairs={{4,8},{8,4},{12,0},{0,12},{2,6},{6,2},{10,14},{14,10},{5,9},{9,5},... | collective-permute-start | bytes 393224 | tf_op jit(solution)/shard_map/ppermute | solution.py:432
  178.9 4.2 %collective-permute-start.23 = (f32[240,128]{1,0:T(8,128)S(1)}, f32[240,128]{1,0:T(8,128)S(1)}, u32[]{:S(2)}, u32[]{:S(2)}) collective-permute-start(f32[240,128]{1,0:T(8,128)S(1)} %slice_add_fusion.refs_0_), channel_id=1, source_target_pairs={{4,8},{8,4},{12,0},{0,12},{2,6},{6,2},{10,14},{14,10},{5,9},{9,5},... | collective-permute-start | bytes 368648 | tf_op jit(solution)/shard_map/ppermute | solution.py:432
  (6 other events, 69.0 us)

commit v7 on v6

--- a/solution.py
+++ b/solution.py
@@ -11,6 +11,7 @@
 UNITS = 4096
 ITERS = 4
 LINE = ("z", "xl")
+EXCHANGE = ("xl", "z")
 BUS = ("y", "c")
 LINE_BUS = ("z", "xl", "y", "c")
 
@@ -46,6 +47,10 @@
 
 def dot(left, right, dims=((1,), (0,))):
     return lax.dot_general(left, right, (dims, ((), ())), preferred_element_type=F32)
+
+
+def exchange_place(line):
+    return line % 2 * 8 + line // 2
 
 
 def row_index(shape, first):
@@ -269,7 +274,8 @@
 
 
 def flow_kernel(place_ref, high_ref, low_ref, extrap_ref, flow_ref):
-    high, low = halves(extrap_ref[...])
+    blocks = [extrap_ref[exchange_place(line)] for line in range(extrap_ref.shape[0])]
+    high, low = halves(jnp.concatenate(blocks, axis=0))
     pair = jnp.concatenate([high, low], axis=1)
     rows = pl.ds(pl.multiple_of(place_ref[0] * HALF, 16), HALF)
     both = dot(high_ref[rows, :], pair)
@@ -320,7 +326,10 @@
     both = dot(jnp.concatenate([high, low], axis=0), high_ref[rows, :])
     price = both[:128] + both[128:] + dot(high, low_ref[rows, :])
     if len(refs) == 2:
-        refs[1][...] = (refs[0][...] + price).T
+        price = (refs[0][...] + price).T
+        count, local, _ = refs[1].shape
+        for line in range(count):
+            refs[1][exchange_place(line)] = price[line * local : (line + 1) * local]
     else:
         refs[0][...] = price
 
@@ -331,33 +340,41 @@
         price_kernel,
         in_specs=[SMEM] + [VMEM] * (3 + len(part)),
         out_specs=VMEM,
-        out_shape=jax.ShapeDtypeStruct((units, 128) if part else (128, units), F32),
+        out_shape=jax.ShapeDtypeStruct((16, units // 16, 128) if part else (128, units), F32),
         compiler_params=params(8),
         cost_estimate=cost_of(3 * 2 * HALF * 512 * 128, 4 * HALF * 512),
         name="unit_prices",
     )(place, dual, high, low, *part)
 
 
-def joined_kernel(core_ref, mine_ref, other_ref, dual_ref):
-    first = core_ref[0] == 0
-    mine, other = mine_ref[...], other_ref[...]
-    dual_ref[:HALF, :] = jnp.where(first, mine, other)
-    rest = LINES_DEV - HALF
-    dual_ref[HALF:, :] = jnp.where(first, other[:rest], mine[:rest])
-
-
-def joined(core, mine, other):
-    return pl.pallas_call(
-        joined_kernel,
-        in_specs=[SMEM, VMEM, VMEM],
-        out_specs=VMEM,
+def placed_kernel(place_ref, half_ref, *refs):
+    out_ref, arrived = refs[-2:]
+    for place, count in enumerate((HALF, LINES_DEV - HALF)):
+
+        @pl.when(place_ref[0] == place)
+        def _(place=place, count=count):
+            rows = out_ref.at[pl.ds(place * HALF, count), :]
+            copy = pltpu.make_async_copy(half_ref.at[pl.ds(0, count), :], rows, arrived)
+            copy.start()
+            copy.wait()
+
+
+def placed(place, half, *begun):
+    anywhere = pl.BlockSpec(memory_space=pl.ANY)
+    return pl.pallas_call(
+        placed_kernel,
+        in_specs=[SMEM, VMEM] + [anywhere] * len(begun),
+        out_specs=anywhere,
         out_shape=jax.ShapeDtypeStruct((LINES_DEV, 128), F32),
+        scratch_shapes=[pltpu.SemaphoreType.DMA(())],
+        input_output_aliases={2: 0} if begun else {},
         compiler_params=params(8),
-        name="joined",
-    )(core, mine, other)
-
-
-def unit_kernel(price_ref, gen_ref, old_ref, state_ref, table_ref, gen_out, extrap_ref, copies_ref):
+        cost_estimate=cost_of(0, 8 * HALF * 128),
+        name="placed",
+    )(place, half, *begun)
+
+
+def unit_kernel(price_ref, gen_ref, old_ref, state_ref, table_ref, extrap_ref, copies_ref, *gen_out):
     cost = table_ref[:, 0:1]
     lower = table_ref[:, 1:2]
     upper = table_ref[:, 2:3]
@@ -365,24 +382,26 @@
     gradient = cost + jnp.sum(price_ref[...], axis=0) + state_ref[...]
     updated = jnp.clip(gen - PRIMAL_STEP * gradient, lower, upper)
     extrap = 2.0 * updated - gen
-    gen_out[...] = updated
+    for ref in gen_out:
+        ref[...] = updated
     extrap_ref[...] = extrap
     copies_ref[...] = jnp.broadcast_to((extrap - old_ref[...])[None], copies_ref.shape)
 
 
-def unit_step(prices, gen, old, state, table):
+def unit_step(prices, gen, old, state, table, last):
     one = jax.ShapeDtypeStruct(gen.shape, F32)
+    shapes = [one, jax.ShapeDtypeStruct(prices.shape, F32)] + ([] if last else [one])
     return pl.pallas_call(
         unit_kernel,
         in_specs=[VMEM] * 5,
-        out_specs=[VMEM] * 3,
-        out_shape=[one, one, jax.ShapeDtypeStruct(prices.shape, F32)],
+        out_specs=[VMEM] * len(shapes),
+        out_shape=shapes,
         compiler_params=params(8),
         name="unit_step",
     )(prices, gen, old, state, table)
 
 
-def state_kernel(place_ref, own_ref, far_ref, ramp_ref, store_ref, table_ref, ramp_out, store_out, state_ref):
+def state_kernel(place_ref, own_ref, far_ref, ramp_ref, store_ref, table_ref, state_ref, *kept):
     ramp_limit = DUAL_STEP * table_ref[:, 3:4]
     storage = table_ref[:, 4:5]
     store_limit = DUAL_STEP * table_ref[:, 5:6]
@@ -394,7 +413,6 @@
     previous = pltpu.roll(extrap, 1, 1)
     moved = ramp_ref[...] + jnp.where(hour >= 1, DUAL_STEP * (extrap - previous), 0.0)
     ramp = moved - jnp.clip(moved, -ramp_limit, ramp_limit)
-    ramp_out[...] = ramp
     early = lax.broadcasted_iota(jnp.int32, (hours, hours), 0)
     late = lax.broadcasted_iota(jnp.int32, (hours, hours), 1)
     forward = jnp.where(early <= late, 1.0, 0.0)
@@ -402,20 +420,22 @@
     running = jnp.dot(extrap, forward, precision=lax.Precision.HIGHEST, preferred_element_type=F32)
     moved = store_ref[...] + DUAL_STEP * storage * running
     store = moved - jnp.clip(moved, -store_limit, store_limit)
-    store_out[...] = store
+    for ref, value in zip(kept, (ramp, store)):
+        ref[...] = value
     suffix = jnp.dot(store, backward, precision=lax.Precision.HIGHEST, preferred_element_type=F32)
     after = jnp.where(hour < hours - 1, pltpu.roll(ramp, hours - 1, 1), 0.0)
     state = ramp - after + storage * suffix
     state_ref[...] = jnp.where(first, state[:, :128], state[:, 128:])
 
 
-def state_step(place, own, far, ramp, store, table):
+def state_step(place, own, far, ramp, store, table, last):
     wide = jax.ShapeDtypeStruct(ramp.shape, F32)
+    shapes = [jax.ShapeDtypeStruct(own.shape, F32)] + ([] if last else [wide, wide])
     return pl.pallas_call(
         state_kernel,
         in_specs=[SMEM] + [VMEM] * 5,
-        out_specs=[VMEM] * 3,
-        out_shape=[wide, wide, jax.ShapeDtypeStruct(own.shape, F32)],
+        out_specs=[VMEM] * len(shapes),
+        out_shape=shapes,
         compiler_params=params(8),
         cost_estimate=cost_of(12 * 2 * 32 * 256 * 256, 1 << 18),
         name="state_step",
@@ -462,7 +482,7 @@
         last = iteration == ITERS - 1
         total = mine + lax.ppermute(other, "c", SWAP)
         if iteration == 0:
-            ramp, store, state = state_step(place, extrap, far, ramp, store, table)
+            state, ramp, store = state_step(place, extrap, far, ramp, store, table, False)
             total, tied, rows, state = lax.optimization_barrier((total, ptdf, unit_rows, state))
             high, low = unit_columns(tied, rows, line_count * local)
         elif not last:
@@ -476,21 +496,26 @@
         elif not last:
             lefts[0], far = lax.optimization_barrier((lefts[0], far))
         if 0 < iteration < ITERS - 1:
-            ramp, store, state = state_step(place, extrap, far, ramp, store, table)
+            state, *kept = state_step(place, extrap, far, ramp, store, table, iteration == ITERS - 2)
+            ramp, store = kept if kept else (None, None)
         rights = [along_y(left, (FAR, NEAR)) for left in lefts]
         if iteration == 0:
             rights[-1], high, low = lax.optimization_barrier((rights[-1], high, low))
         if last:
             (dual,) = dual_step(lefts, rights, flow, dual, steps, limits, 1)
-            return gen, joined(core, dual, lax.ppermute(dual, "c", SWAP))
+            result = placed(core, dual)
+            return 0.5 * (extrap + before), placed(partner, lax.ppermute(dual, "c", SWAP), result)
         rights[-1], state, ramp, store = lax.optimization_barrier((rights[-1], state, ramp, store))
         dual, flow = dual_step(lefts, rights, flow, dual, steps, limits, 2)
         prices = unit_prices(core, dual, high, low)
         prices = unit_prices(partner, lax.ppermute(dual, "c", SWAP), high, low, prices)
-        prices = prices.reshape(line_count, local, hour_dev)
-        prices = lax.all_to_all(prices, LINE, 0, 0, tiled=True)
-        gen, extrap, copies = unit_step(prices, gen, extrap, state, table)
-        changes = lax.all_to_all(copies, LINE, 0, 0, tiled=True).reshape(-1, hour_dev)
+        prices = lax.all_to_all(prices, EXCHANGE, 0, 0, tiled=True)
+        before = gen
+        extrap, copies, *updated = unit_step(
+            prices, gen, extrap, state, table, iteration == ITERS - 2
+        )
+        gen = updated[0] if updated else None
+        changes = lax.all_to_all(copies, EXCHANGE, 0, 0, tiled=True)
         other = unit_flows(partner, high, low, changes)
         mine = unit_flows(core, high, low, changes)
 

time: 188 us -> 184 us (0.979)
  blocking collectives: 82.2 us -> 77.7 us
    all_to_all x6, blocking collectives: 82.2 us -> 77.7 us  [the longest x3 39.4 us: on_device(): changes = lax.all_to_all(copies, EXCHANGE, 0, 0, tiled=True)]
    ppermute x1 -> x0, starting transfers between devices: 2.46 us -> none  [on_device(): return (gen, joined(core, dual, lax.ppermute(dual, 'c', SWAP)))]
    ppermute x3 -> x4, starting transfers between devices: 9.17 us -> 11.6 us  [on_device(): lax.ppermute(dual, 'c', SWAP)]
  transfers between devices with their start and end apart: 27 -> 27, of which waited for: 22 -> 21; matrix products, arithmetic and copies ran while one was open for 0% -> 1% of each run, Pallas kernels for 8% -> 9%
where the time goes in v7:
time: 184 us; the launch traced here: 183 us
  blocking collectives  77.7 us (42%)
  starting transfers between devices  51.2 us (28%)
  waiting for transfers between devices  27.3 us (15%)
  Pallas kernels  24.8 us (13%)
    all_to_all x3, blocking collectives, on_device(): changes = lax.all_to_all(copies, EXCHANGE, 0, 0, tiled=True)  39.4 us
    all_to_all x3, blocking collectives, on_device(): prices = lax.all_to_all(prices, EXCHANGE, 0, 0, tiled=True)  38.3 us
    ppermute x16, waiting for transfers between devices, along_y(): return lax.ppermute(value, BUS, pairs)  18.2 us
    ppermute x16, starting transfers between devices, along_y(): return lax.ppermute(value, BUS, pairs)  12.7 us
    ppermute x4, starting transfers between devices, on_device(): total = mine + lax.ppermute(other, 'c', SWAP)  11.9 us
    ppermute x4, starting transfers between devices, on_device(): lax.ppermute(dual, 'c', SWAP)  11.6 us
    all_to_all x1, starting transfers between devices, on_device(): unit_rows = lax.all_to_all(copies, LINE, 0, 0, tiled=True)  10 us
    pallas_call x2, Pallas kernels, unit_columns(): pl.pallas_call(functools.partial(columns_kernel, group), grid=(ROWS // BL...  5.9 us
  transfers between devices with their start and end apart: 27, of which 21 were waited for; matrix products, arithmetic and copies ran while one was open for 1% of the time, Pallas kernels for 9%

profile of v7, /device:TPU:1, one launch (start us, length us, event | category | flops | bytes accessed | tf_op | source)
XLA Modules:
  0.0 183.4 jit_solution(14620252226544222455)
XLA Ops:
  2.1 10.0 %all-to-all-start = ((f32[16,8,128]{2,1,0:T(8,128)}), f32[16,8,128]{2,1,0:T(8,128)S(1)}, u32[]{:S(2)}, u32[]{:S(2)}) async-start(f32[16,8,128]{2,1,0:T(8,128)} %get-tuple-element.63), calls=%async_computation | async-start | bytes 131072 | tf_op jit(solution)/shard_map/all_to_all | solution.py:465
  12.2 4.7 %load_flows.1 = (f32[992,128]{1,0:T(8,128)S(1)}, f32[320,1536]{1,0:T(8,128)S(1)}) custom-call(f32[960,1536]{1,0:T(8,128)} %ptdf_ref.3, f32[1536,128]{1,0:T(8,128)} %load_ref.1), custom_call_target="tpu_custom_call" | custom-call | flops 1207959552 | bytes 6291456 | tf_op jit(solution)/shard_map/load_flows/pallas_call | solution.py:156
  16.9 3.2 %all-to-all-done.unit_ref = f32[16,8,128]{2,1,0:T(8,128)S(1)} async-done(((f32[16,8,128]{2,1,0:T(8,128)}), f32[16,8,128]{2,1,0:T(8,128)S(1)}, u32[]{:S(2)}, u32[]{:S(2)}) %all-to-all-start) | async-done | bytes 65568 | tf_op jit(solution)/shard_map/all_to_all | solution.py:465
  20.1 2.6 %first_flows.1 = (f32[496,128]{1,0:T(8,128)S(1)}, f32[496,128]{1,0:T(8,128)S(1)}) custom-call(s32[1]{0:T(128)} %bitcast.core_ref.place_ref, f32[960,1536]{1,0:T(8,128)} %ptdf_ref.3, f32[992,128]{1,0:T(8,128)S(1)} %get-tuple-element.61.load_ref, f32[320,1536]{1,0:T(8,128)S(1)} %get-tuple-element.62.kept_ref, f32[16,8,128]{2,1,0:T(8,128)S(1)} %all-to-all-done.unit_ref), custom_call_target="tpu_custom_call" | custom-call | flops 3145728 | bytes 6291456 | tf_op jit(solution)/shard_map/first_flows/pallas_call | solution.py:209
  26.1 2.8 %collective-permute-start.3 = (f32[240,128]{1,0:T(8,128)S(1)}, f32[240,128]{1,0:T(8,128)S(1)}, u32[]{:S(2)}, u32[]{:S(2)}) collective-permute-start(f32[240,128]{1,0:T(8,128)S(1)} %slice.25), channel_id=1, source_target_pairs={{0,4},{4,0},{8,12},{12,8},{6,10},{10,6},{14,2},{2,14},{1,5},{5,1},... | collective-permute-start | bytes 368648 | tf_op jit(solution)/shard_map/ppermute | solution.py:452
  29.1 2.9 %unit_columns.2 = (bf16[1024,512]{1,0:T(8,128)(2,1)S(1)}, bf16[1024,512]{1,0:T(8,128)(2,1)S(1)}) custom-call(f32[960,1536]{1,0:T(8,128)} %ptdf_ref.3, f32[16,8,128]{2,1,0:T(8,128)S(1)} %all-to-all-done.unit_ref), custom_call_target="tpu_custom_call" | custom-call | flops 805306368 | bytes 3145728 | tf_op jit(solution)/shard_map/unit_columns/pallas_call | solution.py:258
  34.5 3.0 %unit_columns.3 = (bf16[1024,512]{1,0:T(8,128)(2,1)S(1)}, bf16[1024,512]{1,0:T(8,128)(2,1)S(1)}) custom-call(f32[960,1536]{1,0:T(8,128)} %ptdf_ref.3, f32[16,8,128]{2,1,0:T(8,128)S(1)} %all-to-all-done.unit_ref, bf16[1024,512]{1,0:T(8,128)(2,1)S(1)} %get-tuple-element.74.refs_0_, ...), custom_call_target="tpu_custom_call", output_to_operand_aliasing={{0}: (2, {}), {1}: (3, {})} | custom-call | flops 805306368 | bytes 3145728 | tf_op jit(solution)/shard_map/unit_columns/pallas_call | solution.py:258
  38.4 3.2 %collective-permute-start.5 = (f32[496,128]{1,0:T(8,128)S(1)}, f32[496,128]{1,0:T(8,128)S(1)}, u32[]{:S(2)}, u32[]{:S(2)}) collective-permute-start(f32[496,128]{1,0:T(8,128)S(1)} %get-tuple-element.86.dual_ref.refs_5_), channel_id=1, source_target_pairs={{0,2},{2,0},{1,3},{3,1},{4,6},{6,4},{5,7},{7,5},{8,10},{10,8},{9,1... | collective-permute-start | bytes 761864 | tf_op jit(solution)/shard_map/ppermute | solution.py:511
  43.2 12.3 %all_to_all.35.price_ref = f32[16,32,128]{2,1,0:T(8,128)S(1)} all-to-all(f32[16,32,128]{2,1,0:T(8,128)S(1)} %unit_prices.7), channel_id=1, replica_groups=mesh['z'=8,'xl'=2,'y'=4,'c'=2,'t'=2] {'xl','z'}, dimensions={0} | all-to-all | bytes 524288 | tf_op jit(solution)/shard_map/all_to_all | solution.py:512
  55.6 13.1 %all_to_all.36.extrap_ref = f32[16,32,128]{2,1,0:T(8,128)S(1)} all-to-all(f32[16,32,128]{2,1,0:T(8,128)S(1)} %get-tuple-element.88), channel_id=1, replica_groups=mesh['z'=8,'xl'=2,'y'=4,'c'=2,'t'=2] {'xl','z'}, dimensions={0} | all-to-all | bytes 524288 | tf_op jit(solution)/shard_map/all_to_all | solution.py:518
  69.2 3.2 %collective-permute-start.6 = (f32[496,128]{1,0:T(8,128)S(1)}, f32[496,128]{1,0:T(8,128)S(1)}, u32[]{:S(2)}, u32[]{:S(2)}) collective-permute-start(f32[496,128]{1,0:T(8,128)S(1)} %unit_flows.7), channel_id=1, source_target_pairs={{0,2},{2,0},{1,3},{3,1},{4,6},{6,4},{5,7},{7,5},{8,10},{10,8},{9,1... | collective-permute-start | bytes 761864 | tf_op jit(solution)/shard_map/ppermute | solution.py:483
  76.5 2.4 %collective-permute-start.8 = (f32[32,128]{1,0:T(8,128)S(1)}, f32[32,128]{1,0:T(8,128)S(1)}, u32[]{:S(2)}, u32[]{:S(2)}) collective-permute-start(f32[32,128]{1,0:T(8,128)S(1)} %get-tuple-element.91.own_ref.old_ref), channel_id=1, source_target_pairs={{0,1},{1,0},{2,3},{3,2},{4,5},{5,4},{6,7},{7,6},{8,9},{9,8},{10,11... | collective-permute-start | bytes 49160 | tf_op jit(solution)/shard_map/ppermute | solution.py:490
  84.9 3.0 %collective-permute-start.12 = (f32[496,128]{1,0:T(8,128)S(1)}, f32[496,128]{1,0:T(8,128)S(1)}, u32[]{:S(2)}, u32[]{:S(2)}) collective-permute-start(f32[496,128]{1,0:T(8,128)S(1)} %get-tuple-element.101.dual_ref.refs_5_), channel_id=1, source_target_pairs={{0,2},{2,0},{1,3},{3,1},{4,6},{6,4},{5,7},{7,5},{8,10},{10,8},{9,1... | collective-permute-start | bytes 761864 | tf_op jit(solution)/shard_map/ppermute | solution.py:511
  89.6 13.0 %all_to_all.37.price_ref = f32[16,32,128]{2,1,0:T(8,128)S(1)} all-to-all(f32[16,32,128]{2,1,0:T(8,128)S(1)} %unit_prices.9), channel_id=1, replica_groups=mesh['z'=8,'xl'=2,'y'=4,'c'=2,'t'=2] {'xl','z'}, dimensions={0} | all-to-all | bytes 524288 | tf_op jit(solution)/shard_map/all_to_all | solution.py:512
  102.7 13.1 %all_to_all.38.extrap_ref = f32[16,32,128]{2,1,0:T(8,128)S(1)} all-to-all(f32[16,32,128]{2,1,0:T(8,128)S(1)} %get-tuple-element.104), channel_id=1, replica_groups=mesh['z'=8,'xl'=2,'y'=4,'c'=2,'t'=2] {'xl','z'}, dimensions={0} | all-to-all | bytes 524288 | tf_op jit(solution)/shard_map/all_to_all | solution.py:518
  116.3 3.2 %collective-permute-start.13 = (f32[496,128]{1,0:T(8,128)S(1)}, f32[496,128]{1,0:T(8,128)S(1)}, u32[]{:S(2)}, u32[]{:S(2)}) collective-permute-start(f32[496,128]{1,0:T(8,128)S(1)} %unit_flows.9), channel_id=1, source_target_pairs={{0,2},{2,0},{1,3},{3,1},{4,6},{6,4},{5,7},{7,5},{8,10},{10,8},{9,1... | collective-permute-start | bytes 761864 | tf_op jit(solution)/shard_map/ppermute | solution.py:483
  123.6 2.4 %collective-permute-start.15 = (f32[32,128]{1,0:T(8,128)S(1)}, f32[32,128]{1,0:T(8,128)S(1)}, u32[]{:S(2)}, u32[]{:S(2)}) collective-permute-start(f32[32,128]{1,0:T(8,128)S(1)} %get-tuple-element.107.own_ref.old_ref), channel_id=1, source_target_pairs={{0,1},{1,0},{2,3},{3,2},{4,5},{5,4},{6,7},{7,6},{8,9},{9,8},{10,11... | collective-permute-start | bytes 49160 | tf_op jit(solution)/shard_map/ppermute | solution.py:490
  132.0 3.0 %collective-permute-start.19 = (f32[496,128]{1,0:T(8,128)S(1)}, f32[496,128]{1,0:T(8,128)S(1)}, u32[]{:S(2)}, u32[]{:S(2)}) collective-permute-start(f32[496,128]{1,0:T(8,128)S(1)} %get-tuple-element.114.dual_ref.refs_5_), channel_id=1, source_target_pairs={{0,2},{2,0},{1,3},{3,1},{4,6},{6,4},{5,7},{7,5},{8,10},{10,8},{9,1... | collective-permute-start | bytes 761864 | tf_op jit(solution)/shard_map/ppermute | solution.py:511
  136.7 13.0 %all_to_all.39.price_ref = f32[16,32,128]{2,1,0:T(8,128)S(1)} all-to-all(f32[16,32,128]{2,1,0:T(8,128)S(1)} %unit_prices.11), channel_id=1, replica_groups=mesh['z'=8,'xl'=2,'y'=4,'c'=2,'t'=2] {'xl','z'}, dimensions={0} | all-to-all | bytes 524288 | tf_op jit(solution)/shard_map/all_to_all | solution.py:512
  149.8 13.1 %all_to_all.40.extrap_ref = f32[16,32,128]{2,1,0:T(8,128)S(1)} all-to-all(f32[16,32,128]{2,1,0:T(8,128)S(1)} %get-tuple-element.118), channel_id=1, replica_groups=mesh['z'=8,'xl'=2,'y'=4,'c'=2,'t'=2] {'xl','z'}, dimensions={0} | all-to-all | bytes 524288 | tf_op jit(solution)/shard_map/all_to_all | solution.py:518
  163.4 3.2 %collective-permute-start.20 = (f32[496,128]{1,0:T(8,128)S(1)}, f32[496,128]{1,0:T(8,128)S(1)}, u32[]{:S(2)}, u32[]{:S(2)}) collective-permute-start(f32[496,128]{1,0:T(8,128)S(1)} %unit_flows.11), channel_id=1, source_target_pairs={{0,2},{2,0},{1,3},{3,1},{4,6},{6,4},{5,7},{7,5},{8,10},{10,8},{9,1... | collective-permute-start | bytes 761864 | tf_op jit(solution)/shard_map/ppermute | solution.py:483
  170.7 2.3 %collective-permute-done.22 = f32[256,128]{1,0:T(8,128)S(1)} collective-permute-done((f32[256,128]{1,0:T(8,128)S(1)}, f32[256,128]{1,0:T(8,128)S(1)}, u32[]{:S(2)}, u32[]{:S(2)}) %collective-permute-start.22) | collective-permute-done | bytes 131104 | tf_op jit(solution)/shard_map/ppermute | solution.py:452
  174.6 3.9 %collective-permute-done.23.refs_2_ = f32[240,128]{1,0:T(8,128)S(1)} collective-permute-done((f32[240,128]{1,0:T(8,128)S(1)}, f32[240,128]{1,0:T(8,128)S(1)}, u32[]{:S(2)}, u32[]{:S(2)}) %collective-permute-start.23) | collective-permute-done | bytes 122912 | tf_op jit(solution)/shard_map/ppermute | solution.py:452
  178.8 2.5 %collective-permute-start.25 = (f32[496,128]{1,0:T(8,128)S(1)}, f32[496,128]{1,0:T(8,128)S(1)}, u32[]{:S(2)}, u32[]{:S(2)}) collective-permute-start(f32[496,128]{1,0:T(8,128)S(1)} %dual_step.7.half_ref), channel_id=1, source_target_pairs={{0,2},{2,0},{1,3},{3,1},{4,6},{6,4},{5,7},{7,5},{8,10},{10,8},{9,1... | collective-permute-start | bytes 761864 | tf_op jit(solution)/shard_map/ppermute | solution.py:507
  (99 shorter events, 42.9 us)
Async XLA Ops:
  2.1 18.0 %all-to-all-start = ((f32[16,8,128]{2,1,0:T(8,128)}), f32[16,8,128]{2,1,0:T(8,128)S(1)}, u32[]{:S(2)}, u32[]{:S(2)}) async-start(f32[16,8,128]{2,1,0:T(8,128)} %get-tuple-element.63), calls=%async_computation | async-start | bytes 131072 | tf_op jit(solution)/shard_map/all_to_all | solution.py:465
  26.1 6.0 %collective-permute-start.3 = (f32[240,128]{1,0:T(8,128)S(1)}, f32[240,128]{1,0:T(8,128)S(1)}, u32[]{:S(2)}, u32[]{:S(2)}) collective-permute-start(f32[240,128]{1,0:T(8,128)S(1)} %slice.25), channel_id=1, source_target_pairs={{0,4},{4,0},{8,12},{12,8},{6,10},{10,6},{14,2},{2,14},{1,5},{5,1},... | collective-permute-start | bytes 368648 | tf_op jit(solution)/shard_map/ppermute | solution.py:452
  29.0 5.1 %collective-permute-start.1 = (f32[256,128]{1,0:T(8,128)S(1)}, f32[256,128]{1,0:T(8,128)S(1)}, u32[]{:S(2)}, u32[]{:S(2)}) collective-permute-start(f32[256,128]{1,0:T(8,128)S(1)} %slice.24), channel_id=1, source_target_pairs={{0,4},{4,0},{8,12},{12,8},{6,10},{10,6},{14,2},{2,14},{1,5},{5,1},... | collective-permute-start | bytes 393224 | tf_op jit(solution)/shard_map/ppermute | solution.py:452
  32.1 6.0 %collective-permute-start.4 = (f32[240,128]{1,0:T(8,128)S(1)}, f32[240,128]{1,0:T(8,128)S(1)}, u32[]{:S(2)}, u32[]{:S(2)}) collective-permute-start(f32[240,128]{1,0:T(8,128)S(1)} %slice_add_fusion.3.refs_0_), channel_id=1, source_target_pairs={{4,8},{8,4},{12,0},{0,12},{2,6},{6,2},{10,14},{14,10},{5,9},{9,5},... | collective-permute-start | bytes 368648 | tf_op jit(solution)/shard_map/ppermute | solution.py:452
  38.4 4.3 %collective-permute-start.5 = (f32[496,128]{1,0:T(8,128)S(1)}, f32[496,128]{1,0:T(8,128)S(1)}, u32[]{:S(2)}, u32[]{:S(2)}) collective-permute-start(f32[496,128]{1,0:T(8,128)S(1)} %get-tuple-element.86.dual_ref.refs_5_), channel_id=1, source_target_pairs={{0,2},{2,0},{1,3},{3,1},{4,6},{6,4},{5,7},{7,5},{8,10},{10,8},{9,1... | collective-permute-start | bytes 761864 | tf_op jit(solution)/shard_map/ppermute | solution.py:511
  69.2 4.4 %collective-permute-start.6 = (f32[496,128]{1,0:T(8,128)S(1)}, f32[496,128]{1,0:T(8,128)S(1)}, u32[]{:S(2)}, u32[]{:S(2)}) collective-permute-start(f32[496,128]{1,0:T(8,128)S(1)} %unit_flows.7), channel_id=1, source_target_pairs={{0,2},{2,0},{1,3},{3,1},{4,6},{6,4},{5,7},{7,5},{8,10},{10,8},{9,1... | collective-permute-start | bytes 761864 | tf_op jit(solution)/shard_map/ppermute | solution.py:483
  73.6 5.3 %collective-permute-start.9 = (f32[256,128]{1,0:T(8,128)S(1)}, f32[256,128]{1,0:T(8,128)S(1)}, u32[]{:S(2)}, u32[]{:S(2)}) collective-permute-start(f32[256,128]{1,0:T(8,128)S(1)} %slice.27), channel_id=1, source_target_pairs={{0,4},{4,0},{8,12},{12,8},{6,10},{10,6},{14,2},{2,14},{1,5},{5,1},... | collective-permute-start | bytes 393224 | tf_op jit(solution)/shard_map/ppermute | solution.py:452
  74.6 5.4 %collective-permute-start.7 = (f32[240,128]{1,0:T(8,128)S(1)}, f32[240,128]{1,0:T(8,128)S(1)}, u32[]{:S(2)}, u32[]{:S(2)}) collective-permute-start(f32[240,128]{1,0:T(8,128)S(1)} %slice.26), channel_id=1, source_target_pairs={{0,4},{4,0},{8,12},{12,8},{6,10},{10,6},{14,2},{2,14},{1,5},{5,1},... | collective-permute-start | bytes 368648 | tf_op jit(solution)/shard_map/ppermute | solution.py:452
  76.5 4.1 %collective-permute-start.8 = (f32[32,128]{1,0:T(8,128)S(1)}, f32[32,128]{1,0:T(8,128)S(1)}, u32[]{:S(2)}, u32[]{:S(2)}) collective-permute-start(f32[32,128]{1,0:T(8,128)S(1)} %get-tuple-element.91.own_ref.old_ref), channel_id=1, source_target_pairs={{0,1},{1,0},{2,3},{3,2},{4,5},{5,4},{6,7},{7,6},{8,9},{9,8},{10,11... | collective-permute-start | bytes 49160 | tf_op jit(solution)/shard_map/ppermute | solution.py:490
  78.9 4.1 %collective-permute-start.11 = (f32[256,128]{1,0:T(8,128)S(1)}, f32[256,128]{1,0:T(8,128)S(1)}, u32[]{:S(2)}, u32[]{:S(2)}) collective-permute-start(f32[256,128]{1,0:T(8,128)S(1)} %slice_add_fusion.6.refs_1_), channel_id=1, source_target_pairs={{4,8},{8,4},{12,0},{0,12},{2,6},{6,2},{10,14},{14,10},{5,9},{9,5},... | collective-permute-start | bytes 393224 | tf_op jit(solution)/shard_map/ppermute | solution.py:452
  80.5 4.1 %collective-permute-start.10 = (f32[240,128]{1,0:T(8,128)S(1)}, f32[240,128]{1,0:T(8,128)S(1)}, u32[]{:S(2)}, u32[]{:S(2)}) collective-permute-start(f32[240,128]{1,0:T(8,128)S(1)} %slice_add_fusion.2.refs_0_), channel_id=1, source_target_pairs={{4,8},{8,4},{12,0},{0,12},{2,6},{6,2},{10,14},{14,10},{5,9},{9,5},... | collective-permute-start | bytes 368648 | tf_op jit(solution)/shard_map/ppermute | solution.py:452
  84.9 4.1 %collective-permute-start.12 = (f32[496,128]{1,0:T(8,128)S(1)}, f32[496,128]{1,0:T(8,128)S(1)}, u32[]{:S(2)}, u32[]{:S(2)}) collective-permute-start(f32[496,128]{1,0:T(8,128)S(1)} %get-tuple-element.101.dual_ref.refs_5_), channel_id=1, source_target_pairs={{0,2},{2,0},{1,3},{3,1},{4,6},{6,4},{5,7},{7,5},{8,10},{10,8},{9,1... | collective-permute-start | bytes 761864 | tf_op jit(solution)/shard_map/ppermute | solution.py:511
  116.3 4.4 %collective-permute-start.13 = (f32[496,128]{1,0:T(8,128)S(1)}, f32[496,128]{1,0:T(8,128)S(1)}, u32[]{:S(2)}, u32[]{:S(2)}) collective-permute-start(f32[496,128]{1,0:T(8,128)S(1)} %unit_flows.9), channel_id=1, source_target_pairs={{0,2},{2,0},{1,3},{3,1},{4,6},{6,4},{5,7},{7,5},{8,10},{10,8},{9,1... | collective-permute-start | bytes 761864 | tf_op jit(solution)/shard_map/ppermute | solution.py:483
  120.7 5.3 %collective-permute-start.16 = (f32[256,128]{1,0:T(8,128)S(1)}, f32[256,128]{1,0:T(8,128)S(1)}, u32[]{:S(2)}, u32[]{:S(2)}) collective-permute-start(f32[256,128]{1,0:T(8,128)S(1)} %slice.29), channel_id=1, source_target_pairs={{0,4},{4,0},{8,12},{12,8},{6,10},{10,6},{14,2},{2,14},{1,5},{5,1},... | collective-permute-start | bytes 393224 | tf_op jit(solution)/shard_map/ppermute | solution.py:452
  121.8 5.4 %collective-permute-start.14 = (f32[240,128]{1,0:T(8,128)S(1)}, f32[240,128]{1,0:T(8,128)S(1)}, u32[]{:S(2)}, u32[]{:S(2)}) collective-permute-start(f32[240,128]{1,0:T(8,128)S(1)} %slice.28), channel_id=1, source_target_pairs={{0,4},{4,0},{8,12},{12,8},{6,10},{10,6},{14,2},{2,14},{1,5},{5,1},... | collective-permute-start | bytes 368648 | tf_op jit(solution)/shard_map/ppermute | solution.py:452
  123.6 4.1 %collective-permute-start.15 = (f32[32,128]{1,0:T(8,128)S(1)}, f32[32,128]{1,0:T(8,128)S(1)}, u32[]{:S(2)}, u32[]{:S(2)}) collective-permute-start(f32[32,128]{1,0:T(8,128)S(1)} %get-tuple-element.107.own_ref.old_ref), channel_id=1, source_target_pairs={{0,1},{1,0},{2,3},{3,2},{4,5},{5,4},{6,7},{7,6},{8,9},{9,8},{10,11... | collective-permute-start | bytes 49160 | tf_op jit(solution)/shard_map/ppermute | solution.py:490
  126.1 3.9 %collective-permute-start.18 = (f32[256,128]{1,0:T(8,128)S(1)}, f32[256,128]{1,0:T(8,128)S(1)}, u32[]{:S(2)}, u32[]{:S(2)}) collective-permute-start(f32[256,128]{1,0:T(8,128)S(1)} %slice_add_fusion.5.refs_1_), channel_id=1, source_target_pairs={{4,8},{8,4},{12,0},{0,12},{2,6},{6,2},{10,14},{14,10},{5,9},{9,5},... | collective-permute-start | bytes 393224 | tf_op jit(solution)/shard_map/ppermute | solution.py:452
  127.7 4.0 %collective-permute-start.17 = (f32[240,128]{1,0:T(8,128)S(1)}, f32[240,128]{1,0:T(8,128)S(1)}, u32[]{:S(2)}, u32[]{:S(2)}) collective-permute-start(f32[240,128]{1,0:T(8,128)S(1)} %slice_add_fusion.1.refs_0_), channel_id=1, source_target_pairs={{4,8},{8,4},{12,0},{0,12},{2,6},{6,2},{10,14},{14,10},{5,9},{9,5},... | collective-permute-start | bytes 368648 | tf_op jit(solution)/shard_map/ppermute | solution.py:452
  132.0 4.2 %collective-permute-start.19 = (f32[496,128]{1,0:T(8,128)S(1)}, f32[496,128]{1,0:T(8,128)S(1)}, u32[]{:S(2)}, u32[]{:S(2)}) collective-permute-start(f32[496,128]{1,0:T(8,128)S(1)} %get-tuple-element.114.dual_ref.refs_5_), channel_id=1, source_target_pairs={{0,2},{2,0},{1,3},{3,1},{4,6},{6,4},{5,7},{7,5},{8,10},{10,8},{9,1... | collective-permute-start | bytes 761864 | tf_op jit(solution)/shard_map/ppermute | solution.py:511
  163.4 4.4 %collective-permute-start.20 = (f32[496,128]{1,0:T(8,128)S(1)}, f32[496,128]{1,0:T(8,128)S(1)}, u32[]{:S(2)}, u32[]{:S(2)}) collective-permute-start(f32[496,128]{1,0:T(8,128)S(1)} %unit_flows.11), channel_id=1, source_target_pairs={{0,2},{2,0},{1,3},{3,1},{4,6},{6,4},{5,7},{7,5},{8,10},{10,8},{9,1... | collective-permute-start | bytes 761864 | tf_op jit(solution)/shard_map/ppermute | solution.py:483
  167.8 5.1 %collective-permute-start.22 = (f32[256,128]{1,0:T(8,128)S(1)}, f32[256,128]{1,0:T(8,128)S(1)}, u32[]{:S(2)}, u32[]{:S(2)}) collective-permute-start(f32[256,128]{1,0:T(8,128)S(1)} %slice.33), channel_id=1, source_target_pairs={{0,4},{4,0},{8,12},{12,8},{6,10},{10,6},{14,2},{2,14},{1,5},{5,1},... | collective-permute-start | bytes 393224 | tf_op jit(solution)/shard_map/ppermute | solution.py:452
  168.9 5.4 %collective-permute-start.21 = (f32[240,128]{1,0:T(8,128)S(1)}, f32[240,128]{1,0:T(8,128)S(1)}, u32[]{:S(2)}, u32[]{:S(2)}) collective-permute-start(f32[240,128]{1,0:T(8,128)S(1)} %slice.32), channel_id=1, source_target_pairs={{0,4},{4,0},{8,12},{12,8},{6,10},{10,6},{14,2},{2,14},{1,5},{5,1},... | collective-permute-start | bytes 368648 | tf_op jit(solution)/shard_map/ppermute | solution.py:452
  173.0 5.5 %collective-permute-start.24 = (f32[256,128]{1,0:T(8,128)S(1)}, f32[256,128]{1,0:T(8,128)S(1)}, u32[]{:S(2)}, u32[]{:S(2)}) collective-permute-start(f32[256,128]{1,0:T(8,128)S(1)} %slice_add_fusion.4.refs_1_), channel_id=1, source_target_pairs={{4,8},{8,4},{12,0},{0,12},{2,6},{6,2},{10,14},{14,10},{5,9},{9,5},... | collective-permute-start | bytes 393224 | tf_op jit(solution)/shard_map/ppermute | solution.py:452
  174.3 4.2 %collective-permute-start.23 = (f32[240,128]{1,0:T(8,128)S(1)}, f32[240,128]{1,0:T(8,128)S(1)}, u32[]{:S(2)}, u32[]{:S(2)}) collective-permute-start(f32[240,128]{1,0:T(8,128)S(1)} %slice_add_fusion.refs_0_), channel_id=1, source_target_pairs={{4,8},{8,4},{12,0},{0,12},{2,6},{6,2},{10,14},{14,10},{5,9},{9,5},... | collective-permute-start | bytes 368648 | tf_op jit(solution)/shard_map/ppermute | solution.py:452
  (6 other events, 67.1 us)

commit v8 on v7

--- a/solution.py
+++ b/solution.py
@@ -185,8 +185,8 @@
     lane = lax.broadcasted_iota(jnp.int32, (units, 128), 1)
     tiles = [jnp.zeros((units, 128), F32)] * (buses // 128)
     for peer in range(peers):
-        spots = column(unit_ref[peer][0:1, :units]).astype(jnp.int32)
-        extrap = column(unit_ref[peer][1:2, :units])
+        spots = column(unit_ref[exchange_place(peer)][0:1, :units]).astype(jnp.int32)
+        extrap = column(unit_ref[exchange_place(peer)][1:2, :units])
         for tile in range(peer * span // 128, ((peer + 1) * span - 1) // 128 + 1):
             tiles[tile] += jnp.where(lane + tile * 128 == spots, extrap, 0.0)
     injection = jnp.concatenate(
@@ -238,7 +238,7 @@
     @pl.when(step == 0)
     def _():
         for peer in range(peers):
-            spots = column(unit_ref[group * peers + peer][0:1, :local]).astype(jnp.int32)
+            spots = column(unit_ref[exchange_place(group * peers + peer)][0:1, :local]).astype(jnp.int32)
             index = lax.broadcasted_iota(jnp.int32, (local, span), 1) + group * span
             pick = jnp.where(index == spots, 1.0, 0.0).astype(BF16)
             pick_ref[peer * local : (peer + 1) * local, :] = pick
@@ -462,7 +462,7 @@
     table, gen, copies = unit_tables(
         block[None], unit_bus, unit_type, unit_limit, unit_cost, line_count
     )
-    unit_rows = lax.all_to_all(copies, LINE, 0, 0, tiled=True)
+    unit_rows = lax.all_to_all(copies, EXCHANGE, 0, 0, tiled=True)
     load, kept = load_flows(ptdf, bus_load)
     mine, other = first_flows(core[None], ptdf, kept, unit_rows, load)
     extrap = far = 2.0 * gen
@@ -480,15 +480,22 @@
     high = low = None
     for iteration in range(ITERS):
         last = iteration == ITERS - 1
-        total = mine + lax.ppermute(other, "c", SWAP)
+        got = lax.ppermute(other, "c", SWAP)
         if iteration == 0:
             state, ramp, store = state_step(place, extrap, far, ramp, store, table, False)
-            total, tied, rows, state = lax.optimization_barrier((total, ptdf, unit_rows, state))
+            total, tied, rows, state = lax.optimization_barrier(
+                (mine + got, ptdf, unit_rows, state)
+            )
+            lefts = [total[start:stop] for start, stop in CHUNKS]
             high, low = unit_columns(tied, rows, line_count * local)
-        elif not last:
-            total, tied = lax.optimization_barrier((total, extrap))
+        elif last:
+            total = mine + got
+            lefts = [total[start:stop] for start, stop in CHUNKS]
+        else:
+            lefts = [mine[start:stop] + got[start:stop] for start, stop in CHUNKS]
+        if 0 < iteration < ITERS - 1:
+            lefts[0], tied = lax.optimization_barrier((lefts[0], extrap))
             far = lax.ppermute(tied, "t", SWAP)
-        lefts = [total[start:stop] for start, stop in CHUNKS]
         lefts = [left + along_y(left, (NEAR, FAR)) for left in lefts]
         if iteration == 0:
             lefts[0], high, low = lax.optimization_barrier((lefts[0], high, low))
@@ -502,9 +509,10 @@
         if iteration == 0:
             rights[-1], high, low = lax.optimization_barrier((rights[-1], high, low))
         if last:
+            rights[-1], gen = lax.optimization_barrier((rights[-1], 0.5 * (extrap + before)))
             (dual,) = dual_step(lefts, rights, flow, dual, steps, limits, 1)
             result = placed(core, dual)
-            return 0.5 * (extrap + before), placed(partner, lax.ppermute(dual, "c", SWAP), result)
+            return gen, placed(partner, lax.ppermute(dual, "c", SWAP), result)
         rights[-1], state, ramp, store = lax.optimization_barrier((rights[-1], state, ramp, store))
         dual, flow = dual_step(lefts, rights, flow, dual, steps, limits, 2)
         prices = unit_prices(core, dual, high, low)

time: 184 us -> 184 us (level)
    ppermute x4 -> x3, starting transfers between devices: 11.6 us -> 9.17 us  [on_device(): lax.ppermute(dual, 'c', SWAP)]
    ppermute x4 -> x5, starting transfers between devices: 11.9 us -> 14.4 us  [the longest x4 11.9 us: on_device(): got = lax.ppermute(other, 'c', SWAP)]
  transfers between devices with their start and end apart: 27 -> 27, of which waited for: 21 -> 22; matrix products, arithmetic and copies ran while one was open for 1% -> 1% of each run, Pallas kernels for 9% -> 9%
where the time goes in v8:
time: 184 us; the launch traced here: 183 us
  blocking collectives  78.2 us (42%)
  starting transfers between devices  51.1 us (28%)
  waiting for transfers between devices  26.6 us (14%)
  Pallas kernels  24.8 us (13%)
    all_to_all x3, blocking collectives, on_device(): changes = lax.all_to_all(copies, EXCHANGE, 0, 0, tiled=True)  39.4 us
    all_to_all x3, blocking collectives, on_device(): prices = lax.all_to_all(prices, EXCHANGE, 0, 0, tiled=True)  38.8 us
    ppermute x16, waiting for transfers between devices, along_y(): return lax.ppermute(value, BUS, pairs)  17.7 us
    ppermute x16, starting transfers between devices, along_y(): return lax.ppermute(value, BUS, pairs)  12.7 us
    ppermute x4, starting transfers between devices, on_device(): got = lax.ppermute(other, 'c', SWAP)  11.9 us
    all_to_all x1, starting transfers between devices, on_device(): unit_rows = lax.all_to_all(copies, EXCHANGE, 0, 0, tiled=True)  10 us
    ppermute x3, starting transfers between devices, on_device(): lax.ppermute(dual, 'c', SWAP)  9.17 us
    pallas_call x2, Pallas kernels, unit_columns(): pl.pallas_call(functools.partial(columns_kernel, group), grid=(ROWS // BL...  5.9 us
  transfers between devices with their start and end apart: 27, of which 22 were waited for; matrix products, arithmetic and copies ran while one was open for 1% of the time, Pallas kernels for 9%

profile of v8, /device:TPU:1, one launch (start us, length us, event | category | flops | bytes accessed | tf_op | source)
XLA Modules:
  0.0 183.2 jit_solution(5710865235715861291)
XLA Ops:
  2.1 10.0 %all-to-all-start = ((f32[16,8,128]{2,1,0:T(8,128)}), f32[16,8,128]{2,1,0:T(8,128)S(1)}, u32[]{:S(2)}, u32[]{:S(2)}) async-start(f32[16,8,128]{2,1,0:T(8,128)} %get-tuple-element.65), calls=%async_computation | async-start | bytes 131072 | tf_op jit(solution)/shard_map/all_to_all | solution.py:465
  12.2 4.7 %load_flows.1 = (f32[992,128]{1,0:T(8,128)S(1)}, f32[320,1536]{1,0:T(8,128)S(1)}) custom-call(f32[960,1536]{1,0:T(8,128)} %ptdf_ref.3, f32[1536,128]{1,0:T(8,128)} %load_ref.1), custom_call_target="tpu_custom_call" | custom-call | flops 1207959552 | bytes 6291456 | tf_op jit(solution)/shard_map/load_flows/pallas_call | solution.py:156
  16.9 2.7 %all-to-all-done.unit_ref = f32[16,8,128]{2,1,0:T(8,128)S(1)} async-done(((f32[16,8,128]{2,1,0:T(8,128)}), f32[16,8,128]{2,1,0:T(8,128)S(1)}, u32[]{:S(2)}, u32[]{:S(2)}) %all-to-all-start) | async-done | bytes 65568 | tf_op jit(solution)/shard_map/all_to_all | solution.py:465
  19.6 2.6 %first_flows.1 = (f32[496,128]{1,0:T(8,128)S(1)}, f32[496,128]{1,0:T(8,128)S(1)}) custom-call(s32[1]{0:T(128)} %bitcast.core_ref.place_ref, f32[960,1536]{1,0:T(8,128)} %ptdf_ref.3, f32[992,128]{1,0:T(8,128)S(1)} %get-tuple-element.63.load_ref, f32[320,1536]{1,0:T(8,128)S(1)} %get-tuple-element.64.kept_ref, f32[16,8,128]{2,1,0:T(8,128)S(1)} %all-to-all-done.unit_ref), custom_call_target="tpu_custom_call" | custom-call | flops 3145728 | bytes 6291456 | tf_op jit(solution)/shard_map/first_flows/pallas_call | solution.py:209
  22.2 2.2 %collective-permute-start = (f32[496,128]{1,0:T(8,128)S(1)}, f32[496,128]{1,0:T(8,128)S(1)}, u32[]{:S(2)}, u32[]{:S(2)}) collective-permute-start(f32[496,128]{1,0:T(8,128)S(1)} %get-tuple-element.67), channel_id=1, source_target_pairs={{0,2},{2,0},{1,3},{3,1},{4,6},{6,4},{5,7},{7,5},{8,10},{10,8},{9,1... | collective-permute-start | bytes 761864 | tf_op jit(solution)/shard_map/ppermute | solution.py:483
  25.6 2.8 %collective-permute-start.3 = (f32[240,128]{1,0:T(8,128)S(1)}, f32[240,128]{1,0:T(8,128)S(1)}, u32[]{:S(2)}, u32[]{:S(2)}) collective-permute-start(f32[240,128]{1,0:T(8,128)S(1)} %slice.37), channel_id=1, source_target_pairs={{0,4},{4,0},{8,12},{12,8},{6,10},{10,6},{14,2},{2,14},{1,5},{5,1},... | collective-permute-start | bytes 368648 | tf_op jit(solution)/shard_map/ppermute | solution.py:452
  28.6 2.9 %unit_columns.2 = (bf16[1024,512]{1,0:T(8,128)(2,1)S(1)}, bf16[1024,512]{1,0:T(8,128)(2,1)S(1)}) custom-call(f32[960,1536]{1,0:T(8,128)} %ptdf_ref.3, f32[16,8,128]{2,1,0:T(8,128)S(1)} %all-to-all-done.unit_ref), custom_call_target="tpu_custom_call" | custom-call | flops 805306368 | bytes 3145728 | tf_op jit(solution)/shard_map/unit_columns/pallas_call | solution.py:258
  33.9 3.0 %unit_columns.3 = (bf16[1024,512]{1,0:T(8,128)(2,1)S(1)}, bf16[1024,512]{1,0:T(8,128)(2,1)S(1)}) custom-call(f32[960,1536]{1,0:T(8,128)} %ptdf_ref.3, f32[16,8,128]{2,1,0:T(8,128)S(1)} %all-to-all-done.unit_ref, bf16[1024,512]{1,0:T(8,128)(2,1)S(1)} %get-tuple-element.76.refs_0_, ...), custom_call_target="tpu_custom_call", output_to_operand_aliasing={{0}: (2, {}), {1}: (3, {})} | custom-call | flops 805306368 | bytes 3145728 | tf_op jit(solution)/shard_map/unit_columns/pallas_call | solution.py:258
  37.8 3.2 %collective-permute-start.5 = (f32[496,128]{1,0:T(8,128)S(1)}, f32[496,128]{1,0:T(8,128)S(1)}, u32[]{:S(2)}, u32[]{:S(2)}) collective-permute-start(f32[496,128]{1,0:T(8,128)S(1)} %get-tuple-element.88.dual_ref.refs_5_), channel_id=1, source_target_pairs={{0,2},{2,0},{1,3},{3,1},{4,6},{6,4},{5,7},{7,5},{8,10},{10,8},{9,1... | collective-permute-start | bytes 761864 | tf_op jit(solution)/shard_map/ppermute | solution.py:519
  42.7 12.8 %all_to_all.35.price_ref = f32[16,32,128]{2,1,0:T(8,128)S(1)} all-to-all(f32[16,32,128]{2,1,0:T(8,128)S(1)} %unit_prices.7), channel_id=1, replica_groups=mesh['z'=8,'xl'=2,'y'=4,'c'=2,'t'=2] {'xl','z'}, dimensions={0} | all-to-all | bytes 524288 | tf_op jit(solution)/shard_map/all_to_all | solution.py:520
  55.6 13.1 %all_to_all.36.extrap_ref = f32[16,32,128]{2,1,0:T(8,128)S(1)} all-to-all(f32[16,32,128]{2,1,0:T(8,128)S(1)} %get-tuple-element.90), channel_id=1, replica_groups=mesh['z'=8,'xl'=2,'y'=4,'c'=2,'t'=2] {'xl','z'}, dimensions={0} | all-to-all | bytes 524288 | tf_op jit(solution)/shard_map/all_to_all | solution.py:526
  69.2 3.2 %collective-permute-start.6 = (f32[496,128]{1,0:T(8,128)S(1)}, f32[496,128]{1,0:T(8,128)S(1)}, u32[]{:S(2)}, u32[]{:S(2)}) collective-permute-start(f32[496,128]{1,0:T(8,128)S(1)} %unit_flows.7), channel_id=1, source_target_pairs={{0,2},{2,0},{1,3},{3,1},{4,6},{6,4},{5,7},{7,5},{8,10},{10,8},{9,1... | collective-permute-start | bytes 761864 | tf_op jit(solution)/shard_map/ppermute | solution.py:483
  76.4 2.5 %collective-permute-start.8 = (f32[32,128]{1,0:T(8,128)S(1)}, f32[32,128]{1,0:T(8,128)S(1)}, u32[]{:S(2)}, u32[]{:S(2)}) collective-permute-start(f32[32,128]{1,0:T(8,128)S(1)} %get-tuple-element.93.own_ref.old_ref), channel_id=1, source_target_pairs={{0,1},{1,0},{2,3},{3,2},{4,5},{5,4},{6,7},{7,6},{8,9},{9,8},{10,11... | collective-permute-start | bytes 49160 | tf_op jit(solution)/shard_map/ppermute | solution.py:498
  84.9 3.0 %collective-permute-start.12 = (f32[496,128]{1,0:T(8,128)S(1)}, f32[496,128]{1,0:T(8,128)S(1)}, u32[]{:S(2)}, u32[]{:S(2)}) collective-permute-start(f32[496,128]{1,0:T(8,128)S(1)} %get-tuple-element.103.dual_ref.refs_5_), channel_id=1, source_target_pairs={{0,2},{2,0},{1,3},{3,1},{4,6},{6,4},{5,7},{7,5},{8,10},{10,8},{9,1... | collective-permute-start | bytes 761864 | tf_op jit(solution)/shard_map/ppermute | solution.py:519
  89.6 13.0 %all_to_all.37.price_ref = f32[16,32,128]{2,1,0:T(8,128)S(1)} all-to-all(f32[16,32,128]{2,1,0:T(8,128)S(1)} %unit_prices.9), channel_id=1, replica_groups=mesh['z'=8,'xl'=2,'y'=4,'c'=2,'t'=2] {'xl','z'}, dimensions={0} | all-to-all | bytes 524288 | tf_op jit(solution)/shard_map/all_to_all | solution.py:520
  102.7 13.1 %all_to_all.38.extrap_ref = f32[16,32,128]{2,1,0:T(8,128)S(1)} all-to-all(f32[16,32,128]{2,1,0:T(8,128)S(1)} %get-tuple-element.106), channel_id=1, replica_groups=mesh['z'=8,'xl'=2,'y'=4,'c'=2,'t'=2] {'xl','z'}, dimensions={0} | all-to-all | bytes 524288 | tf_op jit(solution)/shard_map/all_to_all | solution.py:526
  116.3 3.2 %collective-permute-start.13 = (f32[496,128]{1,0:T(8,128)S(1)}, f32[496,128]{1,0:T(8,128)S(1)}, u32[]{:S(2)}, u32[]{:S(2)}) collective-permute-start(f32[496,128]{1,0:T(8,128)S(1)} %unit_flows.9), channel_id=1, source_target_pairs={{0,2},{2,0},{1,3},{3,1},{4,6},{6,4},{5,7},{7,5},{8,10},{10,8},{9,1... | collective-permute-start | bytes 761864 | tf_op jit(solution)/shard_map/ppermute | solution.py:483
  123.5 2.5 %collective-permute-start.15 = (f32[32,128]{1,0:T(8,128)S(1)}, f32[32,128]{1,0:T(8,128)S(1)}, u32[]{:S(2)}, u32[]{:S(2)}) collective-permute-start(f32[32,128]{1,0:T(8,128)S(1)} %get-tuple-element.109.own_ref.old_ref), channel_id=1, source_target_pairs={{0,1},{1,0},{2,3},{3,2},{4,5},{5,4},{6,7},{7,6},{8,9},{9,8},{10,11... | collective-permute-start | bytes 49160 | tf_op jit(solution)/shard_map/ppermute | solution.py:498
  131.9 3.0 %collective-permute-start.19 = (f32[496,128]{1,0:T(8,128)S(1)}, f32[496,128]{1,0:T(8,128)S(1)}, u32[]{:S(2)}, u32[]{:S(2)}) collective-permute-start(f32[496,128]{1,0:T(8,128)S(1)} %get-tuple-element.116.dual_ref.refs_5_), channel_id=1, source_target_pairs={{0,2},{2,0},{1,3},{3,1},{4,6},{6,4},{5,7},{7,5},{8,10},{10,8},{9,1... | collective-permute-start | bytes 761864 | tf_op jit(solution)/shard_map/ppermute | solution.py:519
  136.6 13.0 %all_to_all.39.price_ref = f32[16,32,128]{2,1,0:T(8,128)S(1)} all-to-all(f32[16,32,128]{2,1,0:T(8,128)S(1)} %unit_prices.11), channel_id=1, replica_groups=mesh['z'=8,'xl'=2,'y'=4,'c'=2,'t'=2] {'xl','z'}, dimensions={0} | all-to-all | bytes 524288 | tf_op jit(solution)/shard_map/all_to_all | solution.py:520
  149.8 13.1 %all_to_all.40.extrap_ref = f32[16,32,128]{2,1,0:T(8,128)S(1)} all-to-all(f32[16,32,128]{2,1,0:T(8,128)S(1)} %get-tuple-element.119), channel_id=1, replica_groups=mesh['z'=8,'xl'=2,'y'=4,'c'=2,'t'=2] {'xl','z'}, dimensions={0} | all-to-all | bytes 524288 | tf_op jit(solution)/shard_map/all_to_all | solution.py:526
  163.3 3.2 %collective-permute-start.20 = (f32[496,128]{1,0:T(8,128)S(1)}, f32[496,128]{1,0:T(8,128)S(1)}, u32[]{:S(2)}, u32[]{:S(2)}) collective-permute-start(f32[496,128]{1,0:T(8,128)S(1)} %unit_flows.11), channel_id=1, source_target_pairs={{0,2},{2,0},{1,3},{3,1},{4,6},{6,4},{5,7},{7,5},{8,10},{10,8},{9,1... | collective-permute-start | bytes 761864 | tf_op jit(solution)/shard_map/ppermute | solution.py:483
  175.1 3.3 %collective-permute-done.22.refs_3_ = f32[256,128]{1,0:T(8,128)S(1)} collective-permute-done((f32[256,128]{1,0:T(8,128)S(1)}, f32[256,128]{1,0:T(8,128)S(1)}, u32[]{:S(2)}, u32[]{:S(2)}) %collective-permute-start.22) | collective-permute-done | bytes 131104 | tf_op jit(solution)/shard_map/ppermute | solution.py:452
  178.7 2.5 %collective-permute-start.25 = (f32[496,128]{1,0:T(8,128)S(1)}, f32[496,128]{1,0:T(8,128)S(1)}, u32[]{:S(2)}, u32[]{:S(2)}) collective-permute-start(f32[496,128]{1,0:T(8,128)S(1)} %dual_step.7.half_ref), channel_id=1, source_target_pairs={{0,2},{2,0},{1,3},{3,1},{4,6},{6,4},{5,7},{7,5},{8,10},{10,8},{9,1... | collective-permute-start | bytes 761864 | tf_op jit(solution)/shard_map/ppermute | solution.py:515
  (97 shorter events, 43.3 us)
Async XLA Ops:
  2.1 17.4 %all-to-all-start = ((f32[16,8,128]{2,1,0:T(8,128)}), f32[16,8,128]{2,1,0:T(8,128)S(1)}, u32[]{:S(2)}, u32[]{:S(2)}) async-start(f32[16,8,128]{2,1,0:T(8,128)} %get-tuple-element.65), calls=%async_computation | async-start | bytes 131072 | tf_op jit(solution)/shard_map/all_to_all | solution.py:465
  25.6 6.0 %collective-permute-start.3 = (f32[240,128]{1,0:T(8,128)S(1)}, f32[240,128]{1,0:T(8,128)S(1)}, u32[]{:S(2)}, u32[]{:S(2)}) collective-permute-start(f32[240,128]{1,0:T(8,128)S(1)} %slice.37), channel_id=1, source_target_pairs={{0,4},{4,0},{8,12},{12,8},{6,10},{10,6},{14,2},{2,14},{1,5},{5,1},... | collective-permute-start | bytes 368648 | tf_op jit(solution)/shard_map/ppermute | solution.py:452
  28.5 5.1 %collective-permute-start.1 = (f32[256,128]{1,0:T(8,128)S(1)}, f32[256,128]{1,0:T(8,128)S(1)}, u32[]{:S(2)}, u32[]{:S(2)}) collective-permute-start(f32[256,128]{1,0:T(8,128)S(1)} %slice.36), channel_id=1, source_target_pairs={{0,4},{4,0},{8,12},{12,8},{6,10},{10,6},{14,2},{2,14},{1,5},{5,1},... | collective-permute-start | bytes 393224 | tf_op jit(solution)/shard_map/ppermute | solution.py:452
  31.6 6.0 %collective-permute-start.4 = (f32[240,128]{1,0:T(8,128)S(1)}, f32[240,128]{1,0:T(8,128)S(1)}, u32[]{:S(2)}, u32[]{:S(2)}) collective-permute-start(f32[240,128]{1,0:T(8,128)S(1)} %slice_add_fusion.5.refs_0_), channel_id=1, source_target_pairs={{4,8},{8,4},{12,0},{0,12},{2,6},{6,2},{10,14},{14,10},{5,9},{9,5},... | collective-permute-start | bytes 368648 | tf_op jit(solution)/shard_map/ppermute | solution.py:452
  37.8 4.3 %collective-permute-start.5 = (f32[496,128]{1,0:T(8,128)S(1)}, f32[496,128]{1,0:T(8,128)S(1)}, u32[]{:S(2)}, u32[]{:S(2)}) collective-permute-start(f32[496,128]{1,0:T(8,128)S(1)} %get-tuple-element.88.dual_ref.refs_5_), channel_id=1, source_target_pairs={{0,2},{2,0},{1,3},{3,1},{4,6},{6,4},{5,7},{7,5},{8,10},{10,8},{9,1... | collective-permute-start | bytes 761864 | tf_op jit(solution)/shard_map/ppermute | solution.py:519
  69.2 4.4 %collective-permute-start.6 = (f32[496,128]{1,0:T(8,128)S(1)}, f32[496,128]{1,0:T(8,128)S(1)}, u32[]{:S(2)}, u32[]{:S(2)}) collective-permute-start(f32[496,128]{1,0:T(8,128)S(1)} %unit_flows.7), channel_id=1, source_target_pairs={{0,2},{2,0},{1,3},{3,1},{4,6},{6,4},{5,7},{7,5},{8,10},{10,8},{9,1... | collective-permute-start | bytes 761864 | tf_op jit(solution)/shard_map/ppermute | solution.py:483
  73.6 5.3 %collective-permute-start.9 = (f32[256,128]{1,0:T(8,128)S(1)}, f32[256,128]{1,0:T(8,128)S(1)}, u32[]{:S(2)}, u32[]{:S(2)}) collective-permute-start(f32[256,128]{1,0:T(8,128)S(1)} %slice_add_fusion.1), channel_id=1, source_target_pairs={{0,4},{4,0},{8,12},{12,8},{6,10},{10,6},{14,2},{2,14},{1,5},{5,1},... | collective-permute-start | bytes 393224 | tf_op jit(solution)/shard_map/ppermute | solution.py:452
  74.6 5.4 %collective-permute-start.7 = (f32[240,128]{1,0:T(8,128)S(1)}, f32[240,128]{1,0:T(8,128)S(1)}, u32[]{:S(2)}, u32[]{:S(2)}) collective-permute-start(f32[240,128]{1,0:T(8,128)S(1)} %slice_add_fusion.3), channel_id=1, source_target_pairs={{0,4},{4,0},{8,12},{12,8},{6,10},{10,6},{14,2},{2,14},{1,5},{5,1},... | collective-permute-start | bytes 368648 | tf_op jit(solution)/shard_map/ppermute | solution.py:452
  76.4 4.1 %collective-permute-start.8 = (f32[32,128]{1,0:T(8,128)S(1)}, f32[32,128]{1,0:T(8,128)S(1)}, u32[]{:S(2)}, u32[]{:S(2)}) collective-permute-start(f32[32,128]{1,0:T(8,128)S(1)} %get-tuple-element.93.own_ref.old_ref), channel_id=1, source_target_pairs={{0,1},{1,0},{2,3},{3,2},{4,5},{5,4},{6,7},{7,6},{8,9},{9,8},{10,11... | collective-permute-start | bytes 49160 | tf_op jit(solution)/shard_map/ppermute | solution.py:498
  78.9 4.1 %collective-permute-start.11 = (f32[256,128]{1,0:T(8,128)S(1)}, f32[256,128]{1,0:T(8,128)S(1)}, u32[]{:S(2)}, u32[]{:S(2)}) collective-permute-start(f32[256,128]{1,0:T(8,128)S(1)} %add.76.refs_1_), channel_id=1, source_target_pairs={{4,8},{8,4},{12,0},{0,12},{2,6},{6,2},{10,14},{14,10},{5,9},{9,5},... | collective-permute-start | bytes 393224 | tf_op jit(solution)/shard_map/ppermute | solution.py:452
  80.5 4.1 %collective-permute-start.10 = (f32[240,128]{1,0:T(8,128)S(1)}, f32[240,128]{1,0:T(8,128)S(1)}, u32[]{:S(2)}, u32[]{:S(2)}) collective-permute-start(f32[240,128]{1,0:T(8,128)S(1)} %add.74.refs_0_), channel_id=1, source_target_pairs={{4,8},{8,4},{12,0},{0,12},{2,6},{6,2},{10,14},{14,10},{5,9},{9,5},... | collective-permute-start | bytes 368648 | tf_op jit(solution)/shard_map/ppermute | solution.py:452
  84.9 4.1 %collective-permute-start.12 = (f32[496,128]{1,0:T(8,128)S(1)}, f32[496,128]{1,0:T(8,128)S(1)}, u32[]{:S(2)}, u32[]{:S(2)}) collective-permute-start(f32[496,128]{1,0:T(8,128)S(1)} %get-tuple-element.103.dual_ref.refs_5_), channel_id=1, source_target_pairs={{0,2},{2,0},{1,3},{3,1},{4,6},{6,4},{5,7},{7,5},{8,10},{10,8},{9,1... | collective-permute-start | bytes 761864 | tf_op jit(solution)/shard_map/ppermute | solution.py:519
  116.3 4.4 %collective-permute-start.13 = (f32[496,128]{1,0:T(8,128)S(1)}, f32[496,128]{1,0:T(8,128)S(1)}, u32[]{:S(2)}, u32[]{:S(2)}) collective-permute-start(f32[496,128]{1,0:T(8,128)S(1)} %unit_flows.9), channel_id=1, source_target_pairs={{0,2},{2,0},{1,3},{3,1},{4,6},{6,4},{5,7},{7,5},{8,10},{10,8},{9,1... | collective-permute-start | bytes 761864 | tf_op jit(solution)/shard_map/ppermute | solution.py:483
  120.7 5.3 %collective-permute-start.16 = (f32[256,128]{1,0:T(8,128)S(1)}, f32[256,128]{1,0:T(8,128)S(1)}, u32[]{:S(2)}, u32[]{:S(2)}) collective-permute-start(f32[256,128]{1,0:T(8,128)S(1)} %slice_add_fusion), channel_id=1, source_target_pairs={{0,4},{4,0},{8,12},{12,8},{6,10},{10,6},{14,2},{2,14},{1,5},{5,1},... | collective-permute-start | bytes 393224 | tf_op jit(solution)/shard_map/ppermute | solution.py:452
  121.7 5.4 %collective-permute-start.14 = (f32[240,128]{1,0:T(8,128)S(1)}, f32[240,128]{1,0:T(8,128)S(1)}, u32[]{:S(2)}, u32[]{:S(2)}) collective-permute-start(f32[240,128]{1,0:T(8,128)S(1)} %slice_add_fusion.2), channel_id=1, source_target_pairs={{0,4},{4,0},{8,12},{12,8},{6,10},{10,6},{14,2},{2,14},{1,5},{5,1},... | collective-permute-start | bytes 368648 | tf_op jit(solution)/shard_map/ppermute | solution.py:452
  123.5 4.1 %collective-permute-start.15 = (f32[32,128]{1,0:T(8,128)S(1)}, f32[32,128]{1,0:T(8,128)S(1)}, u32[]{:S(2)}, u32[]{:S(2)}) collective-permute-start(f32[32,128]{1,0:T(8,128)S(1)} %get-tuple-element.109.own_ref.old_ref), channel_id=1, source_target_pairs={{0,1},{1,0},{2,3},{3,2},{4,5},{5,4},{6,7},{7,6},{8,9},{9,8},{10,11... | collective-permute-start | bytes 49160 | tf_op jit(solution)/shard_map/ppermute | solution.py:498
  126.0 3.9 %collective-permute-start.18 = (f32[256,128]{1,0:T(8,128)S(1)}, f32[256,128]{1,0:T(8,128)S(1)}, u32[]{:S(2)}, u32[]{:S(2)}) collective-permute-start(f32[256,128]{1,0:T(8,128)S(1)} %add.80.refs_1_), channel_id=1, source_target_pairs={{4,8},{8,4},{12,0},{0,12},{2,6},{6,2},{10,14},{14,10},{5,9},{9,5},... | collective-permute-start | bytes 393224 | tf_op jit(solution)/shard_map/ppermute | solution.py:452
  127.6 4.0 %collective-permute-start.17 = (f32[240,128]{1,0:T(8,128)S(1)}, f32[240,128]{1,0:T(8,128)S(1)}, u32[]{:S(2)}, u32[]{:S(2)}) collective-permute-start(f32[240,128]{1,0:T(8,128)S(1)} %add.78.refs_0_), channel_id=1, source_target_pairs={{4,8},{8,4},{12,0},{0,12},{2,6},{6,2},{10,14},{14,10},{5,9},{9,5},... | collective-permute-start | bytes 368648 | tf_op jit(solution)/shard_map/ppermute | solution.py:452
  131.9 4.2 %collective-permute-start.19 = (f32[496,128]{1,0:T(8,128)S(1)}, f32[496,128]{1,0:T(8,128)S(1)}, u32[]{:S(2)}, u32[]{:S(2)}) collective-permute-start(f32[496,128]{1,0:T(8,128)S(1)} %get-tuple-element.116.dual_ref.refs_5_), channel_id=1, source_target_pairs={{0,2},{2,0},{1,3},{3,1},{4,6},{6,4},{5,7},{7,5},{8,10},{10,8},{9,1... | collective-permute-start | bytes 761864 | tf_op jit(solution)/shard_map/ppermute | solution.py:519
  163.3 4.4 %collective-permute-start.20 = (f32[496,128]{1,0:T(8,128)S(1)}, f32[496,128]{1,0:T(8,128)S(1)}, u32[]{:S(2)}, u32[]{:S(2)}) collective-permute-start(f32[496,128]{1,0:T(8,128)S(1)} %unit_flows.11), channel_id=1, source_target_pairs={{0,2},{2,0},{1,3},{3,1},{4,6},{6,4},{5,7},{7,5},{8,10},{10,8},{9,1... | collective-permute-start | bytes 761864 | tf_op jit(solution)/shard_map/ppermute | solution.py:483
  167.8 5.0 %collective-permute-start.23 = (f32[240,128]{1,0:T(8,128)S(1)}, f32[240,128]{1,0:T(8,128)S(1)}, u32[]{:S(2)}, u32[]{:S(2)}) collective-permute-start(f32[240,128]{1,0:T(8,128)S(1)} %slice.57), channel_id=1, source_target_pairs={{0,4},{4,0},{8,12},{12,8},{6,10},{10,6},{14,2},{2,14},{1,5},{5,1},... | collective-permute-start | bytes 368648 | tf_op jit(solution)/shard_map/ppermute | solution.py:452
  168.8 5.4 %collective-permute-start.21 = (f32[256,128]{1,0:T(8,128)S(1)}, f32[256,128]{1,0:T(8,128)S(1)}, u32[]{:S(2)}, u32[]{:S(2)}) collective-permute-start(f32[256,128]{1,0:T(8,128)S(1)} %slice.56), channel_id=1, source_target_pairs={{0,4},{4,0},{8,12},{12,8},{6,10},{10,6},{14,2},{2,14},{1,5},{5,1},... | collective-permute-start | bytes 393224 | tf_op jit(solution)/shard_map/ppermute | solution.py:452
  172.8 5.6 %collective-permute-start.24 = (f32[240,128]{1,0:T(8,128)S(1)}, f32[240,128]{1,0:T(8,128)S(1)}, u32[]{:S(2)}, u32[]{:S(2)}) collective-permute-start(f32[240,128]{1,0:T(8,128)S(1)} %slice_add_fusion.4.refs_0_), channel_id=1, source_target_pairs={{4,8},{8,4},{12,0},{0,12},{2,6},{6,2},{10,14},{14,10},{5,9},{9,5},... | collective-permute-start | bytes 368648 | tf_op jit(solution)/shard_map/ppermute | solution.py:452
  174.2 4.2 %collective-permute-start.22 = (f32[256,128]{1,0:T(8,128)S(1)}, f32[256,128]{1,0:T(8,128)S(1)}, u32[]{:S(2)}, u32[]{:S(2)}) collective-permute-start(f32[256,128]{1,0:T(8,128)S(1)} %slice_add_fusion.6.refs_1_), channel_id=1, source_target_pairs={{4,8},{8,4},{12,0},{0,12},{2,6},{6,2},{10,14},{14,10},{5,9},{9,5},... | collective-permute-start | bytes 393224 | tf_op jit(solution)/shard_map/ppermute | solution.py:452
  (6 other events, 66.9 us)

commit v9 on v8

--- a/solution.py
+++ b/solution.py
@@ -74,7 +74,7 @@
 
 def table_kernel(
     place_ref, bus_in, type_in, limit_in, cost_in, table_ref, first_ref, copies_ref,
-    bus_ref, type_ref, limit_ref, cost_ref, arrived
+    bus_ref, type_ref, limit_ref, cost_ref, send_ref, rows_ref, arrived
 ):
     pairs = (
         (bus_in, bus_ref.at[0]),
@@ -87,25 +87,24 @@
         copy.start()
     for copy in copies:
         copy.wait()
-    kinds = column(type_ref[...])
-    capacity = column(limit_ref[...]).astype(F32) / 100.0
-    cost = column(cost_ref[...]) * picked(kinds, COST_FACTORS)
+    kinds = type_ref[...]
+    capacity = limit_ref[...].astype(F32) / 100.0
+    cost = cost_ref[...] * picked(kinds, COST_FACTORS)
     storage = jnp.where(kinds == 3, 1.0, 0.0)
     lower = -capacity * storage
-    lane = lax.broadcasted_iota(jnp.int32, table_ref.shape, 1)
-    table = jnp.zeros(table_ref.shape, F32)
-    parts = (cost, lower, capacity, picked(kinds, RAMP_RATES) * capacity, storage, 2.0 * capacity)
-    for spot, part in enumerate(parts):
-        table = jnp.where(lane == spot, part, table)
+    first = jnp.clip(-PRIMAL_STEP * cost, lower, capacity)
+    ramp = picked(kinds, RAMP_RATES) * capacity
+    units = kinds.shape[1]
+    send_ref[...] = jnp.zeros(send_ref.shape, F32)
+    send_ref[0:1, :units] = (bus_ref[...] - place_ref[0]).astype(F32)
+    send_ref[1:2, :units] = 2.0 * first
+    copies_ref[...] = jnp.broadcast_to(send_ref[...][None], copies_ref.shape)
+    rows_ref[...] = jnp.zeros(rows_ref.shape, F32)
+    for spot, part in enumerate((cost, lower, capacity, ramp, storage, 2.0 * capacity, first)):
+        rows_ref[spot : spot + 1, :units] = part
+    table = rows_ref[...].T[:units]
     table_ref[...] = table
-    first = jnp.clip(-PRIMAL_STEP * cost, lower, capacity)
-    first_ref[...] = jnp.broadcast_to(first, first_ref.shape)
-    bus = column(bus_ref[...] - place_ref[0]).astype(F32)
-    same = lane == lax.broadcasted_iota(jnp.int32, table_ref.shape, 0)
-    bus = jnp.sum(jnp.where(same, bus, 0.0), axis=0, keepdims=True)
-    extrap = jnp.sum(jnp.where(same, 2.0 * first, 0.0), axis=0, keepdims=True)
-    sent = jnp.where(lax.broadcasted_iota(jnp.int32, (8, 128), 0) == 0, bus, extrap)
-    copies_ref[...] = jnp.broadcast_to(sent[None], copies_ref.shape)
+    first_ref[...] = jnp.broadcast_to(table[:, 6:7], first_ref.shape)
 
 
 def unit_tables(place, unit_bus, unit_type, unit_limit, unit_cost, line_count):
@@ -122,7 +121,7 @@
             jax.ShapeDtypeStruct((line_count, 8, 128), F32),
         ],
         scratch_shapes=[pltpu.VMEM((1, units), row.dtype) for row in rows]
-        + [pltpu.SemaphoreType.DMA((4,))],
+        + [pltpu.VMEM((8, 128), F32), pltpu.VMEM((128, 128), F32), pltpu.SemaphoreType.DMA((4,))],
         compiler_params=params(16),
         name="unit_tables",
     )(place, *(pltpu.with_memory_space_constraint(x, pltpu.HBM) for x in rows))

time: 184 us -> 184 us (level)
  no operation moved by 1% of the time
where the time goes in v9:
time: 184 us; the launch traced here: 183 us
  blocking collectives  78.2 us (42%)
  starting transfers between devices  51.1 us (28%)
  waiting for transfers between devices  26.6 us (14%)
  Pallas kernels  24.6 us (13%)
    all_to_all x3, blocking collectives, on_device(): changes = lax.all_to_all(copies, EXCHANGE, 0, 0, tiled=True)  39.4 us
    all_to_all x3, blocking collectives, on_device(): prices = lax.all_to_all(prices, EXCHANGE, 0, 0, tiled=True)  38.8 us
    ppermute x16, waiting for transfers between devices, along_y(): return lax.ppermute(value, BUS, pairs)  17.7 us
    ppermute x16, starting transfers between devices, along_y(): return lax.ppermute(value, BUS, pairs)  12.7 us
    ppermute x4, starting transfers between devices, on_device(): got = lax.ppermute(other, 'c', SWAP)  11.9 us
    all_to_all x1, starting transfers between devices, on_device(): unit_rows = lax.all_to_all(copies, EXCHANGE, 0, 0, tiled=True)  10 us
    ppermute x3, starting transfers between devices, on_device(): lax.ppermute(dual, 'c', SWAP)  9.17 us
    pallas_call x2, Pallas kernels, unit_columns(): pl.pallas_call(functools.partial(columns_kernel, group), grid=(ROWS // BL...  5.9 us
  transfers between devices with their start and end apart: 27, of which 22 were waited for; matrix products, arithmetic and copies ran while one was open for 1% of the time, Pallas kernels for 9%

profile of v9, /device:TPU:1, one launch (start us, length us, event | category | flops | bytes accessed | tf_op | source)
XLA Modules:
  0.0 183.1 jit_solution(16344737661369062887)
XLA Ops:
  2.0 10.0 %all-to-all-start = ((f32[16,8,128]{2,1,0:T(8,128)}), f32[16,8,128]{2,1,0:T(8,128)S(1)}, u32[]{:S(2)}, u32[]{:S(2)}) async-start(f32[16,8,128]{2,1,0:T(8,128)} %get-tuple-element.65), calls=%async_computation | async-start | bytes 131072 | tf_op jit(solution)/shard_map/all_to_all | solution.py:464
  12.1 4.7 %load_flows.1 = (f32[992,128]{1,0:T(8,128)S(1)}, f32[320,1536]{1,0:T(8,128)S(1)}) custom-call(f32[960,1536]{1,0:T(8,128)} %ptdf_ref.3, f32[1536,128]{1,0:T(8,128)} %load_ref.1), custom_call_target="tpu_custom_call" | custom-call | flops 1207959552 | bytes 6291456 | tf_op jit(solution)/shard_map/load_flows/pallas_call | solution.py:155
  16.8 2.7 %all-to-all-done.unit_ref = f32[16,8,128]{2,1,0:T(8,128)S(1)} async-done(((f32[16,8,128]{2,1,0:T(8,128)}), f32[16,8,128]{2,1,0:T(8,128)S(1)}, u32[]{:S(2)}, u32[]{:S(2)}) %all-to-all-start) | async-done | bytes 65568 | tf_op jit(solution)/shard_map/all_to_all | solution.py:464
  19.5 2.6 %first_flows.1 = (f32[496,128]{1,0:T(8,128)S(1)}, f32[496,128]{1,0:T(8,128)S(1)}) custom-call(s32[1]{0:T(128)} %bitcast.core_ref.place_ref, f32[960,1536]{1,0:T(8,128)} %ptdf_ref.3, f32[992,128]{1,0:T(8,128)S(1)} %get-tuple-element.63.load_ref, f32[320,1536]{1,0:T(8,128)S(1)} %get-tuple-element.64.kept_ref, f32[16,8,128]{2,1,0:T(8,128)S(1)} %all-to-all-done.unit_ref), custom_call_target="tpu_custom_call" | custom-call | flops 3145728 | bytes 6291456 | tf_op jit(solution)/shard_map/first_flows/pallas_call | solution.py:208
  22.1 2.2 %collective-permute-start = (f32[496,128]{1,0:T(8,128)S(1)}, f32[496,128]{1,0:T(8,128)S(1)}, u32[]{:S(2)}, u32[]{:S(2)}) collective-permute-start(f32[496,128]{1,0:T(8,128)S(1)} %get-tuple-element.67), channel_id=1, source_target_pairs={{0,2},{2,0},{1,3},{3,1},{4,6},{6,4},{5,7},{7,5},{8,10},{10,8},{9,1... | collective-permute-start | bytes 761864 | tf_op jit(solution)/shard_map/ppermute | solution.py:482
  25.5 2.8 %collective-permute-start.3 = (f32[240,128]{1,0:T(8,128)S(1)}, f32[240,128]{1,0:T(8,128)S(1)}, u32[]{:S(2)}, u32[]{:S(2)}) collective-permute-start(f32[240,128]{1,0:T(8,128)S(1)} %slice.37), channel_id=1, source_target_pairs={{0,4},{4,0},{8,12},{12,8},{6,10},{10,6},{14,2},{2,14},{1,5},{5,1},... | collective-permute-start | bytes 368648 | tf_op jit(solution)/shard_map/ppermute | solution.py:451
  28.5 2.9 %unit_columns.2 = (bf16[1024,512]{1,0:T(8,128)(2,1)S(1)}, bf16[1024,512]{1,0:T(8,128)(2,1)S(1)}) custom-call(f32[960,1536]{1,0:T(8,128)} %ptdf_ref.3, f32[16,8,128]{2,1,0:T(8,128)S(1)} %all-to-all-done.unit_ref), custom_call_target="tpu_custom_call" | custom-call | flops 805306368 | bytes 3145728 | tf_op jit(solution)/shard_map/unit_columns/pallas_call | solution.py:257
  33.8 3.0 %unit_columns.3 = (bf16[1024,512]{1,0:T(8,128)(2,1)S(1)}, bf16[1024,512]{1,0:T(8,128)(2,1)S(1)}) custom-call(f32[960,1536]{1,0:T(8,128)} %ptdf_ref.3, f32[16,8,128]{2,1,0:T(8,128)S(1)} %all-to-all-done.unit_ref, bf16[1024,512]{1,0:T(8,128)(2,1)S(1)} %get-tuple-element.76.refs_0_, ...), custom_call_target="tpu_custom_call", output_to_operand_aliasing={{0}: (2, {}), {1}: (3, {})} | custom-call | flops 805306368 | bytes 3145728 | tf_op jit(solution)/shard_map/unit_columns/pallas_call | solution.py:257
  37.7 3.2 %collective-permute-start.5 = (f32[496,128]{1,0:T(8,128)S(1)}, f32[496,128]{1,0:T(8,128)S(1)}, u32[]{:S(2)}, u32[]{:S(2)}) collective-permute-start(f32[496,128]{1,0:T(8,128)S(1)} %get-tuple-element.88.dual_ref.refs_5_), channel_id=1, source_target_pairs={{0,2},{2,0},{1,3},{3,1},{4,6},{6,4},{5,7},{7,5},{8,10},{10,8},{9,1... | collective-permute-start | bytes 761864 | tf_op jit(solution)/shard_map/ppermute | solution.py:518
  42.6 12.8 %all_to_all.35.price_ref = f32[16,32,128]{2,1,0:T(8,128)S(1)} all-to-all(f32[16,32,128]{2,1,0:T(8,128)S(1)} %unit_prices.7), channel_id=1, replica_groups=mesh['z'=8,'xl'=2,'y'=4,'c'=2,'t'=2] {'xl','z'}, dimensions={0} | all-to-all | bytes 524288 | tf_op jit(solution)/shard_map/all_to_all | solution.py:519
  55.5 13.1 %all_to_all.36.extrap_ref = f32[16,32,128]{2,1,0:T(8,128)S(1)} all-to-all(f32[16,32,128]{2,1,0:T(8,128)S(1)} %get-tuple-element.90), channel_id=1, replica_groups=mesh['z'=8,'xl'=2,'y'=4,'c'=2,'t'=2] {'xl','z'}, dimensions={0} | all-to-all | bytes 524288 | tf_op jit(solution)/shard_map/all_to_all | solution.py:525
  69.1 3.2 %collective-permute-start.6 = (f32[496,128]{1,0:T(8,128)S(1)}, f32[496,128]{1,0:T(8,128)S(1)}, u32[]{:S(2)}, u32[]{:S(2)}) collective-permute-start(f32[496,128]{1,0:T(8,128)S(1)} %unit_flows.7), channel_id=1, source_target_pairs={{0,2},{2,0},{1,3},{3,1},{4,6},{6,4},{5,7},{7,5},{8,10},{10,8},{9,1... | collective-permute-start | bytes 761864 | tf_op jit(solution)/shard_map/ppermute | solution.py:482
  76.3 2.5 %collective-permute-start.8 = (f32[32,128]{1,0:T(8,128)S(1)}, f32[32,128]{1,0:T(8,128)S(1)}, u32[]{:S(2)}, u32[]{:S(2)}) collective-permute-start(f32[32,128]{1,0:T(8,128)S(1)} %get-tuple-element.93.own_ref.old_ref), channel_id=1, source_target_pairs={{0,1},{1,0},{2,3},{3,2},{4,5},{5,4},{6,7},{7,6},{8,9},{9,8},{10,11... | collective-permute-start | bytes 49160 | tf_op jit(solution)/shard_map/ppermute | solution.py:497
  84.8 3.0 %collective-permute-start.12 = (f32[496,128]{1,0:T(8,128)S(1)}, f32[496,128]{1,0:T(8,128)S(1)}, u32[]{:S(2)}, u32[]{:S(2)}) collective-permute-start(f32[496,128]{1,0:T(8,128)S(1)} %get-tuple-element.103.dual_ref.refs_5_), channel_id=1, source_target_pairs={{0,2},{2,0},{1,3},{3,1},{4,6},{6,4},{5,7},{7,5},{8,10},{10,8},{9,1... | collective-permute-start | bytes 761864 | tf_op jit(solution)/shard_map/ppermute | solution.py:518
  89.4 13.0 %all_to_all.37.price_ref = f32[16,32,128]{2,1,0:T(8,128)S(1)} all-to-all(f32[16,32,128]{2,1,0:T(8,128)S(1)} %unit_prices.9), channel_id=1, replica_groups=mesh['z'=8,'xl'=2,'y'=4,'c'=2,'t'=2] {'xl','z'}, dimensions={0} | all-to-all | bytes 524288 | tf_op jit(solution)/shard_map/all_to_all | solution.py:519
  102.6 13.1 %all_to_all.38.extrap_ref = f32[16,32,128]{2,1,0:T(8,128)S(1)} all-to-all(f32[16,32,128]{2,1,0:T(8,128)S(1)} %get-tuple-element.106), channel_id=1, replica_groups=mesh['z'=8,'xl'=2,'y'=4,'c'=2,'t'=2] {'xl','z'}, dimensions={0} | all-to-all | bytes 524288 | tf_op jit(solution)/shard_map/all_to_all | solution.py:525
  116.1 3.2 %collective-permute-start.13 = (f32[496,128]{1,0:T(8,128)S(1)}, f32[496,128]{1,0:T(8,128)S(1)}, u32[]{:S(2)}, u32[]{:S(2)}) collective-permute-start(f32[496,128]{1,0:T(8,128)S(1)} %unit_flows.9), channel_id=1, source_target_pairs={{0,2},{2,0},{1,3},{3,1},{4,6},{6,4},{5,7},{7,5},{8,10},{10,8},{9,1... | collective-permute-start | bytes 761864 | tf_op jit(solution)/shard_map/ppermute | solution.py:482
  123.4 2.4 %collective-permute-start.15 = (f32[32,128]{1,0:T(8,128)S(1)}, f32[32,128]{1,0:T(8,128)S(1)}, u32[]{:S(2)}, u32[]{:S(2)}) collective-permute-start(f32[32,128]{1,0:T(8,128)S(1)} %get-tuple-element.109.own_ref.old_ref), channel_id=1, source_target_pairs={{0,1},{1,0},{2,3},{3,2},{4,5},{5,4},{6,7},{7,6},{8,9},{9,8},{10,11... | collective-permute-start | bytes 49160 | tf_op jit(solution)/shard_map/ppermute | solution.py:497
  131.8 3.0 %collective-permute-start.19 = (f32[496,128]{1,0:T(8,128)S(1)}, f32[496,128]{1,0:T(8,128)S(1)}, u32[]{:S(2)}, u32[]{:S(2)}) collective-permute-start(f32[496,128]{1,0:T(8,128)S(1)} %get-tuple-element.116.dual_ref.refs_5_), channel_id=1, source_target_pairs={{0,2},{2,0},{1,3},{3,1},{4,6},{6,4},{5,7},{7,5},{8,10},{10,8},{9,1... | collective-permute-start | bytes 761864 | tf_op jit(solution)/shard_map/ppermute | solution.py:518
  136.5 13.0 %all_to_all.39.price_ref = f32[16,32,128]{2,1,0:T(8,128)S(1)} all-to-all(f32[16,32,128]{2,1,0:T(8,128)S(1)} %unit_prices.11), channel_id=1, replica_groups=mesh['z'=8,'xl'=2,'y'=4,'c'=2,'t'=2] {'xl','z'}, dimensions={0} | all-to-all | bytes 524288 | tf_op jit(solution)/shard_map/all_to_all | solution.py:519
  149.7 13.1 %all_to_all.40.extrap_ref = f32[16,32,128]{2,1,0:T(8,128)S(1)} all-to-all(f32[16,32,128]{2,1,0:T(8,128)S(1)} %get-tuple-element.119), channel_id=1, replica_groups=mesh['z'=8,'xl'=2,'y'=4,'c'=2,'t'=2] {'xl','z'}, dimensions={0} | all-to-all | bytes 524288 | tf_op jit(solution)/shard_map/all_to_all | solution.py:525
  163.2 3.2 %collective-permute-start.20 = (f32[496,128]{1,0:T(8,128)S(1)}, f32[496,128]{1,0:T(8,128)S(1)}, u32[]{:S(2)}, u32[]{:S(2)}) collective-permute-start(f32[496,128]{1,0:T(8,128)S(1)} %unit_flows.11), channel_id=1, source_target_pairs={{0,2},{2,0},{1,3},{3,1},{4,6},{6,4},{5,7},{7,5},{8,10},{10,8},{9,1... | collective-permute-start | bytes 761864 | tf_op jit(solution)/shard_map/ppermute | solution.py:482
  175.0 3.3 %collective-permute-done.22.refs_3_ = f32[256,128]{1,0:T(8,128)S(1)} collective-permute-done((f32[256,128]{1,0:T(8,128)S(1)}, f32[256,128]{1,0:T(8,128)S(1)}, u32[]{:S(2)}, u32[]{:S(2)}) %collective-permute-start.22) | collective-permute-done | bytes 131104 | tf_op jit(solution)/shard_map/ppermute | solution.py:451
  178.6 2.5 %collective-permute-start.25 = (f32[496,128]{1,0:T(8,128)S(1)}, f32[496,128]{1,0:T(8,128)S(1)}, u32[]{:S(2)}, u32[]{:S(2)}) collective-permute-start(f32[496,128]{1,0:T(8,128)S(1)} %dual_step.7.half_ref), channel_id=1, source_target_pairs={{0,2},{2,0},{1,3},{3,1},{4,6},{6,4},{5,7},{7,5},{8,10},{10,8},{9,1... | collective-permute-start | bytes 761864 | tf_op jit(solution)/shard_map/ppermute | solution.py:514
  (97 shorter events, 43.2 us)
Async XLA Ops:
  2.0 17.4 %all-to-all-start = ((f32[16,8,128]{2,1,0:T(8,128)}), f32[16,8,128]{2,1,0:T(8,128)S(1)}, u32[]{:S(2)}, u32[]{:S(2)}) async-start(f32[16,8,128]{2,1,0:T(8,128)} %get-tuple-element.65), calls=%async_computation | async-start | bytes 131072 | tf_op jit(solution)/shard_map/all_to_all | solution.py:464
  25.5 6.0 %collective-permute-start.3 = (f32[240,128]{1,0:T(8,128)S(1)}, f32[240,128]{1,0:T(8,128)S(1)}, u32[]{:S(2)}, u32[]{:S(2)}) collective-permute-start(f32[240,128]{1,0:T(8,128)S(1)} %slice.37), channel_id=1, source_target_pairs={{0,4},{4,0},{8,12},{12,8},{6,10},{10,6},{14,2},{2,14},{1,5},{5,1},... | collective-permute-start | bytes 368648 | tf_op jit(solution)/shard_map/ppermute | solution.py:451
  28.4 5.1 %collective-permute-start.1 = (f32[256,128]{1,0:T(8,128)S(1)}, f32[256,128]{1,0:T(8,128)S(1)}, u32[]{:S(2)}, u32[]{:S(2)}) collective-permute-start(f32[256,128]{1,0:T(8,128)S(1)} %slice.36), channel_id=1, source_target_pairs={{0,4},{4,0},{8,12},{12,8},{6,10},{10,6},{14,2},{2,14},{1,5},{5,1},... | collective-permute-start | bytes 393224 | tf_op jit(solution)/shard_map/ppermute | solution.py:451
  31.5 6.0 %collective-permute-start.4 = (f32[240,128]{1,0:T(8,128)S(1)}, f32[240,128]{1,0:T(8,128)S(1)}, u32[]{:S(2)}, u32[]{:S(2)}) collective-permute-start(f32[240,128]{1,0:T(8,128)S(1)} %slice_add_fusion.5.refs_0_), channel_id=1, source_target_pairs={{4,8},{8,4},{12,0},{0,12},{2,6},{6,2},{10,14},{14,10},{5,9},{9,5},... | collective-permute-start | bytes 368648 | tf_op jit(solution)/shard_map/ppermute | solution.py:451
  37.7 4.3 %collective-permute-start.5 = (f32[496,128]{1,0:T(8,128)S(1)}, f32[496,128]{1,0:T(8,128)S(1)}, u32[]{:S(2)}, u32[]{:S(2)}) collective-permute-start(f32[496,128]{1,0:T(8,128)S(1)} %get-tuple-element.88.dual_ref.refs_5_), channel_id=1, source_target_pairs={{0,2},{2,0},{1,3},{3,1},{4,6},{6,4},{5,7},{7,5},{8,10},{10,8},{9,1... | collective-permute-start | bytes 761864 | tf_op jit(solution)/shard_map/ppermute | solution.py:518
  69.1 4.4 %collective-permute-start.6 = (f32[496,128]{1,0:T(8,128)S(1)}, f32[496,128]{1,0:T(8,128)S(1)}, u32[]{:S(2)}, u32[]{:S(2)}) collective-permute-start(f32[496,128]{1,0:T(8,128)S(1)} %unit_flows.7), channel_id=1, source_target_pairs={{0,2},{2,0},{1,3},{3,1},{4,6},{6,4},{5,7},{7,5},{8,10},{10,8},{9,1... | collective-permute-start | bytes 761864 | tf_op jit(solution)/shard_map/ppermute | solution.py:482
  73.5 5.3 %collective-permute-start.9 = (f32[256,128]{1,0:T(8,128)S(1)}, f32[256,128]{1,0:T(8,128)S(1)}, u32[]{:S(2)}, u32[]{:S(2)}) collective-permute-start(f32[256,128]{1,0:T(8,128)S(1)} %slice_add_fusion.1), channel_id=1, source_target_pairs={{0,4},{4,0},{8,12},{12,8},{6,10},{10,6},{14,2},{2,14},{1,5},{5,1},... | collective-permute-start | bytes 393224 | tf_op jit(solution)/shard_map/ppermute | solution.py:451
  74.5 5.4 %collective-permute-start.7 = (f32[240,128]{1,0:T(8,128)S(1)}, f32[240,128]{1,0:T(8,128)S(1)}, u32[]{:S(2)}, u32[]{:S(2)}) collective-permute-start(f32[240,128]{1,0:T(8,128)S(1)} %slice_add_fusion.3), channel_id=1, source_target_pairs={{0,4},{4,0},{8,12},{12,8},{6,10},{10,6},{14,2},{2,14},{1,5},{5,1},... | collective-permute-start | bytes 368648 | tf_op jit(solution)/shard_map/ppermute | solution.py:451
  76.3 4.1 %collective-permute-start.8 = (f32[32,128]{1,0:T(8,128)S(1)}, f32[32,128]{1,0:T(8,128)S(1)}, u32[]{:S(2)}, u32[]{:S(2)}) collective-permute-start(f32[32,128]{1,0:T(8,128)S(1)} %get-tuple-element.93.own_ref.old_ref), channel_id=1, source_target_pairs={{0,1},{1,0},{2,3},{3,2},{4,5},{5,4},{6,7},{7,6},{8,9},{9,8},{10,11... | collective-permute-start | bytes 49160 | tf_op jit(solution)/shard_map/ppermute | solution.py:497
  78.8 4.1 %collective-permute-start.11 = (f32[256,128]{1,0:T(8,128)S(1)}, f32[256,128]{1,0:T(8,128)S(1)}, u32[]{:S(2)}, u32[]{:S(2)}) collective-permute-start(f32[256,128]{1,0:T(8,128)S(1)} %add.76.refs_1_), channel_id=1, source_target_pairs={{4,8},{8,4},{12,0},{0,12},{2,6},{6,2},{10,14},{14,10},{5,9},{9,5},... | collective-permute-start | bytes 393224 | tf_op jit(solution)/shard_map/ppermute | solution.py:451
  80.4 4.1 %collective-permute-start.10 = (f32[240,128]{1,0:T(8,128)S(1)}, f32[240,128]{1,0:T(8,128)S(1)}, u32[]{:S(2)}, u32[]{:S(2)}) collective-permute-start(f32[240,128]{1,0:T(8,128)S(1)} %add.74.refs_0_), channel_id=1, source_target_pairs={{4,8},{8,4},{12,0},{0,12},{2,6},{6,2},{10,14},{14,10},{5,9},{9,5},... | collective-permute-start | bytes 368648 | tf_op jit(solution)/shard_map/ppermute | solution.py:451
  84.8 4.1 %collective-permute-start.12 = (f32[496,128]{1,0:T(8,128)S(1)}, f32[496,128]{1,0:T(8,128)S(1)}, u32[]{:S(2)}, u32[]{:S(2)}) collective-permute-start(f32[496,128]{1,0:T(8,128)S(1)} %get-tuple-element.103.dual_ref.refs_5_), channel_id=1, source_target_pairs={{0,2},{2,0},{1,3},{3,1},{4,6},{6,4},{5,7},{7,5},{8,10},{10,8},{9,1... | collective-permute-start | bytes 761864 | tf_op jit(solution)/shard_map/ppermute | solution.py:518
  116.1 4.4 %collective-permute-start.13 = (f32[496,128]{1,0:T(8,128)S(1)}, f32[496,128]{1,0:T(8,128)S(1)}, u32[]{:S(2)}, u32[]{:S(2)}) collective-permute-start(f32[496,128]{1,0:T(8,128)S(1)} %unit_flows.9), channel_id=1, source_target_pairs={{0,2},{2,0},{1,3},{3,1},{4,6},{6,4},{5,7},{7,5},{8,10},{10,8},{9,1... | collective-permute-start | bytes 761864 | tf_op jit(solution)/shard_map/ppermute | solution.py:482
  120.5 5.3 %collective-permute-start.16 = (f32[256,128]{1,0:T(8,128)S(1)}, f32[256,128]{1,0:T(8,128)S(1)}, u32[]{:S(2)}, u32[]{:S(2)}) collective-permute-start(f32[256,128]{1,0:T(8,128)S(1)} %slice_add_fusion), channel_id=1, source_target_pairs={{0,4},{4,0},{8,12},{12,8},{6,10},{10,6},{14,2},{2,14},{1,5},{5,1},... | collective-permute-start | bytes 393224 | tf_op jit(solution)/shard_map/ppermute | solution.py:451
  121.6 5.4 %collective-permute-start.14 = (f32[240,128]{1,0:T(8,128)S(1)}, f32[240,128]{1,0:T(8,128)S(1)}, u32[]{:S(2)}, u32[]{:S(2)}) collective-permute-start(f32[240,128]{1,0:T(8,128)S(1)} %slice_add_fusion.2), channel_id=1, source_target_pairs={{0,4},{4,0},{8,12},{12,8},{6,10},{10,6},{14,2},{2,14},{1,5},{5,1},... | collective-permute-start | bytes 368648 | tf_op jit(solution)/shard_map/ppermute | solution.py:451
  123.4 4.1 %collective-permute-start.15 = (f32[32,128]{1,0:T(8,128)S(1)}, f32[32,128]{1,0:T(8,128)S(1)}, u32[]{:S(2)}, u32[]{:S(2)}) collective-permute-start(f32[32,128]{1,0:T(8,128)S(1)} %get-tuple-element.109.own_ref.old_ref), channel_id=1, source_target_pairs={{0,1},{1,0},{2,3},{3,2},{4,5},{5,4},{6,7},{7,6},{8,9},{9,8},{10,11... | collective-permute-start | bytes 49160 | tf_op jit(solution)/shard_map/ppermute | solution.py:497
  125.9 3.9 %collective-permute-start.18 = (f32[256,128]{1,0:T(8,128)S(1)}, f32[256,128]{1,0:T(8,128)S(1)}, u32[]{:S(2)}, u32[]{:S(2)}) collective-permute-start(f32[256,128]{1,0:T(8,128)S(1)} %add.80.refs_1_), channel_id=1, source_target_pairs={{4,8},{8,4},{12,0},{0,12},{2,6},{6,2},{10,14},{14,10},{5,9},{9,5},... | collective-permute-start | bytes 393224 | tf_op jit(solution)/shard_map/ppermute | solution.py:451
  127.5 4.0 %collective-permute-start.17 = (f32[240,128]{1,0:T(8,128)S(1)}, f32[240,128]{1,0:T(8,128)S(1)}, u32[]{:S(2)}, u32[]{:S(2)}) collective-permute-start(f32[240,128]{1,0:T(8,128)S(1)} %add.78.refs_0_), channel_id=1, source_target_pairs={{4,8},{8,4},{12,0},{0,12},{2,6},{6,2},{10,14},{14,10},{5,9},{9,5},... | collective-permute-start | bytes 368648 | tf_op jit(solution)/shard_map/ppermute | solution.py:451
  131.8 4.2 %collective-permute-start.19 = (f32[496,128]{1,0:T(8,128)S(1)}, f32[496,128]{1,0:T(8,128)S(1)}, u32[]{:S(2)}, u32[]{:S(2)}) collective-permute-start(f32[496,128]{1,0:T(8,128)S(1)} %get-tuple-element.116.dual_ref.refs_5_), channel_id=1, source_target_pairs={{0,2},{2,0},{1,3},{3,1},{4,6},{6,4},{5,7},{7,5},{8,10},{10,8},{9,1... | collective-permute-start | bytes 761864 | tf_op jit(solution)/shard_map/ppermute | solution.py:518
  163.2 4.4 %collective-permute-start.20 = (f32[496,128]{1,0:T(8,128)S(1)}, f32[496,128]{1,0:T(8,128)S(1)}, u32[]{:S(2)}, u32[]{:S(2)}) collective-permute-start(f32[496,128]{1,0:T(8,128)S(1)} %unit_flows.11), channel_id=1, source_target_pairs={{0,2},{2,0},{1,3},{3,1},{4,6},{6,4},{5,7},{7,5},{8,10},{10,8},{9,1... | collective-permute-start | bytes 761864 | tf_op jit(solution)/shard_map/ppermute | solution.py:482
  167.7 5.0 %collective-permute-start.23 = (f32[240,128]{1,0:T(8,128)S(1)}, f32[240,128]{1,0:T(8,128)S(1)}, u32[]{:S(2)}, u32[]{:S(2)}) collective-permute-start(f32[240,128]{1,0:T(8,128)S(1)} %slice.57), channel_id=1, source_target_pairs={{0,4},{4,0},{8,12},{12,8},{6,10},{10,6},{14,2},{2,14},{1,5},{5,1},... | collective-permute-start | bytes 368648 | tf_op jit(solution)/shard_map/ppermute | solution.py:451
  168.7 5.4 %collective-permute-start.21 = (f32[256,128]{1,0:T(8,128)S(1)}, f32[256,128]{1,0:T(8,128)S(1)}, u32[]{:S(2)}, u32[]{:S(2)}) collective-permute-start(f32[256,128]{1,0:T(8,128)S(1)} %slice.56), channel_id=1, source_target_pairs={{0,4},{4,0},{8,12},{12,8},{6,10},{10,6},{14,2},{2,14},{1,5},{5,1},... | collective-permute-start | bytes 393224 | tf_op jit(solution)/shard_map/ppermute | solution.py:451
  172.7 5.6 %collective-permute-start.24 = (f32[240,128]{1,0:T(8,128)S(1)}, f32[240,128]{1,0:T(8,128)S(1)}, u32[]{:S(2)}, u32[]{:S(2)}) collective-permute-start(f32[240,128]{1,0:T(8,128)S(1)} %slice_add_fusion.4.refs_0_), channel_id=1, source_target_pairs={{4,8},{8,4},{12,0},{0,12},{2,6},{6,2},{10,14},{14,10},{5,9},{9,5},... | collective-permute-start | bytes 368648 | tf_op jit(solution)/shard_map/ppermute | solution.py:451
  174.1 4.2 %collective-permute-start.22 = (f32[256,128]{1,0:T(8,128)S(1)}, f32[256,128]{1,0:T(8,128)S(1)}, u32[]{:S(2)}, u32[]{:S(2)}) collective-permute-start(f32[256,128]{1,0:T(8,128)S(1)} %slice_add_fusion.6.refs_1_), channel_id=1, source_target_pairs={{4,8},{8,4},{12,0},{0,12},{2,6},{6,2},{10,14},{14,10},{5,9},{9,5},... | collective-permute-start | bytes 393224 | tf_op jit(solution)/shard_map/ppermute | solution.py:451
  (6 other events, 66.9 us)
